TPU v7x, 32 devices: a whole 2x2x4 slice. The times are simulated.
32 devices in a mesh: groups: 2 (over y), req: 4 (over z), head: 2 (over x), sub: 2 (over core).
Axes of the slice: x: 2, y: 2, z: 4, core: 2. Of those that a mesh axis runs over, the one named last changes fastest.
Arguments:
- q_nope: bfloat16 [2048, 8192], P(('groups', 'req', 'sub'), 'head'), parts along dimension 0, may hold values from -12 to 12
- q_rope: bfloat16 [2048, 4096], P(('groups', 'req', 'sub'), 'head'), parts along dimension 0, may hold values from -16 to 16
- new_latent: bfloat16 [2048, 512], P(('groups', 'req', 'sub')), parts along dimension 0, may hold values from -6 to 6
- new_rope: bfloat16 [2048, 64], P(('groups', 'req', 'sub')), parts along dimension 0, may hold values from -8 to 8
- pool_latent: bfloat16 [128, 128, 512], P(('groups', 'req'), None, 'sub'), parts along dimension 0, may hold values from -6 to 6
- pool_rope: bfloat16 [128, 128, 64], P(('groups', 'req')), parts along dimension 0, may hold values from -6 to 6
- w_uk: bfloat16 [512, 8192], P(None, 'head'), may hold values from -0.25 to 0.25
- w_uv: bfloat16 [512, 8192], P(None, 'head'), may hold values from -0.25 to 0.25
- block_list: int32 [8, 6], P(('groups', 'req')), parts along dimension 0, may hold values from 0 to 63, as said below
- prefix_len: int32 [8], P(('groups', 'req')), parts along dimension 0, may hold values from 192 to 768, as said below
- block_slot: int32 [128], P('groups'), parts along dimension 0, may hold values from 0 to 63, as said below
Outputs:
- attended: bfloat16 [2048, 8192], P(('groups', 'req', 'sub'), 'head'), parts along dimension 0
There are 2 independent parts, one for each index of `groups`. A program takes and returns all parts, laid end to end along the dimension named above; an argument that names none is the same for every part. Nothing has to cross between parts.
Inputs may be any that keep to these rules, and one draw needn't show every extreme that they name: `block_list`: each row lists 6 different block ids; no row lists more than 2 blocks stored with one owner (storage positions o * 16 to o * 16 + 15), and in every draw some owner stores 2 blocks of every row. `prefix_len`: some row has the full 6 * 128 prefix tokens. `block_slot`: each storage position once.
All inputs are finite; a program needn't handle non-finite values.
Results may differ from a plain program's by a relative error of at most 0.0072.
Values may be sent and summed in bfloat16 or wider, within the bound.
No kernel may reach another device: no remote copies, remote signals or barrier semaphores. Data moves between devices by JAX's collectives and lax.ppermute only.
A program may use at most 128 MiB of HBM per device.

v0:
```python
import math

import jax
import jax.numpy as jnp
from jax import lax
from jax.sharding import PartitionSpec as P

NOPE = 128
ROPE = 64
VDIM = 128
CAP = 2


def shards(
    q_nope,
    q_rope,
    new_latent,
    new_rope,
    pool_latent,
    pool_rope,
    w_uk,
    w_uv,
    block_list,
    prefix_len,
    block_slot,
):
    owners = lax.axis_size("req")
    pool_local = pool_latent.shape[0]
    block = pool_latent.shape[1]
    blocks = block_list.shape[1]
    wanted = block_list[0]
    pool_ids = jnp.arange(block_slot.shape[0], dtype=jnp.int32)
    physical = jnp.sum(
        jnp.where(wanted[:, None] == pool_ids[None, :], block_slot[None, :], 0), axis=1
    )
    owner = physical // pool_local
    local = physical % pool_local
    order = jnp.arange(blocks, dtype=jnp.int32)
    earlier = jnp.sum(
        ((owner[None, :] == owner[:, None]) & (order[None, :] < order[:, None])).astype(jnp.int32),
        axis=1,
    )
    slot = owner * CAP + earlier
    slot_ids = jnp.arange(owners * CAP, dtype=jnp.int32)
    request = jnp.sum(jnp.where(slot[:, None] == slot_ids[None, :], local[:, None], 0), axis=0)
    request = request.reshape(owners, CAP)
    asked = lax.all_to_all(request, "req", split_axis=0, concat_axis=0, tiled=True).reshape(-1)
    sent_lat = jnp.take(pool_latent, asked, axis=0).reshape(owners, CAP, block, -1)
    sent_rope = jnp.take(pool_rope, asked, axis=0).reshape(owners, CAP, block, -1)
    got_lat, got_rope = (
        lax.all_to_all(sent_lat, "req", split_axis=0, concat_axis=0, tiled=True),
        lax.all_to_all(sent_rope, "req", split_axis=0, concat_axis=0, tiled=True),
    )
    prefix_lat = jnp.take(got_lat.reshape(owners * CAP, block, -1), slot, axis=0)
    prefix_rope = jnp.take(got_rope.reshape(owners * CAP, block, -1), slot, axis=0)
    prefix_lat = lax.all_gather(prefix_lat, "sub", axis=2, tiled=True)
    fresh_lat, fresh_rope = (
        lax.all_gather(new_latent, "sub", axis=0, tiled=True),
        lax.all_gather(new_rope, "sub", axis=0, tiled=True),
    )
    prefix = blocks * block
    key_latent = jnp.concatenate([prefix_lat.reshape(prefix, -1), fresh_lat], axis=0)
    key_rope = jnp.concatenate([prefix_rope.reshape(prefix, -1), fresh_rope], axis=0)
    total = key_latent.shape[0]
    heads = w_uk.shape[1] // NOPE
    key_nope = (
        jnp.dot(key_latent, w_uk, preferred_element_type=jnp.float32)
        .astype(jnp.bfloat16)
        .reshape(total, heads, NOPE)
    )
    values = (
        jnp.dot(key_latent, w_uv, preferred_element_type=jnp.float32)
        .astype(jnp.bfloat16)
        .reshape(total, heads, VDIM)
    )
    queries_here = q_nope.shape[0]
    query_nope = q_nope.reshape(queries_here, heads, NOPE)
    query_rope = q_rope.reshape(queries_here, heads, ROPE)
    scores = jnp.einsum("qhd,khd->hqk", query_nope, key_nope, preferred_element_type=jnp.float32)
    scores = scores + jnp.einsum(
        "qhd,kd->hqk", query_rope, key_rope, preferred_element_type=jnp.float32
    )
    scores = scores * (1.0 / math.sqrt(NOPE + ROPE))
    key_pos = jnp.arange(total, dtype=jnp.int32)
    query_pos = lax.axis_index("sub") * queries_here + jnp.arange(queries_here, dtype=jnp.int32)
    visible = jnp.where(
        key_pos[None, :] < prefix,
        key_pos[None, :] < prefix_len[0],
        key_pos[None, :] - prefix <= query_pos[:, None],
    )
    scores = jnp.where(visible[None], scores, jnp.float32(-1e30))
    peak = jnp.max(scores, axis=2, keepdims=True)
    expo = jnp.where(visible[None], jnp.exp(scores - peak), jnp.float32(0.0))
    weights = (expo / jnp.sum(expo, axis=2, keepdims=True)).astype(jnp.bfloat16)
    out = jnp.einsum("hqk,khd->qhd", weights, values, preferred_element_type=jnp.float32)
    return out.astype(jnp.bfloat16).reshape(queries_here, heads * VDIM)


def solution(mesh):
    placed = (
        P(("groups", "req", "sub"), "head"),
        P(("groups", "req", "sub"), "head"),
        P(("groups", "req", "sub"), None),
        P(("groups", "req", "sub"), None),
        P(("groups", "req"), None, "sub"),
        P(("groups", "req"), None, None),
        P(None, "head"),
        P(None, "head"),
        P(("groups", "req"), None),
        P(("groups", "req")),
        P("groups"),
    )
    return jax.shard_map(
        shards,
        mesh=mesh,
        in_specs=placed,
        out_specs=P(("groups", "req", "sub"), "head"),
        check_vma=False,
    )
```

profile of v0, /device:TPU:0, one launch (start us, length us, event | category | flops | bytes accessed | tf_op | source)
XLA Modules:
  0.0 116.5 jit_solution(15153417149714006731)
XLA Ops:
  0.0 0.9 select_reduce_fusion.1
  1.2 0.7 all_to_all.12
  1.9 6.3 %all-to-all-start = ((s32[4,1,2]{2,1,0:T(1,128)}), s32[4,1,2]{2,1,0:T(1,128)S(1)}, u32[]{:S(2)}, u32[]{:S(2)}) async-start(s32[4,1,2]{2,1,0:T(1,128)} %bitcast.1), calls=%async_computation | async-start | bytes 4096 | tf_op jit(solution)/shard_map/all_to_all | solution.py:47
  8.3 2.2 %all_gather.10 = bf16[256,512]{1,0:T(8,128)(2,1)S(1)} all-gather(bf16[128,512]{1,0:T(8,128)(2,1)} %param.13), channel_id=1, replica_groups=mesh['groups'=2,'req'=4,'head'=2,'sub'=2] {'sub'}, dimensions={0}, use_global_device_ids=true | all-gather | bytes 393216 | tf_op jit(solution)/shard_map/all_gather | solution.py:58
  11.2 1.3 %copy.49 = bf16[128,2048]{0,1:T(8,128)(2,1)S(1)} copy(bf16[128,2048]{1,0:T(8,128)(2,1)} %param.12) | data formatting | bytes 1048576 | tf_op args[1]
  12.5 2.1 %all_gather.11 = bf16[256,64]{0,1:T(8,128)(2,1)S(1)} all-gather(bf16[128,64]{0,1:T(8,128)(2,1)} %param.14), channel_id=1, replica_groups=mesh['groups'=2,'req'=4,'head'=2,'sub'=2] {'sub'}, dimensions={0}, use_global_device_ids=true | all-gather | bytes 49152 | tf_op jit(solution)/shard_map/all_gather | solution.py:59
  15.1 0.7 reduce.3
  16.1 1.8 %gather_fusion = bf16[8,128,256]{2,1,0:T(8,128)(2,1)S(1)} fusion(bf16[16,128,256]{2,1,0:T(8,128)(2,1)} %param.15, s32[1024]{0:T(1024)S(1)} %pad_clamp_fusion.1), kind=kCustom, calls=%fused_computation | custom fusion | bytes 1048608 | tf_op jit(solution)/shard_map/jit(_take)/gather | solution.py:48
  17.9 1.5 %gather_fusion.2 = bf16[8,128,64]{1,2,0:T(8,128)(2,1)S(1)} fusion(bf16[16,128,64]{1,2,0:T(8,128)(2,1)} %param.16, s32[1024]{0:T(1024)S(1)} %pad_clamp_fusion.1), kind=kCustom, calls=%fused_computation.2 | custom fusion | bytes 262176 | tf_op jit(solution)/shard_map/jit(_take)/gather | solution.py:49
  19.4 0.7 broadcast_select_fusion.2
  20.1 5.1 %all-to-all-start.2 = ((bf16[4,2,128,64]{2,3,1,0:T(8,128)(2,1)}), bf16[4,2,128,64]{2,3,1,0:T(8,128)(2,1)S(1)}, u32[]{:S(2)}, u32[]{:S(2)}) async-start(bf16[4,2,128,64]{2,3,1,0:T(8,128)(2,1)} %broadcast_select_fusion.2), calls=%async_computation.2 | async-start | bytes 262144 | tf_op jit(solution)/shard_map/all_to_all | solution.py:52
  25.2 0.9 broadcast_select_fusion
  26.1 5.3 %all-to-all-done.2 = bf16[4,2,128,64]{2,3,1,0:T(8,128)(2,1)S(1)} async-done(((bf16[4,2,128,64]{2,3,1,0:T(8,128)(2,1)}), bf16[4,2,128,64]{2,3,1,0:T(8,128)(2,1)S(1)}, u32[]{:S(2)}, u32[]{:S(2)}) %all-to-all-start.2) | async-done | bytes 131104 | tf_op jit(solution)/shard_map/all_to_all | solution.py:52
  31.4 3.5 %all-to-all-start.1 = ((bf16[4,2,128,256]{3,2,1,0:T(8,128)(2,1)}), bf16[4,2,128,256]{3,2,1,0:T(8,128)(2,1)S(1)}, u32[]{:S(2)}, u32[]{:S(2)}) async-start(bf16[4,2,128,256]{3,2,1,0:T(8,128)(2,1)} %broadcast_select_fusion), calls=%async_computation.1 | async-start | bytes 1048576 | tf_op jit(solution)/shard_map/all_to_all | solution.py:51
  35.0 0.8 compare_select_fusion
  36.5 11.9 %all-to-all-done.1 = bf16[4,2,128,256]{3,2,1,0:T(8,128)(2,1)S(1)} async-done(((bf16[4,2,128,256]{3,2,1,0:T(8,128)(2,1)}), bf16[4,2,128,256]{3,2,1,0:T(8,128)(2,1)S(1)}, u32[]{:S(2)}, u32[]{:S(2)}) %all-to-all-start.1) | async-done | bytes 524320 | tf_op jit(solution)/shard_map/all_to_all | solution.py:51
  49.1 2.4 %all_gather.9 = bf16[6,128,512]{2,1,0:T(8,128)(2,1)S(1)} all-gather(bf16[6,128,256]{2,1,0:T(8,128)(2,1)S(1)} %broadcast_select_fusion.1), channel_id=1, replica_groups=mesh['groups'=2,'req'=4,'head'=2,'sub'=2] {'sub'}, dimensions={2}, use_global_device_ids=true | all-gather | bytes 1179648 | tf_op jit(solution)/shard_map/all_gather | solution.py:56
  51.5 9.5 %convert_bitcast_fusion = bf16[128,32,8,128]{3,2,1,0:T(8,128)(2,1)} fusion(bf16[512,4096]{1,0:T(8,128)(2,1)} %param.17, bf16[256,512]{1,0:T(8,128)(2,1)S(1)} %all_gather.10, bf16[768,512]{1,0:T(8,128)(2,1)S(1)} %bitcast.80), kind=kOutput, calls=%fused_computation.13 | convolution fusion | flops 4301258752 | bytes 13631488 | tf_op jit(solution)/shard_map/dot_general | solution.py:67
  61.0 6.7 %convolution_convert_fusion = bf16[1024,4096]{1,0:T(8,128)(2,1)} fusion(bf16[512,4096]{1,0:T(8,128)(2,1)S(1)} %copy-done.2, bf16[256,512]{1,0:T(8,128)(2,1)S(1)} %all_gather.10, bf16[768,512]{1,0:T(8,128)(2,1)S(1)} %bitcast.81), kind=kOutput, calls=%fused_computation.15 | convolution fusion | flops 4301258752 | bytes 13631488 | tf_op jit(solution)/shard_map/dot_general | solution.py:72
  67.7 12.0 %copy.54 = bf16[1024,4096]{0,1:T(8,128)(2,1)} copy(bf16[1024,4096]{1,0:T(8,128)(2,1)} %convolution_convert_fusion) | data formatting | bytes 16777216 | tf_op jit(solution)/shard_map/reshape | solution.py:74
  79.6 11.4 %fusion.3 = f32[32,1024,128]{2,1,0:T(8,128)} fusion(bf16[128,32,8,128]{3,2,1,0:T(8,128)(2,1)} %convert_bitcast_fusion, bf16[128,4096]{1,0:T(8,128)(2,1)S(1)} %copy-done), kind=kOutput, calls=%fused_computation.10 | convolution fusion | flops 1073741824 | bytes 26214400 | tf_op jit(solution)/shard_map/qhd,khd->hqk/dot_general | solution.py:79
  91.1 13.4 %fusion.18 = (f32[32,128]{1,0:T(8,128)S(1)}, f32[32,128,1024]{1,2,0:T(8,128)}) fusion(pred[128,1024]{0,1:T(8,128)(4,1)S(1)} %compare_select_fusion, f32[32,1024,128]{2,1,0:T(8,128)} %fusion.3, bf16[128,32,64]{0,2,1:T(8,128)(2,1)S(1)} %bitcast.82, bf16[256,64]{0,1:T(8,128)(2,1)S(1)} %all_gather.11, bf16[768,64]{0,1:T(8,128)(2,1)S(1)} %bitcast_select_fusion), kind=kOutput, calls=%fused_computation.65 | convolution fusion | flops 562299904 | bytes 34357248 | tf_op jit(solution)/shard_map/sub | solution.py:93
  104.5 10.7 %fusion.7 = bf16[32,128,128]{2,1,0:T(8,128)(2,1)S(1)} fusion(bf16[1024,32,128]{0,2,1:T(8,128)(2,1)} %bitcast.74, f32[32,128,1024]{1,2,0:T(8,128)} %get-tuple-element.10, f32[32,128]{1,0:T(8,128)S(1)} %get-tuple-element.9), kind=kOutput, calls=%fused_computation.16 | convolution fusion | flops 1082654720 | bytes 26230784 | tf_op jit(solution)/shard_map/hqk,khd->qhd/dot_general | solution.py:95
  115.2 1.3 %copy.52 = bf16[128,4096]{1,0:T(8,128)(2,1)} copy(bf16[128,4096]{0,1:T(8,128)(2,1)S(1)} %bitcast.78) | data formatting | bytes 2097152 | tf_op jit(solution)/shard_map/reshape | solution.py:96
  (28 shorter events, 2.5 us)
Async XLA Ops:
  0.0 79.6 %copy-start = (bf16[128,4096]{1,0:T(8,128)(2,1)S(1)}, bf16[128,4096]{1,0:T(8,128)(2,1)}, u32[]{:S(2)}) copy-start(bf16[128,4096]{1,0:T(8,128)(2,1)} %param.11) | copy-start | bytes 3145732
  1.9 12.7 %all-to-all-start = ((s32[4,1,2]{2,1,0:T(1,128)}), s32[4,1,2]{2,1,0:T(1,128)S(1)}, u32[]{:S(2)}, u32[]{:S(2)}) async-start(s32[4,1,2]{2,1,0:T(1,128)} %bitcast.1), calls=%async_computation | async-start | bytes 4096 | tf_op jit(solution)/shard_map/all_to_all | solution.py:47
  20.1 11.3 %all-to-all-start.2 = ((bf16[4,2,128,64]{2,3,1,0:T(8,128)(2,1)}), bf16[4,2,128,64]{2,3,1,0:T(8,128)(2,1)S(1)}, u32[]{:S(2)}, u32[]{:S(2)}) async-start(bf16[4,2,128,64]{2,3,1,0:T(8,128)(2,1)} %broadcast_select_fusion.2), calls=%async_computation.2 | async-start | bytes 262144 | tf_op jit(solution)/shard_map/all_to_all | solution.py:52
  31.4 17.0 %all-to-all-start.1 = ((bf16[4,2,128,256]{3,2,1,0:T(8,128)(2,1)}), bf16[4,2,128,256]{3,2,1,0:T(8,128)(2,1)S(1)}, u32[]{:S(2)}, u32[]{:S(2)}) async-start(bf16[4,2,128,256]{3,2,1,0:T(8,128)(2,1)} %broadcast_select_fusion), calls=%async_computation.1 | async-start | bytes 1048576 | tf_op jit(solution)/shard_map/all_to_all | solution.py:51
  51.5 9.5 %copy-start.2 = (bf16[512,4096]{1,0:T(8,128)(2,1)S(1)}, bf16[512,4096]{1,0:T(8,128)(2,1)}, u32[]{:S(2)}) copy-start(bf16[512,4096]{1,0:T(8,128)(2,1)} %param.18) | copy-start | bytes 12582916
  104.5 12.0 %copy-start.1 = (bf16[128,4096]{1,0:T(8,128)(2,1)S(1)}, bf16[128,4096]{1,0:T(8,128)(2,1)}, u32[]{:S(2)}) copy-start(bf16[128,4096]{1,0:T(8,128)(2,1)} %param.11) | copy-start | bytes 3145732
where the time goes:
time: 117 us
  matrix products  51.7 us (44%)
  local copies, waits for them, and re-layouts  20.6 us (18%)
  waiting for transfers between devices  17.3 us (15%)
  starting transfers between devices  14.9 us (13%)
  blocking collectives  6.65 us (6%)
  other arithmetic  4.56 us (4%)
    sub x1, matrix products, shards(): expo = jnp.where(visible[None], jnp.exp(scores - peak), jnp.float32(0.0))  13.4 us
    reshape x1, local copies, waits for them, and re-layouts, shards(): values = jnp.dot(key_latent, w_uv, preferred_element_type=jnp.float32).as...  12 us
    all_to_all x1, waiting for transfers between devices, shards(): lax.all_to_all(sent_lat, 'req', split_axis=0, concat_axis=0, tiled=True)  11.9 us
    dot_general x1, matrix products, shards(): jnp.einsum('qhd,khd->hqk', query_nope, key_nope, preferred_element_type=j...  11.4 us
    dot_general x1, matrix products, shards(): jnp.einsum('hqk,khd->qhd', weights, values, preferred_element_type=jnp.fl...  10.7 us
    dot_general x1, matrix products, shards(): jnp.dot(key_latent, w_uk, preferred_element_type=jnp.float32)  9.52 us
    dot_general x1, matrix products, shards(): jnp.dot(key_latent, w_uv, preferred_element_type=jnp.float32)  6.65 us
    all_to_all x1, starting transfers between devices, shards(): lax.all_to_all(request, 'req', split_axis=0, concat_axis=0, tiled=True)  6.35 us
  transfers between devices with their start and end apart: 3, of which 2 were waited for; matrix products, arithmetic and copies ran while one was open for 3% of the time, Pallas kernels for 0%

commit v1 on v0

v1 whole, which is shorter than its diff:
```python
import functools
import math

import jax
import jax.numpy as jnp
from jax import lax
from jax.experimental import pallas as pl
from jax.experimental.pallas import tpu as pltpu
from jax.sharding import PartitionSpec as P

NOPE = 128
ROPE = 64
VDIM = 128
CAP = 2
LANES = 128
HIDE = -1e30


def pack_kernel(n, blocks, pool_local, lists, slots_ref, pool_ref, rope_ref, outs, where_ref,
                index_ref, count_ref, rope_buf, lat_sem, rope_sem):
    me = lax.axis_index("req")
    sub = lax.axis_index("sub")
    block = pool_ref.shape[1]
    width = pool_ref.shape[2]
    for i in range(n * CAP):
        index_ref[i] = 0
        where_ref[i] = -1
    for i in range(n):
        count_ref[i] = 0
    for k in range(n):
        found = jnp.int32(0)
        for p in range(blocks):
            physical = slots_ref[lists[k][0, p]]
            owner = physical // pool_local
            mine = owner == me

            @pl.when(mine)
            def _():
                index_ref[k * CAP + found] = physical - owner * pool_local

            found = found + mine.astype(jnp.int32)
            if k == 0:
                shift = lax.rem(me - owner + n, n)
                earlier = count_ref[shift]
                where_ref[shift * CAP + earlier] = p
                count_ref[shift] = earlier + 1
    lat_copies = []
    rope_copies = []
    for k in range(n):
        copy = pltpu.make_async_copy(
            rope_ref.at[index_ref[k * CAP + sub]], rope_buf.at[k], rope_sem.at[k]
        )
        copy.start()
        rope_copies.append(copy)
        for c in range(CAP):
            copy = pltpu.make_async_copy(
                pool_ref.at[index_ref[k * CAP + c]],
                outs[k].at[pl.ds(c * block, block)],
                lat_sem.at[k * CAP + c],
            )
            copy.start()
            lat_copies.append(copy)
    parts = width // ROPE
    rows = block // parts
    for k in range(n):
        rope_copies[k].wait()
        piece = rope_buf[k]
        outs[k][CAP * block :, :] = jnp.concatenate(
            [piece[i * rows : (i + 1) * rows] for i in range(parts)], axis=1
        )
    for copy in lat_copies:
        copy.wait()


def pack(n, lists, block_slot, pool_latent, pool_rope):
    pool_local, block, width = pool_latent.shape
    blocks = lists[0].shape[1]
    rows = CAP * block + block * ROPE // width
    vmem = pl.BlockSpec(memory_space=pltpu.VMEM)
    smem = pl.BlockSpec(memory_space=pltpu.SMEM)

    def body(*refs):
        pack_kernel(
            n, blocks, pool_local, refs[:n], refs[n], refs[n + 1], refs[n + 2],
            refs[n + 3 : 2 * n + 3], refs[2 * n + 3], *refs[2 * n + 4 :],
        )

    out = pl.pallas_call(
        body,
        out_shape=[jax.ShapeDtypeStruct((rows, width), jnp.bfloat16)] * n
        + [jax.ShapeDtypeStruct((n * CAP,), jnp.int32)],
        in_specs=[smem] * (n + 1) + [pl.BlockSpec(memory_space=pl.ANY)] * 2,
        out_specs=[vmem] * n + [smem],
        scratch_shapes=[
            pltpu.SMEM((n * CAP,), jnp.int32),
            pltpu.SMEM((n,), jnp.int32),
            pltpu.VMEM((n, block, ROPE), jnp.bfloat16),
            pltpu.SemaphoreType.DMA((n * CAP,)),
            pltpu.SemaphoreType.DMA((n,)),
        ],
        cost_estimate=pl.CostEstimate(flops=0, bytes_accessed=4 * n * rows * width, transcendentals=0),
        name="pack",
    )(*lists, block_slot, pool_latent, pool_rope)
    return out[:n], out[n]


def attend_kernel(n, blocks, sub_ref, len_ref, where_ref, *refs):
    mine = refs[:n]
    theirs = refs[n : 2 * n]
    (lat_a, rope_a, lat_b, rope_b, qn_a, qr_a, qn_b, qr_b, wk_ref, wv_ref,
     out_ref, send_ref, lat, tails, bias) = refs[2 * n :]
    sub = sub_ref[0]
    block = lat_a.shape[0]
    width = mine[0].shape[1]
    prefix = blocks * block
    queries = 2 * block

    @pl.when(pl.program_id(0) == 0)
    def _():
        parts = width // ROPE
        rows = block // parts
        lane = lax.broadcasted_iota(jnp.int32, (block, ROPE), 1)
        row = lax.broadcasted_iota(jnp.int32, (block, ROPE), 0)
        plain = jnp.zeros((block, ROPE), jnp.bfloat16)

        def put_tails(base, rope, mask):
            tails[0, pl.ds(base, block), :] = jnp.concatenate([rope, mask], axis=1)
            tails[1, pl.ds(base, block), :] = jnp.concatenate([mask, rope], axis=1)

        for k in range(n):
            for c in range(CAP):
                p = where_ref[k * CAP + c]

                @pl.when(p >= 0)
                def _():
                    base = pl.multiple_of(p * block, block)
                    here = pl.multiple_of(sub * width, width)
                    there = pl.multiple_of((1 - sub) * width, width)
                    lat[pl.ds(base, block), pl.ds(here, width)] = mine[k][pl.ds(c * block, block), :]
                    lat[pl.ds(base, block), pl.ds(there, width)] = theirs[k][pl.ds(c * block, block), :]
                    packed = jnp.where(
                        sub == c, mine[k][CAP * block :, :], theirs[k][CAP * block :, :]
                    )
                    rope = jnp.concatenate(
                        [packed[:, i * ROPE : (i + 1) * ROPE] for i in range(parts)], axis=0
                    )
                    hidden = (lane == 0) & (base + row >= len_ref[0])
                    put_tails(base, rope, jnp.where(hidden, HIDE, 0.0).astype(jnp.bfloat16))

        lat[prefix : prefix + block, :] = lat_a[...]
        lat[prefix + block :, :] = lat_b[...]
        put_tails(prefix, rope_a[...], plain)
        put_tails(prefix + block, rope_b[:, :ROPE], plain)
        i = lax.broadcasted_iota(jnp.int32, (queries, queries), 0)
        j = lax.broadcasted_iota(jnp.int32, (queries, queries), 1)
        flip = sub * block
        query_pos = jnp.bitwise_xor(i, flip)
        key_pos = jnp.bitwise_xor(j, flip)
        bias[...] = jnp.where(key_pos <= query_pos, 0.0, HIDE)

    keys = lat[...]
    k2 = jnp.dot(keys, wk_ref[...], preferred_element_type=jnp.float32).astype(jnp.bfloat16)
    v2 = jnp.dot(keys, wv_ref[...], preferred_element_type=jnp.float32).astype(jnp.bfloat16)
    qn = jnp.concatenate([qn_a[...], qn_b[...]], axis=0)
    qr = jnp.concatenate([qr_a[...], qr_b[...]], axis=0)
    lane = lax.broadcasted_iota(jnp.int32, (queries, LANES), 1)
    ones = jnp.ones((keys.shape[0], LANES), jnp.bfloat16)
    rate = math.log2(math.e) / math.sqrt(NOPE + ROPE)
    for j in range(2):
        fill = jnp.where(lane == (1 - j) * ROPE, 1.0, 0.0).astype(jnp.bfloat16)
        own = (lane >= ROPE) if j else (lane < ROPE)
        qc = jnp.concatenate([qn[:, j * NOPE : (j + 1) * NOPE], jnp.where(own, qr, fill)], axis=1)
        kc = jnp.concatenate([k2[:, j * NOPE : (j + 1) * NOPE], tails[j]], axis=1)
        s = lax.dot_general(qc, kc, (((1,), (1,)), ((), ())), preferred_element_type=jnp.float32)
        s = jnp.concatenate([s[:, :prefix], s[:, prefix:] + bias[...]], axis=1)
        peak = jnp.max(s, axis=1, keepdims=True)
        e = jnp.exp2((s - peak) * rate).astype(jnp.bfloat16)
        vc = jnp.concatenate([v2[:, j * VDIM : (j + 1) * VDIM], ones], axis=1)
        o = jnp.dot(e, vc, preferred_element_type=jnp.float32)
        o = (o[:, :VDIM] / o[:, VDIM : VDIM + 1]).astype(jnp.bfloat16)
        out_ref[:, j * VDIM : (j + 1) * VDIM] = o[:block]
        send_ref[:, j * VDIM : (j + 1) * VDIM] = o[block:]


def attend(n, blocks, sub, prefix_len, where, mine, theirs, new_latent, new_rope, q_nope, q_rope,
           other, w_uk, w_uv):
    block, latent = new_latent.shape
    heads = w_uk.shape[1] // NOPE // 2
    pairs = heads // 2
    keys = (blocks + 2) * block
    whole = lambda a: pl.BlockSpec(a.shape, lambda g, *_: (0,) * a.ndim)
    half = heads * NOPE
    nope_at = latent
    rope_at = nope_at + half
    tail_at = rope_at + heads * ROPE

    def at(width, first, follow):
        if follow:
            return pl.BlockSpec((block, width), lambda g, *_: (0, first // width + g))
        return pl.BlockSpec((block, width), lambda g, *_: (0, first // width))

    def ours(rows, width):
        return pl.BlockSpec((rows, width), lambda g, s, *_: (0, s[0] * pairs + g))

    spec = pltpu.PrefetchScalarGridSpec(
        num_scalar_prefetch=3,
        grid=(pairs,),
        in_specs=[whole(a) for a in mine]
        + [whole(a) for a in theirs]
        + [
            whole(new_latent),
            whole(new_rope),
            at(latent, 0, False),
            at(LANES, tail_at, False),
            ours(block, 2 * NOPE),
            ours(block, 2 * ROPE),
            at(2 * NOPE, nope_at, True),
            at(2 * ROPE, rope_at, True),
            ours(latent, 2 * NOPE),
            ours(latent, 2 * VDIM),
        ],
        out_specs=[
            ours(block, 2 * VDIM),
            pl.BlockSpec((block, 2 * VDIM), lambda g, *_: (0, g)),
        ],
        scratch_shapes=[
            pltpu.VMEM((keys, latent), jnp.bfloat16),
            pltpu.VMEM((2, keys, LANES), jnp.bfloat16),
            pltpu.VMEM((2 * block, 2 * block), jnp.float32),
        ],
    )
    return pl.pallas_call(
        functools.partial(attend_kernel, n, blocks),
        grid_spec=spec,
        out_shape=[
            jax.ShapeDtypeStruct((block, 2 * heads * VDIM), jnp.bfloat16),
            jax.ShapeDtypeStruct((block, heads * VDIM), jnp.bfloat16),
        ],
        cost_estimate=pl.CostEstimate(
            flops=4 * keys * latent * heads * NOPE + 8 * block * keys * heads * 256,
            bytes_accessed=8 * 1024 * 1024,
            transcendentals=2 * block * keys * heads,
        ),
        name="attend",
    )(sub, prefix_len, where, *mine, *theirs, new_latent, new_rope, other, other, q_nope, q_rope,
      other, other, w_uk, w_uv)


def shards(
    q_nope,
    q_rope,
    new_latent,
    new_rope,
    pool_latent,
    pool_rope,
    w_uk,
    w_uv,
    block_list,
    prefix_len,
    block_slot,
):
    n = lax.axis_size("req")
    blocks = block_list.shape[1]
    sub = lax.axis_index("sub")
    swap = lambda a: lax.ppermute(a, "sub", [(0, 1), (1, 0)])
    lists = [block_list] + [
        lax.ppermute(block_list, "req", [(i, (i - k) % n) for i in range(n)]) for k in range(1, n)
    ]
    half = q_nope.shape[1] // 2
    rope_half = q_rope.shape[1] // 2
    other = jnp.concatenate(
        [
            new_latent,
            lax.dynamic_slice_in_dim(q_nope, (1 - sub) * half, half, 1),
            lax.dynamic_slice_in_dim(q_rope, (1 - sub) * rope_half, rope_half, 1),
            new_rope,
            jnp.zeros((new_rope.shape[0], LANES - ROPE), jnp.bfloat16),
        ],
        axis=1,
    )
    other = swap(other)
    sent, where = pack(n, lists, block_slot, pool_latent, pool_rope)
    mine = [sent[0]] + [
        lax.ppermute(sent[k], "req", [(i, (i + k) % n) for i in range(n)]) for k in range(1, n)
    ]
    theirs = [swap(a) for a in mine]
    kept, gone = attend(
        n, blocks, sub.reshape(1), prefix_len, where, mine, theirs, new_latent, new_rope, q_nope,
        q_rope, other, w_uk, w_uv,
    )
    back = swap(gone)
    return lax.dynamic_update_slice_in_dim(kept, back, (1 - sub) * half, 1)


def solution(mesh):
    placed = (
        P(("groups", "req", "sub"), "head"),
        P(("groups", "req", "sub"), "head"),
        P(("groups", "req", "sub"), None),
        P(("groups", "req", "sub"), None),
        P(("groups", "req"), None, "sub"),
        P(("groups", "req"), None, None),
        P(None, "head"),
        P(None, "head"),
        P(("groups", "req"), None),
        P(("groups", "req")),
        P("groups"),
    )
    return jax.shard_map(
        shards,
        mesh=mesh,
        in_specs=placed,
        out_specs=P(("groups", "req", "sub"), "head"),
        check_vma=False,
    )
```

time: 117 us -> 56.9 us (0.49)
  matrix products: 51.7 us -> 0 us
  Pallas kernels: 0 us -> 22.2 us
  local copies, waits for them, and re-layouts: 20.6 us -> 8.3 us
  blocking collectives: 6.65 us -> 0 us
  other arithmetic: 4.56 us -> 0 us
  starting transfers between devices: 14.9 us -> 11 us
  waiting for transfers between devices: 17.3 us -> 14.2 us
    dot_general x4 -> x0, matrix products: 38.3 us -> none  [the longest x1 11.4 us: shards(): jnp.einsum('qhd,khd->hqk', query_nope, key_nope, preferred_element_type=j...]
    pallas_call x0 -> x2, Pallas kernels: none -> 22.2 us  [the longest x1 19.2 us: attend(): pl.pallas_call(functools.partial(attend_kernel, n, blocks), grid_spec=spe...]
    all_to_all x3 -> x0, waiting for transfers between devices: 17.3 us -> none  [the longest x1 11.9 us: shards(): lax.all_to_all(sent_lat, 'req', split_axis=0, concat_axis=0, tiled=True)]
    all_to_all x3 -> x0, starting transfers between devices: 14.9 us -> none  [the longest x1 6.35 us: shards(): lax.all_to_all(request, 'req', split_axis=0, concat_axis=0, tiled=True)]
    ppermute x0 -> x12, waiting for transfers between devices: none -> 14.2 us  [the longest x3 9.11 us: shards(): lax.ppermute(sent[k], 'req', [(i, (i + k) % n) for i in range(n)])]
    sub x1 -> x0, matrix products: 13.4 us -> none  [shards(): expo = jnp.where(visible[None], jnp.exp(scores - peak), jnp.float32(0.0))]
    reshape x3 -> x0, local copies, waits for them, and re-layouts: 13.4 us -> none  [the longest x1 12 us: shards(): values = jnp.dot(key_latent, w_uv, preferred_element_type=jnp.float32).as...]
    ppermute x0 -> x12, starting transfers between devices: none -> 11 us  [the longest x3 5.68 us: shards(): lax.ppermute(block_list, 'req', [(i, (i - k) % n) for i in range(n)])]
  transfers between devices with their start and end apart: 3 -> 12, of which waited for: 2 -> 6; matrix products, arithmetic and copies ran while one was open for 3% -> 3% of each run, Pallas kernels for 0% -> 5%
where the time goes in v1:
time: 56.9 us; the launch traced here: 56.4 us
  Pallas kernels  22.2 us (39%)
  waiting for transfers between devices  14.2 us (25%)
  starting transfers between devices  11 us (19%)
  local copies, waits for them, and re-layouts  8.3 us (15%)
  between operations  0.8 us (1%)
    pallas_call x1, Pallas kernels, attend(): pl.pallas_call(functools.partial(attend_kernel, n, blocks), grid_spec=spe...  19.2 us
    ppermute x3, waiting for transfers between devices, shards(): lax.ppermute(sent[k], 'req', [(i, (i + k) % n) for i in range(n)])  9.11 us
    ppermute x3, starting transfers between devices, shards(): lax.ppermute(block_list, 'req', [(i, (i - k) % n) for i in range(n)])  5.68 us
    unnamed x26, local copies, waits for them, and re-layouts  4.34 us
    ppermute x3, starting transfers between devices, shards(): lax.ppermute(sent[k], 'req', [(i, (i + k) % n) for i in range(n)])  3.87 us
    pallas_call x1, Pallas kernels, pack(): pl.pallas_call(body, out_shape=[jax.ShapeDtypeStruct((rows, width), jnp.b...  2.96 us
    ppermute x3, waiting for transfers between devices, shards(): lax.ppermute(block_list, 'req', [(i, (i - k) % n) for i in range(n)])  2.85 us
    ppermute x6, waiting for transfers between devices, shards(): swap = lambda a: lax.ppermute(a, 'sub', [(0, 1), (1, 0)])  2.19 us
  transfers between devices with their start and end apart: 12, of which 6 were waited for; matrix products, arithmetic and copies ran while one was open for 3% of the time, Pallas kernels for 5%

profile of v1, /device:TPU:0, one launch (start us, length us, event | category | flops | bytes accessed | tf_op | source)
XLA Modules:
  0.0 56.4 jit_solution(9797296619534695249)
XLA Ops:
  0.0 0.8 %copy.14.refs_9_ = bf16[128,64]{1,0:T(8,128)(2,1)S(1)} copy(bf16[128,64]{0,1:T(8,128)(2,1)} %param.14) | data formatting | bytes 32768 | tf_op args[3]
  0.8 1.0 %constant_dynamic-slice_fusion = bf16[128,1024]{1,0:T(8,128)(2,1)S(1)} fusion(bf16[128,2048]{1,0:T(8,128)(2,1)} %refs_13_.1, s32[]{:T(128)S(6)} %select_n.8), kind=kLoop, calls=%fused_computation.1 | loop fusion | bytes 524292 | tf_op jit(solution)/shard_map/dynamic_slice | solution.py:275
  1.8 1.1 %constant_dynamic-slice_fusion.1 = bf16[128,2048]{1,0:T(8,128)(2,1)S(1)} fusion(bf16[128,4096]{1,0:T(8,128)(2,1)} %refs_12_.1, s32[]{:T(128)S(6)} %select_n.7), kind=kLoop, calls=%fused_computation.2 | loop fusion | bytes 1048580 | tf_op jit(solution)/shard_map/dynamic_slice | solution.py:274
  2.9 1.1 %concatenate.3 = bf16[128,3712]{1,0:T(8,128)(2,1)S(1)} concatenate(bf16[128,512]{1,0:T(8,128)(2,1)} %refs_8_.1, bf16[128,2048]{1,0:T(8,128)(2,1)S(1)} %constant_dynamic-slice_fusion.1, bf16[128,1024]{1,0:T(8,128)(2,1)S(1)} %constant_dynamic-slice_fusion, bf16[128,64]{1,0:T(8,128)(2,1)S(1)} %copy.14.refs_9_, bf16[128,64]{1,0:T(8,128)(2,1)S(1)} %broadcast_in_dim.3), dimensions={1} | concatenate | bytes 1900544 | tf_op jit(solution)/shard_map/concatenate | solution.py:271
  4.0 0.6 collective-permute-start.10
  4.6 3.7 %collective-permute-start.1 = (s32[1,6]{1,0:T(1,128)}, s32[1,6]{1,0:T(1,128)S(1)}, u32[]{:S(2)}, u32[]{:S(2)}) collective-permute-start(s32[1,6]{1,0:T(1,128)} %refs_0_.1), channel_id=1, source_target_pairs={{0,8},{4,12},{8,0},{12,4},{1,9},{5,13},{9,1},{13,5},{2,10},{6,14},... | collective-permute-start | bytes 80 | tf_op jit(solution)/shard_map/ppermute | solution.py:267
  8.2 1.3 %collective-permute-start = (s32[1,6]{1,0:T(1,128)}, s32[1,6]{1,0:T(1,128)S(1)}, u32[]{:S(2)}, u32[]{:S(2)}) collective-permute-start(s32[1,6]{1,0:T(1,128)} %refs_0_.1), channel_id=1, source_target_pairs={{0,12},{4,0},{8,4},{12,8},{1,13},{5,1},{9,5},{13,9},{2,14},{6,2},{... | collective-permute-start | bytes 80 | tf_op jit(solution)/shard_map/ppermute | solution.py:267
  9.6 0.7 %collective-permute-start.2 = (s32[1,6]{1,0:T(1,128)}, s32[1,6]{1,0:T(1,128)S(1)}, u32[]{:S(2)}, u32[]{:S(2)}) collective-permute-start(s32[1,6]{1,0:T(1,128)} %refs_0_.1), channel_id=1, source_target_pairs={{0,4},{4,8},{8,12},{12,0},{1,5},{5,9},{9,13},{13,1},{2,6},{6,10},{... | collective-permute-start | bytes 80 | tf_op jit(solution)/shard_map/ppermute | solution.py:267
  10.2 2.0 %copy.12.refs_6_ = bf16[16,128,64]{2,1,0:T(8,128)(2,1)} copy(bf16[16,128,64]{1,2,0:T(8,128)(2,1)} %param.16) | data formatting | bytes 524288 | tf_op args[5]
  12.2 2.8 %collective-permute-done.2.refs_3_ = s32[1,6]{1,0:T(1,128)S(1)} collective-permute-done((s32[1,6]{1,0:T(1,128)}, s32[1,6]{1,0:T(1,128)S(1)}, u32[]{:S(2)}, u32[]{:S(2)}) %collective-permute-start.2) | collective-permute-done | bytes 56 | tf_op jit(solution)/shard_map/ppermute | solution.py:267
  15.1 0.6 %copy-done.3 = s32[1,6]{1,0:T(1,128)} copy-done((s32[1,6]{1,0:T(1,128)}, s32[1,6]{1,0:T(1,128)S(1)}, u32[]{:S(2)}) %copy-start.3) | copy-done | bytes 48
  15.6 3.0 %pack.1 = (bf16[288,256]{1,0:T(8,128)(2,1)}, bf16[288,256]{1,0:T(8,128)(2,1)}, bf16[288,256]{1,0:T(8,128)(2,1)}, bf16[288,256]{1,0:T(8,128)(2,1)}, s32[8]{0:T(128)}) custom-call(s32[1,6]{1,0:T(1,128)} %refs_0_.1, s32[1,6]{1,0:T(1,128)} %copy-done.2, s32[1,6]{1,0:T(1,128)} %copy-done.1, s32[1,6]{1,0:T(1,128)} %copy-done.3, s32[64]{0:T(128)} %refs_4_.1, ...), custom_call_target="tpu_custom_call" | custom-call | bytes 1179648 | tf_op jit(solution)/shard_map/pack/pallas_call | solution.py:88
  18.7 1.4 %collective-permute-start.4 = (bf16[288,256]{1,0:T(8,128)(2,1)}, bf16[288,256]{1,0:T(8,128)(2,1)S(1)}, u32[]{:S(2)}, u32[]{:S(2)}) collective-permute-start(bf16[288,256]{1,0:T(8,128)(2,1)} %get-tuple-element.15), channel_id=1, source_target_pairs={{0,8},{4,12},{8,0},{12,4},{1,9},{5,13},{9,1},{13,5},{2,10},{6,14},... | collective-permute-start | bytes 442376 | tf_op jit(solution)/shard_map/ppermute | solution.py:284
  20.1 2.4 %collective-permute-start.5 = (bf16[288,256]{1,0:T(8,128)(2,1)}, bf16[288,256]{1,0:T(8,128)(2,1)S(1)}, u32[]{:S(2)}, u32[]{:S(2)}) collective-permute-start(bf16[288,256]{1,0:T(8,128)(2,1)} %get-tuple-element.16), channel_id=1, source_target_pairs={{0,12},{4,0},{8,4},{12,8},{1,13},{5,1},{9,5},{13,9},{2,14},{6,2},{... | collective-permute-start | bytes 442376 | tf_op jit(solution)/shard_map/ppermute | solution.py:284
  22.5 5.0 %collective-permute-done.3.refs_1_ = bf16[288,256]{1,0:T(8,128)(2,1)S(1)} collective-permute-done((bf16[288,256]{1,0:T(8,128)(2,1)}, bf16[288,256]{1,0:T(8,128)(2,1)S(1)}, u32[]{:S(2)}, u32[]{:S(2)}) %collective-permute-start.3) | collective-permute-done | bytes 147488 | tf_op jit(solution)/shard_map/ppermute | solution.py:284
  27.5 4.2 %collective-permute-done.4.refs_2_ = bf16[288,256]{1,0:T(8,128)(2,1)S(1)} collective-permute-done((bf16[288,256]{1,0:T(8,128)(2,1)}, bf16[288,256]{1,0:T(8,128)(2,1)S(1)}, u32[]{:S(2)}, u32[]{:S(2)}) %collective-permute-start.4) | collective-permute-done | bytes 147488 | tf_op jit(solution)/shard_map/ppermute | solution.py:284
  31.6 0.5 collective-permute-start.9
  33.2 0.2 copy-done.8
  33.6 0.2 copy-done.11
  33.9 0.3 copy-done.4
  34.2 19.2 %attend.1 = (bf16[128,4096]{1,0:T(8,128)(2,1)}, bf16[128,2048]{1,0:T(8,128)(2,1)}) custom-call(s32[1]{0:T(128)} %bitcast.sub_ref, s32[1]{0:T(128)S(6)} %copy.16.len_ref, s32[8]{0:T(128)} %get-tuple-element.12.where_ref, bf16[288,256]{1,0:T(8,128)(2,1)} %get-tuple-element.13.refs_0_, bf16[288,256]{1,0:T(8,128)(2,1)} %copy-done.5, bf16[288,256]{1,0:T(8,128)(2,1)} %copy-done.6, ...), custom_call_target="tpu_custom_call" | custom-call | flops 8589934592 | bytes 8388608 | tf_op jit(solution)/shard_map/attend/pallas_call | solution.py:232
  53.4 0.4 collective-permute-start.11
  53.8 1.8 %collective-permute-done.11 = bf16[128,2048]{1,0:T(8,128)(2,1)S(1)} collective-permute-done((bf16[128,2048]{1,0:T(8,128)(2,1)}, bf16[128,2048]{1,0:T(8,128)(2,1)S(1)}, u32[]{:S(2)}, u32[]{:S(2)}) %collective-permute-start.11) | collective-permute-done | bytes 524320 | tf_op jit(solution)/shard_map/ppermute | solution.py:265
  55.6 0.8 %constant_dynamic-update-slice_fusion = bf16[128,4096]{1,0:T(8,128)(2,1)} fusion(bf16[128,4096]{1,0:T(8,128)(2,1)} %get-tuple-element.17, bf16[128,2048]{1,0:T(8,128)(2,1)S(1)} %collective-permute-done.11, s32[]{:T(128)S(6)} %select_n.7), kind=kLoop, calls=%fused_computation | loop fusion | bytes 1048580 | tf_op jit(solution)/shard_map/dynamic_update_slice | solution.py:292
  (33 shorter events, 0.7 us)
Async XLA Ops:
  0.8 32.4 %copy-start = (bf16[128,64]{1,0:T(8,128)(2,1)}, bf16[128,64]{1,0:T(8,128)(2,1)S(1)}, u32[]{:S(2)}) copy-start(bf16[128,64]{1,0:T(8,128)(2,1)S(1)} %copy.14.refs_9_) | copy-start | bytes 49156
  4.0 29.2 %collective-permute-start.10 = (bf16[128,3712]{1,0:T(8,128)(2,1)S(1)}, bf16[128,3712]{1,0:T(8,128)(2,1)S(1)}, u32[]{:S(2)}, u32[]{:S(2)}) collective-permute-start(bf16[128,3712]{1,0:T(8,128)(2,1)S(1)} %concatenate.3), channel_id=1, source_target_pairs={{0,1},{1,0},{2,3},{3,2},{4,5},{5,4},{6,7},{7,6},{8,9},{9,8},{10,11... | collective-permute-start | bytes 2850824 | tf_op jit(solution)/shard_map/ppermute | solution.py:265
  4.6 7.6 %collective-permute-start.1 = (s32[1,6]{1,0:T(1,128)}, s32[1,6]{1,0:T(1,128)S(1)}, u32[]{:S(2)}, u32[]{:S(2)}) collective-permute-start(s32[1,6]{1,0:T(1,128)} %refs_0_.1), channel_id=1, source_target_pairs={{0,8},{4,12},{8,0},{12,4},{1,9},{5,13},{9,1},{13,5},{2,10},{6,14},... | collective-permute-start | bytes 80 | tf_op jit(solution)/shard_map/ppermute | solution.py:267
  8.2 4.0 %collective-permute-start = (s32[1,6]{1,0:T(1,128)}, s32[1,6]{1,0:T(1,128)S(1)}, u32[]{:S(2)}, u32[]{:S(2)}) collective-permute-start(s32[1,6]{1,0:T(1,128)} %refs_0_.1), channel_id=1, source_target_pairs={{0,12},{4,0},{8,4},{12,8},{1,13},{5,1},{9,5},{13,9},{2,14},{6,2},{... | collective-permute-start | bytes 80 | tf_op jit(solution)/shard_map/ppermute | solution.py:267
  9.6 5.5 %collective-permute-start.2 = (s32[1,6]{1,0:T(1,128)}, s32[1,6]{1,0:T(1,128)S(1)}, u32[]{:S(2)}, u32[]{:S(2)}) collective-permute-start(s32[1,6]{1,0:T(1,128)} %refs_0_.1), channel_id=1, source_target_pairs={{0,4},{4,8},{8,12},{12,0},{1,5},{5,9},{9,13},{13,1},{2,6},{6,10},{... | collective-permute-start | bytes 80 | tf_op jit(solution)/shard_map/ppermute | solution.py:267
  12.2 2.9 %copy-start.1 = (s32[1,6]{1,0:T(1,128)}, s32[1,6]{1,0:T(1,128)S(1)}, u32[]{:S(2)}) copy-start(s32[1,6]{1,0:T(1,128)S(1)} %collective-permute-done.1.refs_2_) | copy-start | bytes 76
  12.2 2.9 %copy-start.2 = (s32[1,6]{1,0:T(1,128)}, s32[1,6]{1,0:T(1,128)S(1)}, u32[]{:S(2)}) copy-start(s32[1,6]{1,0:T(1,128)S(1)} %collective-permute-done.refs_1_) | copy-start | bytes 76
  15.1 0.6 %copy-start.3 = (s32[1,6]{1,0:T(1,128)}, s32[1,6]{1,0:T(1,128)S(1)}, u32[]{:S(2)}) copy-start(s32[1,6]{1,0:T(1,128)S(1)} %collective-permute-done.2.refs_3_) | copy-start | bytes 76
  18.6 8.8 %collective-permute-start.3 = (bf16[288,256]{1,0:T(8,128)(2,1)}, bf16[288,256]{1,0:T(8,128)(2,1)S(1)}, u32[]{:S(2)}, u32[]{:S(2)}) collective-permute-start(bf16[288,256]{1,0:T(8,128)(2,1)} %get-tuple-element.14), channel_id=1, source_target_pairs={{0,4},{4,8},{8,12},{12,0},{1,5},{5,9},{9,13},{13,1},{2,6},{6,10},{... | collective-permute-start | bytes 442376 | tf_op jit(solution)/shard_map/ppermute | solution.py:284
  18.7 12.9 %collective-permute-start.4 = (bf16[288,256]{1,0:T(8,128)(2,1)}, bf16[288,256]{1,0:T(8,128)(2,1)S(1)}, u32[]{:S(2)}, u32[]{:S(2)}) collective-permute-start(bf16[288,256]{1,0:T(8,128)(2,1)} %get-tuple-element.15), channel_id=1, source_target_pairs={{0,8},{4,12},{8,0},{12,4},{1,9},{5,13},{9,1},{13,5},{2,10},{6,14},... | collective-permute-start | bytes 442376 | tf_op jit(solution)/shard_map/ppermute | solution.py:284
  20.1 11.5 %collective-permute-start.5 = (bf16[288,256]{1,0:T(8,128)(2,1)}, bf16[288,256]{1,0:T(8,128)(2,1)S(1)}, u32[]{:S(2)}, u32[]{:S(2)}) collective-permute-start(bf16[288,256]{1,0:T(8,128)(2,1)} %get-tuple-element.16), channel_id=1, source_target_pairs={{0,12},{4,0},{8,4},{12,8},{1,13},{5,1},{9,5},{13,9},{2,14},{6,2},{... | collective-permute-start | bytes 442376 | tf_op jit(solution)/shard_map/ppermute | solution.py:284
  22.5 10.3 %collective-permute-start.6 = (bf16[288,256]{1,0:T(8,128)(2,1)}, bf16[288,256]{1,0:T(8,128)(2,1)S(1)}, u32[]{:S(2)}, u32[]{:S(2)}) collective-permute-start(bf16[288,256]{1,0:T(8,128)(2,1)} %get-tuple-element.13.refs_0_), channel_id=1, source_target_pairs={{0,1},{1,0},{2,3},{3,2},{4,5},{5,4},{6,7},{7,6},{8,9},{9,8},{10,11... | collective-permute-start | bytes 442376 | tf_op jit(solution)/shard_map/ppermute | solution.py:265
  27.4 5.8 %copy-start.5 = (bf16[288,256]{1,0:T(8,128)(2,1)}, bf16[288,256]{1,0:T(8,128)(2,1)S(1)}, u32[]{:S(2)}) copy-start(bf16[288,256]{1,0:T(8,128)(2,1)S(1)} %collective-permute-done.3.refs_1_) | copy-start | bytes 442372
  27.4 5.3 %collective-permute-start.7 = (bf16[288,256]{1,0:T(8,128)(2,1)S(1)}, bf16[288,256]{1,0:T(8,128)(2,1)S(1)}, u32[]{:S(2)}, u32[]{:S(2)}) collective-permute-start(bf16[288,256]{1,0:T(8,128)(2,1)S(1)} %collective-permute-done.3.refs_1_), channel_id=1, source_target_pairs={{0,1},{1,0},{2,3},{3,2},{4,5},{5,4},{6,7},{7,6},{8,9},{9,8},{10,11... | collective-permute-start | bytes 442376 | tf_op jit(solution)/shard_map/ppermute | solution.py:265
  31.6 1.6 %copy-start.6 = (bf16[288,256]{1,0:T(8,128)(2,1)}, bf16[288,256]{1,0:T(8,128)(2,1)S(1)}, u32[]{:S(2)}) copy-start(bf16[288,256]{1,0:T(8,128)(2,1)S(1)} %collective-permute-done.4.refs_2_) | copy-start | bytes 442372
  31.6 1.4 %collective-permute-start.8 = (bf16[288,256]{1,0:T(8,128)(2,1)S(1)}, bf16[288,256]{1,0:T(8,128)(2,1)S(1)}, u32[]{:S(2)}, u32[]{:S(2)}) collective-permute-start(bf16[288,256]{1,0:T(8,128)(2,1)S(1)} %collective-permute-done.4.refs_2_), channel_id=1, source_target_pairs={{0,1},{1,0},{2,3},{3,2},{4,5},{5,4},{6,7},{7,6},{8,9},{9,8},{10,11... | collective-permute-start | bytes 442376 | tf_op jit(solution)/shard_map/ppermute | solution.py:265
  31.6 1.6 %copy-start.7 = (bf16[288,256]{1,0:T(8,128)(2,1)}, bf16[288,256]{1,0:T(8,128)(2,1)S(1)}, u32[]{:S(2)}) copy-start(bf16[288,256]{1,0:T(8,128)(2,1)S(1)} %collective-permute-done.5.refs_3_) | copy-start | bytes 442372
  31.6 1.6 %collective-permute-start.9 = (bf16[288,256]{1,0:T(8,128)(2,1)S(1)}, bf16[288,256]{1,0:T(8,128)(2,1)S(1)}, u32[]{:S(2)}, u32[]{:S(2)}) collective-permute-start(bf16[288,256]{1,0:T(8,128)(2,1)S(1)} %collective-permute-done.5.refs_3_), channel_id=1, source_target_pairs={{0,1},{1,0},{2,3},{3,2},{4,5},{5,4},{6,7},{7,6},{8,9},{9,8},{10,11... | collective-permute-start | bytes 442376 | tf_op jit(solution)/shard_map/ppermute | solution.py:265
  32.8 0.7 %copy-start.8 = (bf16[288,256]{1,0:T(8,128)(2,1)}, bf16[288,256]{1,0:T(8,128)(2,1)S(1)}, u32[]{:S(2)}) copy-start(bf16[288,256]{1,0:T(8,128)(2,1)S(1)} %collective-permute-done.6.refs_4_) | copy-start | bytes 442372
  32.8 0.7 %copy-start.9 = (bf16[288,256]{1,0:T(8,128)(2,1)}, bf16[288,256]{1,0:T(8,128)(2,1)S(1)}, u32[]{:S(2)}) copy-start(bf16[288,256]{1,0:T(8,128)(2,1)S(1)} %collective-permute-done.7.refs_5_) | copy-start | bytes 442372
  33.0 0.7 %copy-start.10 = (bf16[288,256]{1,0:T(8,128)(2,1)}, bf16[288,256]{1,0:T(8,128)(2,1)S(1)}, u32[]{:S(2)}) copy-start(bf16[288,256]{1,0:T(8,128)(2,1)S(1)} %collective-permute-done.8.refs_6_) | copy-start | bytes 442372
  33.2 0.7 %copy-start.11 = (bf16[288,256]{1,0:T(8,128)(2,1)}, bf16[288,256]{1,0:T(8,128)(2,1)S(1)}, u32[]{:S(2)}) copy-start(bf16[288,256]{1,0:T(8,128)(2,1)S(1)} %collective-permute-done.9.refs_7_) | copy-start | bytes 442372
  33.2 1.0 %copy-start.4 = (bf16[128,3712]{1,0:T(8,128)(2,1)}, bf16[128,3712]{1,0:T(8,128)(2,1)S(1)}, u32[]{:S(2)}) copy-start(bf16[128,3712]{1,0:T(8,128)(2,1)S(1)} %collective-permute-done.10.refs_10_.refs_11_.refs_14_.refs_15_) | copy-start | bytes 2850820
  53.4 2.2 %collective-permute-start.11 = (bf16[128,2048]{1,0:T(8,128)(2,1)}, bf16[128,2048]{1,0:T(8,128)(2,1)S(1)}, u32[]{:S(2)}, u32[]{:S(2)}) collective-permute-start(bf16[128,2048]{1,0:T(8,128)(2,1)} %get-tuple-element.18), channel_id=1, source_target_pairs={{0,1},{1,0},{2,3},{3,2},{4,5},{5,4},{6,7},{7,6},{8,9},{9,8},{10,11... | collective-permute-start | bytes 1572872 | tf_op jit(solution)/shard_map/ppermute | solution.py:265

commit v2 on v1

v2 whole, which is shorter than its diff:
```python
import functools
import math

import jax
import jax.numpy as jnp
from jax import lax
from jax.experimental import pallas as pl
from jax.experimental.pallas import tpu as pltpu
from jax.sharding import PartitionSpec as P


NOPE = 128
ROPE = 64
VDIM = 128
CAP = 2
LANES = 128
HIDE = -1e30


def pack_kernel(n, blocks, pool_local, lists, slots_ref, pool_ref, rope_ref, outs, where_ref,
                index_ref, count_ref, lat_sem, rope_sem):
    me = lax.axis_index("req")
    sub = lax.axis_index("sub")
    block = pool_ref.shape[1]
    width = pool_ref.shape[2]
    for i in range(n * CAP):
        index_ref[i] = 0
        where_ref[i] = -1
    for i in range(n):
        count_ref[i] = 0
    for k in range(n):
        found = jnp.int32(0)
        for p in range(blocks):
            physical = slots_ref[lists[k][0, p]]
            owner = physical // pool_local
            mine = owner == me

            @pl.when(mine)
            def _():
                index_ref[k * CAP + found] = physical - owner * pool_local

            found = found + mine.astype(jnp.int32)
            if k == 0:
                step = jnp.bitwise_xor(me, owner)
                earlier = count_ref[step]
                where_ref[step * CAP + earlier] = p
                count_ref[step] = earlier + 1
    parts = width // block
    rows = ROPE // parts
    copies = []
    for k in range(n):
        for c in range(CAP):
            copies.append(pltpu.make_async_copy(
                pool_ref.at[index_ref[k * CAP + c]],
                outs[k].at[pl.ds(c * block, block)],
                lat_sem.at[k * CAP + c],
            ))
        for i in range(parts):
            copies.append(pltpu.make_async_copy(
                rope_ref.at[index_ref[k * CAP + sub], pl.ds(i * rows, rows)],
                outs[k].at[pl.ds(CAP * block, rows), pl.ds(i * block, block)],
                rope_sem.at[k * parts + i],
            ))
    for copy in copies:
        copy.start()
    for copy in copies:
        copy.wait()


def pack(n, lists, block_slot, pool_latent, rope_turned):
    pool_local, block, width = pool_latent.shape
    blocks = lists[0].shape[1]
    rows = CAP * block + block * ROPE // width
    vmem = pl.BlockSpec(memory_space=pltpu.VMEM)
    smem = pl.BlockSpec(memory_space=pltpu.SMEM)

    def body(*refs):
        pack_kernel(
            n, blocks, pool_local, refs[:n], refs[n], refs[n + 1], refs[n + 2],
            refs[n + 3 : 2 * n + 3], refs[2 * n + 3], *refs[2 * n + 4 :],
        )

    out = pl.pallas_call(
        body,
        out_shape=[jax.ShapeDtypeStruct((rows, width), jnp.bfloat16)] * n
        + [jax.ShapeDtypeStruct((n * CAP,), jnp.int32)],
        in_specs=[smem] * (n + 1) + [pl.BlockSpec(memory_space=pl.ANY)] * 2,
        out_specs=[vmem] * n + [smem],
        scratch_shapes=[
            pltpu.SMEM((n * CAP,), jnp.int32),
            pltpu.SMEM((n,), jnp.int32),
            pltpu.SemaphoreType.DMA((n * CAP,)),
            pltpu.SemaphoreType.DMA((n * width // block,)),
        ],
        compiler_params=pltpu.CompilerParams(vmem_limit_bytes=16 << 20),
        cost_estimate=pl.CostEstimate(flops=0, bytes_accessed=4 * n * rows * width, transcendentals=0),
        name="pack",
    )(*lists, block_slot, pool_latent, rope_turned)
    return out[:n], out[n]


def prepare_kernel(lat_ref, qn_ref, qr_ref, rope_ref, out_ref, sem):
    there = 1 - lax.axis_index("sub")
    latent = lat_ref.shape[1]
    half = qn_ref.shape[1] // 2
    rope_half = qr_ref.shape[1] // 2
    tail = latent + half + rope_half
    copies = [
        pltpu.make_async_copy(lat_ref, out_ref.at[:, pl.ds(0, latent)], sem.at[0]),
        pltpu.make_async_copy(
            qn_ref.at[:, pl.ds(pl.multiple_of(there * half, LANES), half)],
            out_ref.at[:, pl.ds(latent, half)],
            sem.at[1],
        ),
        pltpu.make_async_copy(
            qr_ref.at[:, pl.ds(pl.multiple_of(there * rope_half, LANES), rope_half)],
            out_ref.at[:, pl.ds(latent + half, rope_half)],
            sem.at[2],
        ),
        pltpu.make_async_copy(
            rope_ref, out_ref.at[pl.ds(0, ROPE), pl.ds(tail, rope_ref.shape[1])], sem.at[3]
        ),
    ]
    for copy in copies:
        copy.start()
    for copy in copies:
        copy.wait()


def prepare(new_latent, q_nope, q_rope, rope_turned):
    rows, latent = new_latent.shape
    width = latent + q_nope.shape[1] // 2 + q_rope.shape[1] // 2 + rows
    return pl.pallas_call(
        prepare_kernel,
        out_shape=jax.ShapeDtypeStruct((rows, width), jnp.bfloat16),
        in_specs=[pl.BlockSpec(memory_space=pl.ANY)] * 4,
        out_specs=pl.BlockSpec(memory_space=pltpu.VMEM),
        scratch_shapes=[pltpu.SemaphoreType.DMA((4,))],
        compiler_params=pltpu.CompilerParams(vmem_limit_bytes=16 << 20),
        cost_estimate=pl.CostEstimate(flops=0, bytes_accessed=4 * rows * width, transcendentals=0),
        name="prepare",
    )(new_latent, q_nope, q_rope, rope_turned)


RATE = math.log2(math.e) / math.sqrt(NOPE + ROPE)


def attend_kernel(steps, fresh, sub_ref, len_ref, where_ref, *refs):
    count = len(steps)
    mine = refs[:count]
    theirs = refs[count : 2 * count]
    refs = refs[2 * count :]
    if fresh:
        lat_a, rope_a, lat_b, rope_b, *refs = refs
        qn_a, qr_a, qn_b, qr_b, wk_ref, wv_ref, acc_ref, stat_ref, lat, tails, bias = refs
    else:
        (qn_a, qr_a, qn_b, qr_b, wk_ref, wv_ref, acc_ref, stat_ref, out_ref, send_ref, lat,
         tails) = refs
    sub = sub_ref[0]
    block = qn_a.shape[0]
    chunk = CAP * block
    first = chunk if fresh else 0
    queries = 2 * block

    @pl.when(pl.program_id(0) == 0)
    def _():
        def put_tails(base, rope, mask):
            tails[0, base : base + block, :] = jnp.concatenate([rope, mask], axis=1)
            tails[1, base : base + block, :] = jnp.concatenate([mask, rope], axis=1)

        lane = lax.broadcasted_iota(jnp.int32, (block, ROPE), 1)
        row = lax.broadcasted_iota(jnp.int32, (block, ROPE), 0)
        for i, k in enumerate(steps):
            width = mine[i].shape[1]
            here = pl.multiple_of(sub * width, width)
            there = pl.multiple_of((1 - sub) * width, width)
            base = first + i * chunk
            lat[base : base + chunk, pl.ds(here, width)] = mine[i][:chunk, :]
            lat[base : base + chunk, pl.ds(there, width)] = theirs[i][:chunk, :]
            for c in range(CAP):
                packed = jnp.where(sub == c, mine[i][chunk:, :], theirs[i][chunk:, :])
                rope = jnp.concatenate(
                    [packed[:, j * block : (j + 1) * block] for j in range(width // block)], axis=0
                )
                p = where_ref[k * CAP + c]
                hidden = (lane == 0) & ((p < 0) | (p * block + row >= len_ref[0]))
                put_tails(
                    base + c * block, rope.T, jnp.where(hidden, HIDE, 0.0).astype(jnp.bfloat16)
                )
        if fresh:
            plain = jnp.zeros((block, ROPE), jnp.bfloat16)
            lat[:block, :] = lat_a[...]
            lat[block:chunk, :] = lat_b[...]
            put_tails(0, rope_a[...].T, plain)
            put_tails(block, rope_b[:ROPE, :].T, plain)
            i = lax.broadcasted_iota(jnp.int32, (queries, queries), 0)
            j = lax.broadcasted_iota(jnp.int32, (queries, queries), 1)
            flip = sub * block
            seen = jnp.bitwise_xor(j, flip) <= jnp.bitwise_xor(i, flip)
            bias[...] = jnp.where(seen, 0.0, HIDE)

    chunks = count + (1 if fresh else 0)
    qn = jnp.concatenate([qn_a[...], qn_b[...]], axis=0)
    qr = jnp.concatenate([qr_a[...], qr_b[...]], axis=0)
    lane = lax.broadcasted_iota(jnp.int32, (queries, LANES), 1)
    ones = jnp.ones((chunk, LANES), jnp.bfloat16)
    qc = []
    for j in range(2):
        fill = jnp.where(lane == (1 - j) * ROPE, 1.0, 0.0).astype(jnp.bfloat16)
        own = (lane >= ROPE) if j else (lane < ROPE)
        qc.append(
            jnp.concatenate([qn[:, j * NOPE : (j + 1) * NOPE], jnp.where(own, qr, fill)], axis=1)
        )
    scores = [[], []]
    values = []
    for i in range(chunks):
        keys = lat[i * chunk : (i + 1) * chunk, :]
        k2 = jnp.dot(keys, wk_ref[...], preferred_element_type=jnp.float32).astype(jnp.bfloat16)
        v2 = jnp.dot(keys, wv_ref[...], preferred_element_type=jnp.float32).astype(jnp.bfloat16)
        values.append(v2)
        for j in range(2):
            kc = jnp.concatenate(
                [k2[:, j * NOPE : (j + 1) * NOPE], tails[j, i * chunk : (i + 1) * chunk, :]], axis=1
            )
            s = lax.dot_general(
                qc[j], kc, (((1,), (1,)), ((), ())), preferred_element_type=jnp.float32
            )
            if fresh and i == 0:
                s = s + bias[...]
            scores[j].append(s)
    peaks = []
    sums = []
    for j in range(2):
        peak = functools.reduce(jnp.maximum, scores[j])
        peak = jnp.max(peak, axis=1, keepdims=True)
        if not fresh:
            before = stat_ref[:, j : j + 1]
            peak = jnp.maximum(peak, before)
        o = None
        for i in range(chunks):
            e = jnp.exp2((scores[j][i] - peak) * RATE).astype(jnp.bfloat16)
            vc = jnp.concatenate([values[i][:, j * VDIM : (j + 1) * VDIM], ones], axis=1)
            part = jnp.dot(e, vc, preferred_element_type=jnp.float32)
            o = part if o is None else o + part
        total = o[:, VDIM:]
        o = o[:, :VDIM]
        if fresh:
            acc_ref[:, j * VDIM : (j + 1) * VDIM] = o
            peaks.append(peak)
            sums.append(total)
        else:
            keep = jnp.exp2((before - peak) * RATE)
            total = total[:, :1] + keep * stat_ref[:, 2 + j : 3 + j]
            o = o + keep * acc_ref[:, j * VDIM : (j + 1) * VDIM]
            o = (o / total).astype(jnp.bfloat16)
            out_ref[:, j * VDIM : (j + 1) * VDIM] = o[:block]
            send_ref[:, j * VDIM : (j + 1) * VDIM] = o[block:]
    if fresh:
        stat_ref[...] = jnp.where(
            lane == 0, peaks[0],
            jnp.where(lane == 1, peaks[1], jnp.where(lane == 2, sums[0], sums[1])),
        )


def attend(steps, sub, prefix_len, where, mine, theirs, new_latent, rope_turned, q_nope, q_rope,
           other, w_uk, w_uv, state):
    fresh = state is None
    block, latent = new_latent.shape
    heads = w_uk.shape[1] // NOPE // 2
    pairs = heads // 2
    keys = (len(steps) + (1 if fresh else 0)) * CAP * block
    whole = lambda a: pl.BlockSpec(a.shape, lambda g, *_: (0,) * a.ndim)
    nope_at = latent
    rope_at = nope_at + heads * NOPE
    tail_at = rope_at + heads * ROPE

    def at(width, first, follow):
        if follow:
            return pl.BlockSpec((block, width), lambda g, *_: (0, first // width + g))
        return pl.BlockSpec((block, width), lambda g, *_: (0, first // width))

    def ours(rows, width):
        return pl.BlockSpec((rows, width), lambda g, s, *_: (0, s[0] * pairs + g))

    def step(rows, width):
        return pl.BlockSpec((rows, width), lambda g, *_: (0, g))

    specs = [whole(a) for a in mine] + [whole(a) for a in theirs]
    args = [*mine, *theirs]
    if fresh:
        specs += [whole(new_latent), whole(rope_turned), at(latent, 0, False), at(LANES, tail_at, False)]
        args += [new_latent, rope_turned, other, other]
    specs += [
        ours(block, 2 * NOPE),
        ours(block, 2 * ROPE),
        at(2 * NOPE, nope_at, True),
        at(2 * ROPE, rope_at, True),
        ours(latent, 2 * NOPE),
        ours(latent, 2 * VDIM),
    ]
    args += [q_nope, q_rope, other, other, w_uk, w_uv]
    state_specs = [step(2 * block, 2 * VDIM), step(2 * block, LANES)]
    scratch = [
        pltpu.VMEM((keys, latent), jnp.bfloat16),
        pltpu.VMEM((2, keys, LANES), jnp.bfloat16),
    ]
    if fresh:
        out_specs = state_specs
        out_shape = [
            jax.ShapeDtypeStruct((2 * block, heads * VDIM), jnp.float32),
            jax.ShapeDtypeStruct((2 * block, pairs * LANES), jnp.float32),
        ]
        scratch.append(pltpu.VMEM((2 * block, 2 * block), jnp.float32))
    else:
        specs += state_specs
        args += state
        out_specs = [ours(block, 2 * VDIM), step(block, 2 * VDIM)]
        out_shape = [
            jax.ShapeDtypeStruct((block, 2 * heads * VDIM), jnp.bfloat16),
            jax.ShapeDtypeStruct((block, heads * VDIM), jnp.bfloat16),
        ]
    return pl.pallas_call(
        functools.partial(attend_kernel, steps, fresh),
        grid_spec=pltpu.PrefetchScalarGridSpec(
            num_scalar_prefetch=3,
            grid=(pairs,),
            in_specs=specs,
            out_specs=out_specs,
            scratch_shapes=scratch,
        ),
        out_shape=out_shape,
        compiler_params=pltpu.CompilerParams(vmem_limit_bytes=40 << 20),
        cost_estimate=pl.CostEstimate(
            flops=4 * keys * latent * heads * NOPE + 8 * block * keys * heads * 256,
            bytes_accessed=8 * 1024 * 1024,
            transcendentals=2 * block * keys * heads,
        ),
        name="attend_new" if fresh else "attend_prefix",
    )(sub, prefix_len, where, *args)


def shards(
    q_nope,
    q_rope,
    new_latent,
    new_rope,
    pool_latent,
    pool_rope,
    w_uk,
    w_uv,
    block_list,
    prefix_len,
    block_slot,
):
    n = lax.axis_size("req")
    sub = lax.axis_index("sub")
    half = q_nope.shape[1] // 2
    swap = lambda a: lax.ppermute(a, "sub", [(0, 1), (1, 0)])
    cross = lambda a, k: lax.ppermute(a, "req", [(i, i ^ k) for i in range(n)])
    far = list(range(n - 1, 0, -1))
    keep = lambda a: pltpu.with_memory_space_constraint(a, pltpu.HBM)
    q_nope, q_rope, new_latent, w_uk, w_uv = map(keep, (q_nope, q_rope, new_latent, w_uk, w_uv))
    pool_latent = keep(pool_latent)
    pool_turned = keep(pool_rope.swapaxes(1, 2))
    rope_turned = keep(new_rope.T)
    got = {k: cross(block_list, k) for k in far}
    lists = [block_list] + [got[k] for k in range(1, n)]
    other = prepare(new_latent, q_nope, q_rope, rope_turned)
    other = swap(other)
    sent, where = pack(n, lists, block_slot, pool_latent, pool_turned)
    local = swap(sent[0])
    mine = [cross(sent[k], k) for k in far]
    theirs = [swap(a) for a in mine]
    common = (new_latent, rope_turned, q_nope, q_rope, other, w_uk, w_uv)
    state = attend([0], sub.reshape(1), prefix_len, where, [sent[0]], [local], *common, None)
    kept, gone = attend(far, sub.reshape(1), prefix_len, where, mine, theirs, *common, state)
    back = swap(gone)
    return lax.dynamic_update_slice_in_dim(kept, back, (1 - sub) * half, 1)


def solution(mesh):
    placed = (
        P(("groups", "req", "sub"), "head"),
        P(("groups", "req", "sub"), "head"),
        P(("groups", "req", "sub"), None),
        P(("groups", "req", "sub"), None),
        P(("groups", "req"), None, "sub"),
        P(("groups", "req"), None, None),
        P(None, "head"),
        P(None, "head"),
        P(("groups", "req"), None),
        P(("groups", "req")),
        P("groups"),
    )
    return jax.shard_map(
        shards,
        mesh=mesh,
        in_specs=placed,
        out_specs=P(("groups", "req", "sub"), "head"),
        check_vma=False,
    )
```

time: 56.9 us -> 62.9 us (1.11)
  Pallas kernels: 22.2 us -> 33.9 us
  local copies, waits for them, and re-layouts: 8.3 us -> 2.14 us
  waiting for transfers between devices: 14.2 us -> 15.1 us
    pallas_call x1 -> x3, Pallas kernels: 19.2 us -> 31.3 us  [the longest x2 30.1 us: attend(): pl.pallas_call(functools.partial(attend_kernel, steps, fresh), grid_spec=...]
    unnamed x26 -> x4, local copies, waits for them, and re-layouts: 4.34 us -> 1.31 us
    dynamic_slice x2 -> x0, local copies, waits for them, and re-layouts: 2.07 us -> none  [the longest x1 1.08 us: shards(): lax.dynamic_slice_in_dim(q_nope, (1 - sub) * half, half, 1)]
    ppermute x6, waiting for transfers between devices: 12 us -> 13.2 us  [shards(): cross = lambda a, k: lax.ppermute(a, 'req', [(i, i ^ k) for i in range(n)])]
    concatenate x1 -> x0, local copies, waits for them, and re-layouts: 1.06 us -> none  [shards(): jnp.concatenate([new_latent, lax.dynamic_slice_in_dim(q_nope, (1 - sub) *...]
  transfers between devices with their start and end apart: 12 -> 12, of which waited for: 6 -> 5; matrix products, arithmetic and copies ran while one was open for 3% -> 0% of each run, Pallas kernels for 5% -> 24%
where the time goes in v2:
time: 62.9 us; the launch traced here: 62.6 us
  Pallas kernels  33.9 us (54%)
  waiting for transfers between devices  15.1 us (24%)
  starting transfers between devices  10.8 us (17%)
  local copies, waits for them, and re-layouts  2.14 us (3%)
  between operations  0.71 us (1%)
    pallas_call x2, Pallas kernels, attend(): pl.pallas_call(functools.partial(attend_kernel, steps, fresh), grid_spec=...  30.1 us
    ppermute x6, waiting for transfers between devices, shards(): cross = lambda a, k: lax.ppermute(a, 'req', [(i, i ^ k) for i in range(n)])  13.2 us
    ppermute x6, starting transfers between devices, shards(): cross = lambda a, k: lax.ppermute(a, 'req', [(i, i ^ k) for i in range(n)])  9.68 us
    pallas_call x1, Pallas kernels, pack(): pl.pallas_call(body, out_shape=[jax.ShapeDtypeStruct((rows, width), jnp.b...  2.59 us
    ppermute x6, waiting for transfers between devices, shards(): swap = lambda a: lax.ppermute(a, 'sub', [(0, 1), (1, 0)])  1.92 us
    unnamed x4, local copies, waits for them, and re-layouts  1.31 us
  transfers between devices with their start and end apart: 12, of which 5 were waited for; matrix products, arithmetic and copies ran while one was open for 0% of the time, Pallas kernels for 24%

profile of v2, /device:TPU:0, one launch (start us, length us, event | category | flops | bytes accessed | tf_op | source)
XLA Modules:
  0.0 62.6 jit_solution(1230235782157048643)
XLA Ops:
  0.0 1.2 %prepare.1 = bf16[128,3712]{1,0:T(8,128)(2,1)S(1)} custom-call(bf16[128,512]{1,0:T(8,128)(2,1)} %refs_2_.1, bf16[128,4096]{1,0:T(8,128)(2,1)} %refs_6_.3, bf16[128,2048]{1,0:T(8,128)(2,1)} %refs_7_.3, bf16[64,128]{1,0:T(8,128)(2,1)} %bitcast.4), custom_call_target="tpu_custom_call" | custom-call | bytes 1900544 | tf_op jit(solution)/shard_map/prepare/pallas_call | solution.py:133
  1.2 0.6 collective-permute-start.9
  1.8 2.6 %collective-permute-start = (s32[1,6]{1,0:T(1,128)}, s32[1,6]{1,0:T(1,128)S(1)}, u32[]{:S(2)}, u32[]{:S(2)}) collective-permute-start(s32[1,6]{1,0:T(1,128)} %refs_0_.1), channel_id=1, source_target_pairs={{0,4},{4,0},{8,12},{12,8},{1,5},{5,1},{9,13},{13,9},{2,6},{6,2},{1... | collective-permute-start | bytes 80 | tf_op jit(solution)/shard_map/ppermute | solution.py:359
  4.4 2.6 %collective-permute-start.1 = (s32[1,6]{1,0:T(1,128)}, s32[1,6]{1,0:T(1,128)S(1)}, u32[]{:S(2)}, u32[]{:S(2)}) collective-permute-start(s32[1,6]{1,0:T(1,128)} %refs_0_.1), channel_id=1, source_target_pairs={{0,8},{4,12},{8,0},{12,4},{1,9},{5,13},{9,1},{13,5},{2,10},{6,14},... | collective-permute-start | bytes 80 | tf_op jit(solution)/shard_map/ppermute | solution.py:359
  7.0 2.0 %collective-permute-done.1.refs_2_ = s32[1,6]{1,0:T(1,128)S(1)} collective-permute-done((s32[1,6]{1,0:T(1,128)}, s32[1,6]{1,0:T(1,128)S(1)}, u32[]{:S(2)}, u32[]{:S(2)}) %collective-permute-start.1) | collective-permute-done | bytes 56 | tf_op jit(solution)/shard_map/ppermute | solution.py:359
  9.0 3.5 %collective-permute-done.2.refs_3_ = s32[1,6]{1,0:T(1,128)S(1)} collective-permute-done((s32[1,6]{1,0:T(1,128)}, s32[1,6]{1,0:T(1,128)S(1)}, u32[]{:S(2)}, u32[]{:S(2)}) %collective-permute-start.2) | collective-permute-done | bytes 56 | tf_op jit(solution)/shard_map/ppermute | solution.py:359
  12.5 0.7 %copy-done = s32[1,6]{1,0:T(1,128)S(1)} copy-done((s32[1,6]{1,0:T(1,128)S(1)}, s32[1,6]{1,0:T(1,128)}, u32[]{:S(2)}) %copy-start) | copy-done | bytes 48
  13.2 0.7 %copy-done.1 = s32[64]{0:T(128)S(1)} copy-done((s32[64]{0:T(128)S(1)}, s32[64]{0:T(128)}, u32[]{:S(2)}) %copy-start.1) | copy-done | bytes 280
  13.8 2.6 %pack.1 = (bf16[288,256]{1,0:T(8,128)(2,1)S(1)}, bf16[288,256]{1,0:T(8,128)(2,1)S(1)}, bf16[288,256]{1,0:T(8,128)(2,1)S(1)}, bf16[288,256]{1,0:T(8,128)(2,1)S(1)}, s32[8]{0:T(128)S(1)}) custom-call(s32[1,6]{1,0:T(1,128)S(1)} %copy-done, s32[1,6]{1,0:T(1,128)S(1)} %collective-permute-done.refs_1_, s32[1,6]{1,0:T(1,128)S(1)} %collective-permute-done.1.refs_2_, ...), custom_call_target="tpu_custom_call" | custom-call | bytes 1179648 | tf_op jit(solution)/shard_map/pack/pallas_call | solution.py:83
  16.4 0.1 collective-permute-start.3
  16.5 0.1 collective-permute-start.4
  16.6 4.3 %collective-permute-start.5 = (bf16[288,256]{1,0:T(8,128)(2,1)S(1)}, bf16[288,256]{1,0:T(8,128)(2,1)S(1)}, u32[]{:S(2)}, u32[]{:S(2)}) collective-permute-start(bf16[288,256]{1,0:T(8,128)(2,1)S(1)} %get-tuple-element.17), channel_id=1, source_target_pairs={{0,4},{4,0},{8,12},{12,8},{1,5},{5,1},{9,13},{13,9},{2,6},{6,2},{1... | collective-permute-start | bytes 442376 | tf_op jit(solution)/shard_map/ppermute | solution.py:359
  20.9 0.0 collective-permute-start.10
  21.5 3.5 %collective-permute-done.3.refs_0_ = bf16[288,256]{1,0:T(8,128)(2,1)S(1)} collective-permute-done((bf16[288,256]{1,0:T(8,128)(2,1)S(1)}, bf16[288,256]{1,0:T(8,128)(2,1)S(1)}, u32[]{:S(2)}, u32[]{:S(2)}) %collective-permute-start.3) | collective-permute-done | bytes 147488 | tf_op jit(solution)/shard_map/ppermute | solution.py:359
  25.0 0.0 collective-permute-start.6
  25.0 4.2 %collective-permute-done.4.refs_1_ = bf16[288,256]{1,0:T(8,128)(2,1)S(1)} collective-permute-done((bf16[288,256]{1,0:T(8,128)(2,1)S(1)}, bf16[288,256]{1,0:T(8,128)(2,1)S(1)}, u32[]{:S(2)}, u32[]{:S(2)}) %collective-permute-start.4) | collective-permute-done | bytes 147488 | tf_op jit(solution)/shard_map/ppermute | solution.py:359
  29.2 0.5 collective-permute-start.8
  29.7 0.0 collective-permute-done.9.refs_4_.refs_5_.refs_8_.refs_9_
  29.7 12.4 %attend_new.1 = (f32[256,2048]{1,0:T(8,128)S(1)}, f32[256,1024]{1,0:T(8,128)S(1)}) custom-call(s32[1]{0:T(128)} %bitcast.sub_ref, s32[1]{0:T(128)S(6)} %copy.13.len_ref, s32[8]{0:T(128)S(1)} %get-tuple-element.14.where_ref, bf16[288,256]{1,0:T(8,128)(2,1)S(1)} %get-tuple-element.18.refs_0_, bf16[288,256]{1,0:T(8,128)(2,1)S(1)} %collective-permute-done.10.refs_1_, ...), custom_call_target="tpu_custom_call" | custom-call | flops 4294967296 | bytes 8388608 | tf_op jit(solution)/shard_map/attend_new/pallas_call | solution.py:322
  42.1 0.0 collective-permute-done.6.refs_3_
  42.1 0.0 collective-permute-done.7.refs_4_
  42.1 17.8 %attend_prefix.1 = (bf16[128,4096]{1,0:T(8,128)(2,1)}, bf16[128,2048]{1,0:T(8,128)(2,1)S(1)}) custom-call(s32[1]{0:T(128)} %bitcast.sub_ref, s32[1]{0:T(128)S(6)} %copy.13.len_ref, s32[8]{0:T(128)S(1)} %get-tuple-element.14.where_ref, bf16[288,256]{1,0:T(8,128)(2,1)S(1)} %collective-permute-done.3.refs_0_, ...), custom_call_target="tpu_custom_call" | custom-call | flops 6442450944 | bytes 8388608 | tf_op jit(solution)/shard_map/attend_prefix/pallas_call | solution.py:322
  59.9 1.9 %collective-permute-done.11 = bf16[128,2048]{1,0:T(8,128)(2,1)S(1)} collective-permute-done((bf16[128,2048]{1,0:T(8,128)(2,1)S(1)}, bf16[128,2048]{1,0:T(8,128)(2,1)S(1)}, u32[]{:S(2)}, u32[]{:S(2)}) %collective-permute-start.11) | collective-permute-done | bytes 524320 | tf_op jit(solution)/shard_map/ppermute | solution.py:358
  61.8 0.8 %constant_dynamic-update-slice_fusion = bf16[128,4096]{1,0:T(8,128)(2,1)} fusion(bf16[128,4096]{1,0:T(8,128)(2,1)} %get-tuple-element.21, bf16[128,2048]{1,0:T(8,128)(2,1)S(1)} %collective-permute-done.11, s32[]{:T(128)S(6)} %select_n.3), kind=kLoop, calls=%fused_computation | loop fusion | bytes 1048580 | tf_op jit(solution)/shard_map/dynamic_update_slice | solution.py:378
  (9 shorter events, 0.0 us)
Async XLA Ops:
  1.2 28.5 %collective-permute-start.9 = (bf16[128,3712]{1,0:T(8,128)(2,1)S(1)}, bf16[128,3712]{1,0:T(8,128)(2,1)S(1)}, u32[]{:S(2)}, u32[]{:S(2)}) collective-permute-start(bf16[128,3712]{1,0:T(8,128)(2,1)S(1)} %prepare.1), channel_id=1, source_target_pairs={{0,1},{1,0},{2,3},{3,2},{4,5},{5,4},{6,7},{7,6},{8,9},{9,8},{10,11... | collective-permute-start | bytes 2850824 | tf_op jit(solution)/shard_map/ppermute | solution.py:358
  1.8 5.2 %collective-permute-start = (s32[1,6]{1,0:T(1,128)}, s32[1,6]{1,0:T(1,128)S(1)}, u32[]{:S(2)}, u32[]{:S(2)}) collective-permute-start(s32[1,6]{1,0:T(1,128)} %refs_0_.1), channel_id=1, source_target_pairs={{0,4},{4,0},{8,12},{12,8},{1,5},{5,1},{9,13},{13,9},{2,6},{6,2},{1... | collective-permute-start | bytes 80 | tf_op jit(solution)/shard_map/ppermute | solution.py:359
  4.4 4.6 %collective-permute-start.1 = (s32[1,6]{1,0:T(1,128)}, s32[1,6]{1,0:T(1,128)S(1)}, u32[]{:S(2)}, u32[]{:S(2)}) collective-permute-start(s32[1,6]{1,0:T(1,128)} %refs_0_.1), channel_id=1, source_target_pairs={{0,8},{4,12},{8,0},{12,4},{1,9},{5,13},{9,1},{13,5},{2,10},{6,14},... | collective-permute-start | bytes 80 | tf_op jit(solution)/shard_map/ppermute | solution.py:359
  7.0 5.5 %collective-permute-start.2 = (s32[1,6]{1,0:T(1,128)}, s32[1,6]{1,0:T(1,128)S(1)}, u32[]{:S(2)}, u32[]{:S(2)}) collective-permute-start(s32[1,6]{1,0:T(1,128)} %refs_0_.1), channel_id=1, source_target_pairs={{0,12},{4,8},{8,4},{12,0},{1,13},{5,9},{9,5},{13,1},{2,14},{6,10},... | collective-permute-start | bytes 80 | tf_op jit(solution)/shard_map/ppermute | solution.py:359
  12.5 0.7 %copy-start = (s32[1,6]{1,0:T(1,128)S(1)}, s32[1,6]{1,0:T(1,128)}, u32[]{:S(2)}) copy-start(s32[1,6]{1,0:T(1,128)} %refs_0_.1) | copy-start | bytes 76
  13.2 0.7 %copy-start.1 = (s32[64]{0:T(128)S(1)}, s32[64]{0:T(128)}, u32[]{:S(2)}) copy-start(s32[64]{0:T(128)} %refs_4_.1) | copy-start | bytes 772
  16.4 8.6 %collective-permute-start.3 = (bf16[288,256]{1,0:T(8,128)(2,1)S(1)}, bf16[288,256]{1,0:T(8,128)(2,1)S(1)}, u32[]{:S(2)}, u32[]{:S(2)}) collective-permute-start(bf16[288,256]{1,0:T(8,128)(2,1)S(1)} %get-tuple-element.15), channel_id=1, source_target_pairs={{0,12},{4,8},{8,4},{12,0},{1,13},{5,9},{9,5},{13,1},{2,14},{6,10},... | collective-permute-start | bytes 442376 | tf_op jit(solution)/shard_map/ppermute | solution.py:359
  16.5 12.7 %collective-permute-start.4 = (bf16[288,256]{1,0:T(8,128)(2,1)S(1)}, bf16[288,256]{1,0:T(8,128)(2,1)S(1)}, u32[]{:S(2)}, u32[]{:S(2)}) collective-permute-start(bf16[288,256]{1,0:T(8,128)(2,1)S(1)} %get-tuple-element.16), channel_id=1, source_target_pairs={{0,8},{4,12},{8,0},{12,4},{1,9},{5,13},{9,1},{13,5},{2,10},{6,14},... | collective-permute-start | bytes 442376 | tf_op jit(solution)/shard_map/ppermute | solution.py:359
  16.6 12.6 %collective-permute-start.5 = (bf16[288,256]{1,0:T(8,128)(2,1)S(1)}, bf16[288,256]{1,0:T(8,128)(2,1)S(1)}, u32[]{:S(2)}, u32[]{:S(2)}) collective-permute-start(bf16[288,256]{1,0:T(8,128)(2,1)S(1)} %get-tuple-element.17), channel_id=1, source_target_pairs={{0,4},{4,0},{8,12},{12,8},{1,5},{5,1},{9,13},{13,9},{2,6},{6,2},{1... | collective-permute-start | bytes 442376 | tf_op jit(solution)/shard_map/ppermute | solution.py:359
  20.9 8.8 %collective-permute-start.10 = (bf16[288,256]{1,0:T(8,128)(2,1)S(1)}, bf16[288,256]{1,0:T(8,128)(2,1)S(1)}, u32[]{:S(2)}, u32[]{:S(2)}) collective-permute-start(bf16[288,256]{1,0:T(8,128)(2,1)S(1)} %get-tuple-element.18.refs_0_), channel_id=1, source_target_pairs={{0,1},{1,0},{2,3},{3,2},{4,5},{5,4},{6,7},{7,6},{8,9},{9,8},{10,11... | collective-permute-start | bytes 442376 | tf_op jit(solution)/shard_map/ppermute | solution.py:358
  25.0 17.1 %collective-permute-start.6 = (bf16[288,256]{1,0:T(8,128)(2,1)S(1)}, bf16[288,256]{1,0:T(8,128)(2,1)S(1)}, u32[]{:S(2)}, u32[]{:S(2)}) collective-permute-start(bf16[288,256]{1,0:T(8,128)(2,1)S(1)} %collective-permute-done.3.refs_0_), channel_id=1, source_target_pairs={{0,1},{1,0},{2,3},{3,2},{4,5},{5,4},{6,7},{7,6},{8,9},{9,8},{10,11... | collective-permute-start | bytes 442376 | tf_op jit(solution)/shard_map/ppermute | solution.py:358
  29.2 12.9 %collective-permute-start.7 = (bf16[288,256]{1,0:T(8,128)(2,1)S(1)}, bf16[288,256]{1,0:T(8,128)(2,1)S(1)}, u32[]{:S(2)}, u32[]{:S(2)}) collective-permute-start(bf16[288,256]{1,0:T(8,128)(2,1)S(1)} %collective-permute-done.4.refs_1_), channel_id=1, source_target_pairs={{0,1},{1,0},{2,3},{3,2},{4,5},{5,4},{6,7},{7,6},{8,9},{9,8},{10,11... | collective-permute-start | bytes 442376 | tf_op jit(solution)/shard_map/ppermute | solution.py:358
  29.2 12.9 %collective-permute-start.8 = (bf16[288,256]{1,0:T(8,128)(2,1)S(1)}, bf16[288,256]{1,0:T(8,128)(2,1)S(1)}, u32[]{:S(2)}, u32[]{:S(2)}) collective-permute-start(bf16[288,256]{1,0:T(8,128)(2,1)S(1)} %collective-permute-done.5.refs_2_), channel_id=1, source_target_pairs={{0,1},{1,0},{2,3},{3,2},{4,5},{5,4},{6,7},{7,6},{8,9},{9,8},{10,11... | collective-permute-start | bytes 442376 | tf_op jit(solution)/shard_map/ppermute | solution.py:358
  59.9 1.9 %collective-permute-start.11 = (bf16[128,2048]{1,0:T(8,128)(2,1)S(1)}, bf16[128,2048]{1,0:T(8,128)(2,1)S(1)}, u32[]{:S(2)}, u32[]{:S(2)}) collective-permute-start(bf16[128,2048]{1,0:T(8,128)(2,1)S(1)} %get-tuple-element.22), channel_id=1, source_target_pairs={{0,1},{1,0},{2,3},{3,2},{4,5},{5,4},{6,7},{7,6},{8,9},{9,8},{10,11... | collective-permute-start | bytes 1572872 | tf_op jit(solution)/shard_map/ppermute | solution.py:358

commit v3 on v2

--- a/solution.py
+++ b/solution.py
@@ -145,31 +145,36 @@
 RATE = math.log2(math.e) / math.sqrt(NOPE + ROPE)
 
 
-def attend_kernel(steps, fresh, sub_ref, len_ref, where_ref, *refs):
+def attend_kernel(steps, fresh, pairs, sub_ref, len_ref, where_ref, *refs):
     count = len(steps)
     mine = refs[:count]
     theirs = refs[count : 2 * count]
     refs = refs[2 * count :]
     if fresh:
         lat_a, rope_a, lat_b, rope_b, *refs = refs
-        qn_a, qr_a, qn_b, qr_b, wk_ref, wv_ref, acc_ref, stat_ref, lat, tails, bias = refs
+        (qn_a, qr_a, qn_b, qr_b, wk_ref, wv_ref, acc_ref, stat_ref,
+         lat, kc, vc, score, weight, peak, bias) = refs
     else:
-        (qn_a, qr_a, qn_b, qr_b, wk_ref, wv_ref, acc_ref, stat_ref, out_ref, send_ref, lat,
-         tails) = refs
+        (qn_a, qr_a, qn_b, qr_b, wk_ref, wv_ref, acc_ref, stat_ref, out_ref, send_ref,
+         lat, kc, vc, score, weight, peak) = refs
     sub = sub_ref[0]
     block = qn_a.shape[0]
     chunk = CAP * block
     first = chunk if fresh else 0
     queries = 2 * block
-
-    @pl.when(pl.program_id(0) == 0)
+    keys = lat.shape[0]
+    g = pl.program_id(0)
+    head = lambda j: slice(j * LANES, (j + 1) * LANES)
+
+    @pl.when(g == 0)
     def _():
         def put_tails(base, rope, mask):
-            tails[0, base : base + block, :] = jnp.concatenate([rope, mask], axis=1)
-            tails[1, base : base + block, :] = jnp.concatenate([mask, rope], axis=1)
+            kc[0, base : base + block, NOPE:] = jnp.concatenate([rope, mask], axis=1)
+            kc[1, base : base + block, NOPE:] = jnp.concatenate([mask, rope], axis=1)
 
         lane = lax.broadcasted_iota(jnp.int32, (block, ROPE), 1)
         row = lax.broadcasted_iota(jnp.int32, (block, ROPE), 0)
+        vc[:, :, VDIM:] = jnp.ones((2, keys, LANES), jnp.bfloat16)
         for i, k in enumerate(steps):
             width = mine[i].shape[1]
             here = pl.multiple_of(sub * width, width)
@@ -199,67 +204,71 @@
             seen = jnp.bitwise_xor(j, flip) <= jnp.bitwise_xor(i, flip)
             bias[...] = jnp.where(seen, 0.0, HIDE)
 
-    chunks = count + (1 if fresh else 0)
-    qn = jnp.concatenate([qn_a[...], qn_b[...]], axis=0)
-    qr = jnp.concatenate([qr_a[...], qr_b[...]], axis=0)
-    lane = lax.broadcasted_iota(jnp.int32, (queries, LANES), 1)
-    ones = jnp.ones((chunk, LANES), jnp.bfloat16)
-    qc = []
-    for j in range(2):
-        fill = jnp.where(lane == (1 - j) * ROPE, 1.0, 0.0).astype(jnp.bfloat16)
-        own = (lane >= ROPE) if j else (lane < ROPE)
-        qc.append(
-            jnp.concatenate([qn[:, j * NOPE : (j + 1) * NOPE], jnp.where(own, qr, fill)], axis=1)
-        )
-    scores = [[], []]
-    values = []
-    for i in range(chunks):
-        keys = lat[i * chunk : (i + 1) * chunk, :]
-        k2 = jnp.dot(keys, wk_ref[...], preferred_element_type=jnp.float32).astype(jnp.bfloat16)
-        v2 = jnp.dot(keys, wv_ref[...], preferred_element_type=jnp.float32).astype(jnp.bfloat16)
-        values.append(v2)
+    def step(produce, consume):
+        lane = lax.broadcasted_iota(jnp.int32, (queries, LANES), 1)
+        if consume:
+            top, keep, total = [], [], []
+            for j in range(2):
+                most = peak[j]
+                if not fresh:
+                    stat = stat_ref[:, head(j)]
+                    turned = pltpu.roll(stat, LANES // 2, 1)
+                    before = jnp.where(lane < LANES // 2, stat, turned)
+                    total.append(jnp.where(lane < LANES // 2, turned, stat))
+                    most = jnp.maximum(most, before)
+                    keep.append(jnp.exp2((before - most) * RATE))
+                top.append(most)
+                for i in range(keys // LANES):
+                    s = score[j, :, i * LANES : (i + 1) * LANES]
+                    weight[j, :, i * LANES : (i + 1) * LANES] = jnp.exp2((s - most) * RATE).astype(
+                        jnp.bfloat16
+                    )
+        for i in range(keys // chunk):
+            rows = slice(i * chunk, (i + 1) * chunk)
+            if produce:
+                k2 = jnp.dot(lat[rows, :], wk_ref[...], preferred_element_type=jnp.float32)
+                for j in range(2):
+                    kc[j, rows, :NOPE] = k2[:, head(j)].astype(jnp.bfloat16)
+            if consume:
+                v2 = jnp.dot(lat[rows, :], wv_ref[...], preferred_element_type=jnp.float32)
+                for j in range(2):
+                    vc[j, rows, :VDIM] = v2[:, head(j)].astype(jnp.bfloat16)
         for j in range(2):
-            kc = jnp.concatenate(
-                [k2[:, j * NOPE : (j + 1) * NOPE], tails[j, i * chunk : (i + 1) * chunk, :]], axis=1
-            )
-            s = lax.dot_general(
-                qc[j], kc, (((1,), (1,)), ((), ())), preferred_element_type=jnp.float32
-            )
-            if fresh and i == 0:
-                s = s + bias[...]
-            scores[j].append(s)
-    peaks = []
-    sums = []
-    for j in range(2):
-        peak = functools.reduce(jnp.maximum, scores[j])
-        peak = jnp.max(peak, axis=1, keepdims=True)
-        if not fresh:
-            before = stat_ref[:, j : j + 1]
-            peak = jnp.maximum(peak, before)
-        o = None
-        for i in range(chunks):
-            e = jnp.exp2((scores[j][i] - peak) * RATE).astype(jnp.bfloat16)
-            vc = jnp.concatenate([values[i][:, j * VDIM : (j + 1) * VDIM], ones], axis=1)
-            part = jnp.dot(e, vc, preferred_element_type=jnp.float32)
-            o = part if o is None else o + part
-        total = o[:, VDIM:]
-        o = o[:, :VDIM]
-        if fresh:
-            acc_ref[:, j * VDIM : (j + 1) * VDIM] = o
-            peaks.append(peak)
-            sums.append(total)
-        else:
-            keep = jnp.exp2((before - peak) * RATE)
-            total = total[:, :1] + keep * stat_ref[:, 2 + j : 3 + j]
-            o = o + keep * acc_ref[:, j * VDIM : (j + 1) * VDIM]
-            o = (o / total).astype(jnp.bfloat16)
-            out_ref[:, j * VDIM : (j + 1) * VDIM] = o[:block]
-            send_ref[:, j * VDIM : (j + 1) * VDIM] = o[block:]
-    if fresh:
-        stat_ref[...] = jnp.where(
-            lane == 0, peaks[0],
-            jnp.where(lane == 1, peaks[1], jnp.where(lane == 2, sums[0], sums[1])),
-        )
+            if consume:
+                o = jnp.dot(weight[j], vc[j], preferred_element_type=jnp.float32)
+                o, norm = o[:, :VDIM], o[:, VDIM:]
+                if fresh:
+                    acc_ref[:, head(j)] = o
+                    stat_ref[:, head(j)] = jnp.where(lane < LANES // 2, top[j], norm)
+                else:
+                    norm = norm + keep[j] * total[j]
+                    o = o + keep[j] * acc_ref[:, head(j)]
+                    o = (o / norm).astype(jnp.bfloat16)
+                    out_ref[:, head(j)] = o[:block]
+                    send_ref[:, head(j)] = o[block:]
+            if produce:
+                qn = jnp.concatenate([qn_a[:, head(j)], qn_b[:, head(j)]], axis=0)
+                qr = jnp.concatenate([qr_a[...], qr_b[...]], axis=0)
+                fill = jnp.where(lane == (1 - j) * ROPE, 1.0, 0.0).astype(jnp.bfloat16)
+                own = (lane >= ROPE) if j else (lane < ROPE)
+                qc = jnp.concatenate([qn, jnp.where(own, qr, fill)], axis=1)
+                most = None
+                for i in range(keys // chunk):
+                    s = lax.dot_general(
+                        qc, kc[j, i * chunk : (i + 1) * chunk, :], (((1,), (1,)), ((), ())),
+                        preferred_element_type=jnp.float32,
+                    )
+                    if fresh and i == 0:
+                        s = s + bias[...]
+                    score[j, :, i * chunk : (i + 1) * chunk] = s
+                    for part in range(chunk // LANES):
+                        piece = s[:, head(part)]
+                        most = piece if most is None else jnp.maximum(most, piece)
+                peak[j] = jnp.broadcast_to(jnp.max(most, axis=1, keepdims=True), (queries, LANES))
+
+    pl.when(g == 0)(lambda: step(True, False))
+    pl.when((g > 0) & (g < pairs))(lambda: step(True, True))
+    pl.when(g == pairs)(lambda: step(False, True))
 
 
 def attend(steps, sub, prefix_len, where, mine, theirs, new_latent, rope_turned, q_nope, q_rope,
@@ -274,16 +283,19 @@
     rope_at = nope_at + heads * NOPE
     tail_at = rope_at + heads * ROPE
 
+    now = lambda g: jnp.minimum(g, pairs - 1)
+    past = lambda g: jnp.maximum(g - 1, 0)
+
     def at(width, first, follow):
         if follow:
-            return pl.BlockSpec((block, width), lambda g, *_: (0, first // width + g))
+            return pl.BlockSpec((block, width), lambda g, *_: (0, first // width + now(g)))
         return pl.BlockSpec((block, width), lambda g, *_: (0, first // width))
 
-    def ours(rows, width):
-        return pl.BlockSpec((rows, width), lambda g, s, *_: (0, s[0] * pairs + g))
+    def ours(rows, width, when):
+        return pl.BlockSpec((rows, width), lambda g, s, *_: (0, s[0] * pairs + when(g)))
 
     def step(rows, width):
-        return pl.BlockSpec((rows, width), lambda g, *_: (0, g))
+        return pl.BlockSpec((rows, width), lambda g, *_: (0, past(g)))
 
     specs = [whole(a) for a in mine] + [whole(a) for a in theirs]
     args = [*mine, *theirs]
@@ -291,39 +303,43 @@
         specs += [whole(new_latent), whole(rope_turned), at(latent, 0, False), at(LANES, tail_at, False)]
         args += [new_latent, rope_turned, other, other]
     specs += [
-        ours(block, 2 * NOPE),
-        ours(block, 2 * ROPE),
+        ours(block, 2 * NOPE, now),
+        ours(block, 2 * ROPE, now),
         at(2 * NOPE, nope_at, True),
         at(2 * ROPE, rope_at, True),
-        ours(latent, 2 * NOPE),
-        ours(latent, 2 * VDIM),
+        ours(latent, 2 * NOPE, now),
+        ours(latent, 2 * VDIM, past),
     ]
     args += [q_nope, q_rope, other, other, w_uk, w_uv]
-    state_specs = [step(2 * block, 2 * VDIM), step(2 * block, LANES)]
+    state_specs = [step(2 * block, 2 * VDIM), step(2 * block, 2 * LANES)]
     scratch = [
         pltpu.VMEM((keys, latent), jnp.bfloat16),
-        pltpu.VMEM((2, keys, LANES), jnp.bfloat16),
+        pltpu.VMEM((2, keys, NOPE + LANES), jnp.bfloat16),
+        pltpu.VMEM((2, keys, VDIM + LANES), jnp.bfloat16),
+        pltpu.VMEM((2, 2 * block, keys), jnp.float32),
+        pltpu.VMEM((2, 2 * block, keys), jnp.bfloat16),
+        pltpu.VMEM((2, 2 * block, LANES), jnp.float32),
     ]
     if fresh:
         out_specs = state_specs
         out_shape = [
             jax.ShapeDtypeStruct((2 * block, heads * VDIM), jnp.float32),
-            jax.ShapeDtypeStruct((2 * block, pairs * LANES), jnp.float32),
+            jax.ShapeDtypeStruct((2 * block, heads * LANES), jnp.float32),
         ]
         scratch.append(pltpu.VMEM((2 * block, 2 * block), jnp.float32))
     else:
         specs += state_specs
         args += state
-        out_specs = [ours(block, 2 * VDIM), step(block, 2 * VDIM)]
+        out_specs = [ours(block, 2 * VDIM, past), step(block, 2 * VDIM)]
         out_shape = [
             jax.ShapeDtypeStruct((block, 2 * heads * VDIM), jnp.bfloat16),
             jax.ShapeDtypeStruct((block, heads * VDIM), jnp.bfloat16),
         ]
     return pl.pallas_call(
-        functools.partial(attend_kernel, steps, fresh),
+        functools.partial(attend_kernel, steps, fresh, pairs),
         grid_spec=pltpu.PrefetchScalarGridSpec(
             num_scalar_prefetch=3,
-            grid=(pairs,),
+            grid=(pairs + 1,),
             in_specs=specs,
             out_specs=out_specs,
             scratch_shapes=scratch,

time: 62.9 us -> 57.6 us (0.916)
  Pallas kernels: 33.9 us -> 28.6 us
    pallas_call x2, Pallas kernels: 30.1 us -> 24.8 us  [attend(): pl.pallas_call(functools.partial(attend_kernel, steps, fresh, pairs), gri...]
where the time goes in v3:
time: 57.6 us; the launch traced here: 57.3 us
  Pallas kernels  28.6 us (50%)
  waiting for transfers between devices  15.1 us (26%)
  starting transfers between devices  10.8 us (19%)
  local copies, waits for them, and re-layouts  2.14 us (4%)
  between operations  0.71 us (1%)
    pallas_call x2, Pallas kernels, attend(): pl.pallas_call(functools.partial(attend_kernel, steps, fresh, pairs), gri...  24.8 us
    ppermute x6, waiting for transfers between devices, shards(): cross = lambda a, k: lax.ppermute(a, 'req', [(i, i ^ k) for i in range(n)])  13.2 us
    ppermute x6, starting transfers between devices, shards(): cross = lambda a, k: lax.ppermute(a, 'req', [(i, i ^ k) for i in range(n)])  9.68 us
    pallas_call x1, Pallas kernels, pack(): pl.pallas_call(body, out_shape=[jax.ShapeDtypeStruct((rows, width), jnp.b...  2.59 us
    ppermute x6, waiting for transfers between devices, shards(): swap = lambda a: lax.ppermute(a, 'sub', [(0, 1), (1, 0)])  1.9 us
    unnamed x4, local copies, waits for them, and re-layouts  1.31 us
    pallas_call x1, Pallas kernels, prepare(): pl.pallas_call(prepare_kernel, out_shape=jax.ShapeDtypeStruct((rows, widt...  1.21 us
  transfers between devices with their start and end apart: 12, of which 5 were waited for; matrix products, arithmetic and copies ran while one was open for 0% of the time, Pallas kernels for 24%

profile of v3, /device:TPU:0, one launch (start us, length us, event | category | flops | bytes accessed | tf_op | source)
XLA Modules:
  0.0 57.3 jit_solution(9066671703434025206)
XLA Ops:
  0.0 1.2 %prepare.1 = bf16[128,3712]{1,0:T(8,128)(2,1)S(1)} custom-call(bf16[128,512]{1,0:T(8,128)(2,1)} %refs_2_.1, bf16[128,4096]{1,0:T(8,128)(2,1)} %refs_6_.3, bf16[128,2048]{1,0:T(8,128)(2,1)} %refs_7_.3, bf16[64,128]{1,0:T(8,128)(2,1)} %bitcast.4), custom_call_target="tpu_custom_call" | custom-call | bytes 1900544 | tf_op jit(solution)/shard_map/prepare/pallas_call | solution.py:133
  1.2 0.6 collective-permute-start.9
  1.8 2.6 %collective-permute-start = (s32[1,6]{1,0:T(1,128)}, s32[1,6]{1,0:T(1,128)S(1)}, u32[]{:S(2)}, u32[]{:S(2)}) collective-permute-start(s32[1,6]{1,0:T(1,128)} %refs_0_.1), channel_id=1, source_target_pairs={{0,4},{4,0},{8,12},{12,8},{1,5},{5,1},{9,13},{13,9},{2,6},{6,2},{1... | collective-permute-start | bytes 80 | tf_op jit(solution)/shard_map/ppermute | solution.py:375
  4.4 2.6 %collective-permute-start.1 = (s32[1,6]{1,0:T(1,128)}, s32[1,6]{1,0:T(1,128)S(1)}, u32[]{:S(2)}, u32[]{:S(2)}) collective-permute-start(s32[1,6]{1,0:T(1,128)} %refs_0_.1), channel_id=1, source_target_pairs={{0,8},{4,12},{8,0},{12,4},{1,9},{5,13},{9,1},{13,5},{2,10},{6,14},... | collective-permute-start | bytes 80 | tf_op jit(solution)/shard_map/ppermute | solution.py:375
  7.0 2.0 %collective-permute-done.1.refs_2_ = s32[1,6]{1,0:T(1,128)S(1)} collective-permute-done((s32[1,6]{1,0:T(1,128)}, s32[1,6]{1,0:T(1,128)S(1)}, u32[]{:S(2)}, u32[]{:S(2)}) %collective-permute-start.1) | collective-permute-done | bytes 56 | tf_op jit(solution)/shard_map/ppermute | solution.py:375
  9.0 3.5 %collective-permute-done.2.refs_3_ = s32[1,6]{1,0:T(1,128)S(1)} collective-permute-done((s32[1,6]{1,0:T(1,128)}, s32[1,6]{1,0:T(1,128)S(1)}, u32[]{:S(2)}, u32[]{:S(2)}) %collective-permute-start.2) | collective-permute-done | bytes 56 | tf_op jit(solution)/shard_map/ppermute | solution.py:375
  12.5 0.7 %copy-done = s32[1,6]{1,0:T(1,128)S(1)} copy-done((s32[1,6]{1,0:T(1,128)S(1)}, s32[1,6]{1,0:T(1,128)}, u32[]{:S(2)}) %copy-start) | copy-done | bytes 48
  13.2 0.7 %copy-done.1 = s32[64]{0:T(128)S(1)} copy-done((s32[64]{0:T(128)S(1)}, s32[64]{0:T(128)}, u32[]{:S(2)}) %copy-start.1) | copy-done | bytes 280
  13.8 2.6 %pack.1 = (bf16[288,256]{1,0:T(8,128)(2,1)S(1)}, bf16[288,256]{1,0:T(8,128)(2,1)S(1)}, bf16[288,256]{1,0:T(8,128)(2,1)S(1)}, bf16[288,256]{1,0:T(8,128)(2,1)S(1)}, s32[8]{0:T(128)S(1)}) custom-call(s32[1,6]{1,0:T(1,128)S(1)} %copy-done, s32[1,6]{1,0:T(1,128)S(1)} %collective-permute-done.refs_1_, s32[1,6]{1,0:T(1,128)S(1)} %collective-permute-done.1.refs_2_, ...), custom_call_target="tpu_custom_call" | custom-call | bytes 1179648 | tf_op jit(solution)/shard_map/pack/pallas_call | solution.py:83
  16.4 0.1 collective-permute-start.3
  16.5 0.1 collective-permute-start.4
  16.6 4.3 %collective-permute-start.5 = (bf16[288,256]{1,0:T(8,128)(2,1)S(1)}, bf16[288,256]{1,0:T(8,128)(2,1)S(1)}, u32[]{:S(2)}, u32[]{:S(2)}) collective-permute-start(bf16[288,256]{1,0:T(8,128)(2,1)S(1)} %get-tuple-element.17), channel_id=1, source_target_pairs={{0,4},{4,0},{8,12},{12,8},{1,5},{5,1},{9,13},{13,9},{2,6},{6,2},{1... | collective-permute-start | bytes 442376 | tf_op jit(solution)/shard_map/ppermute | solution.py:375
  20.9 0.0 collective-permute-start.10
  21.5 3.5 %collective-permute-done.3.refs_0_ = bf16[288,256]{1,0:T(8,128)(2,1)S(1)} collective-permute-done((bf16[288,256]{1,0:T(8,128)(2,1)S(1)}, bf16[288,256]{1,0:T(8,128)(2,1)S(1)}, u32[]{:S(2)}, u32[]{:S(2)}) %collective-permute-start.3) | collective-permute-done | bytes 147488 | tf_op jit(solution)/shard_map/ppermute | solution.py:375
  25.0 0.0 collective-permute-start.6
  25.0 4.2 %collective-permute-done.4.refs_1_ = bf16[288,256]{1,0:T(8,128)(2,1)S(1)} collective-permute-done((bf16[288,256]{1,0:T(8,128)(2,1)S(1)}, bf16[288,256]{1,0:T(8,128)(2,1)S(1)}, u32[]{:S(2)}, u32[]{:S(2)}) %collective-permute-start.4) | collective-permute-done | bytes 147488 | tf_op jit(solution)/shard_map/ppermute | solution.py:375
  29.2 0.5 collective-permute-start.8
  29.7 0.0 collective-permute-done.9.refs_4_.refs_5_.refs_8_.refs_9_
  29.7 11.1 %attend_new.1 = (f32[256,2048]{1,0:T(8,128)S(1)}, f32[256,2048]{1,0:T(8,128)S(1)}) custom-call(s32[1]{0:T(128)} %bitcast.sub_ref, s32[1]{0:T(128)S(6)} %copy.13.len_ref, s32[8]{0:T(128)S(1)} %get-tuple-element.14.where_ref, bf16[288,256]{1,0:T(8,128)(2,1)S(1)} %get-tuple-element.18.refs_0_, bf16[288,256]{1,0:T(8,128)(2,1)S(1)} %collective-permute-done.10.refs_1_, ...), custom_call_target="tpu_custom_call" | custom-call | flops 4294967296 | bytes 8388608 | tf_op jit(solution)/shard_map/attend_new/pallas_call | solution.py:338
  40.8 0.0 collective-permute-done.7.refs_4_
  40.8 13.7 %attend_prefix.1 = (bf16[128,4096]{1,0:T(8,128)(2,1)}, bf16[128,2048]{1,0:T(8,128)(2,1)S(1)}) custom-call(s32[1]{0:T(128)} %bitcast.sub_ref, s32[1]{0:T(128)S(6)} %copy.13.len_ref, s32[8]{0:T(128)S(1)} %get-tuple-element.14.where_ref, bf16[288,256]{1,0:T(8,128)(2,1)S(1)} %collective-permute-done.3.refs_0_, ...), custom_call_target="tpu_custom_call" | custom-call | flops 6442450944 | bytes 8388608 | tf_op jit(solution)/shard_map/attend_prefix/pallas_call | solution.py:338
  54.6 0.0 collective-permute-start.11
  54.6 1.9 %collective-permute-done.11 = bf16[128,2048]{1,0:T(8,128)(2,1)S(1)} collective-permute-done((bf16[128,2048]{1,0:T(8,128)(2,1)S(1)}, bf16[128,2048]{1,0:T(8,128)(2,1)S(1)}, u32[]{:S(2)}, u32[]{:S(2)}) %collective-permute-start.11) | collective-permute-done | bytes 524320 | tf_op jit(solution)/shard_map/ppermute | solution.py:374
  56.5 0.8 %constant_dynamic-update-slice_fusion = bf16[128,4096]{1,0:T(8,128)(2,1)} fusion(bf16[128,4096]{1,0:T(8,128)(2,1)} %get-tuple-element.21, bf16[128,2048]{1,0:T(8,128)(2,1)S(1)} %collective-permute-done.11, s32[]{:T(128)S(6)} %select_n.3), kind=kLoop, calls=%fused_computation | loop fusion | bytes 1048580 | tf_op jit(solution)/shard_map/dynamic_update_slice | solution.py:394
  (9 shorter events, 0.0 us)
Async XLA Ops:
  1.2 28.5 %collective-permute-start.9 = (bf16[128,3712]{1,0:T(8,128)(2,1)S(1)}, bf16[128,3712]{1,0:T(8,128)(2,1)S(1)}, u32[]{:S(2)}, u32[]{:S(2)}) collective-permute-start(bf16[128,3712]{1,0:T(8,128)(2,1)S(1)} %prepare.1), channel_id=1, source_target_pairs={{0,1},{1,0},{2,3},{3,2},{4,5},{5,4},{6,7},{7,6},{8,9},{9,8},{10,11... | collective-permute-start | bytes 2850824 | tf_op jit(solution)/shard_map/ppermute | solution.py:374
  1.8 5.2 %collective-permute-start = (s32[1,6]{1,0:T(1,128)}, s32[1,6]{1,0:T(1,128)S(1)}, u32[]{:S(2)}, u32[]{:S(2)}) collective-permute-start(s32[1,6]{1,0:T(1,128)} %refs_0_.1), channel_id=1, source_target_pairs={{0,4},{4,0},{8,12},{12,8},{1,5},{5,1},{9,13},{13,9},{2,6},{6,2},{1... | collective-permute-start | bytes 80 | tf_op jit(solution)/shard_map/ppermute | solution.py:375
  4.4 4.6 %collective-permute-start.1 = (s32[1,6]{1,0:T(1,128)}, s32[1,6]{1,0:T(1,128)S(1)}, u32[]{:S(2)}, u32[]{:S(2)}) collective-permute-start(s32[1,6]{1,0:T(1,128)} %refs_0_.1), channel_id=1, source_target_pairs={{0,8},{4,12},{8,0},{12,4},{1,9},{5,13},{9,1},{13,5},{2,10},{6,14},... | collective-permute-start | bytes 80 | tf_op jit(solution)/shard_map/ppermute | solution.py:375
  7.0 5.5 %collective-permute-start.2 = (s32[1,6]{1,0:T(1,128)}, s32[1,6]{1,0:T(1,128)S(1)}, u32[]{:S(2)}, u32[]{:S(2)}) collective-permute-start(s32[1,6]{1,0:T(1,128)} %refs_0_.1), channel_id=1, source_target_pairs={{0,12},{4,8},{8,4},{12,0},{1,13},{5,9},{9,5},{13,1},{2,14},{6,10},... | collective-permute-start | bytes 80 | tf_op jit(solution)/shard_map/ppermute | solution.py:375
  12.5 0.7 %copy-start = (s32[1,6]{1,0:T(1,128)S(1)}, s32[1,6]{1,0:T(1,128)}, u32[]{:S(2)}) copy-start(s32[1,6]{1,0:T(1,128)} %refs_0_.1) | copy-start | bytes 76
  13.2 0.7 %copy-start.1 = (s32[64]{0:T(128)S(1)}, s32[64]{0:T(128)}, u32[]{:S(2)}) copy-start(s32[64]{0:T(128)} %refs_4_.1) | copy-start | bytes 772
  16.4 8.6 %collective-permute-start.3 = (bf16[288,256]{1,0:T(8,128)(2,1)S(1)}, bf16[288,256]{1,0:T(8,128)(2,1)S(1)}, u32[]{:S(2)}, u32[]{:S(2)}) collective-permute-start(bf16[288,256]{1,0:T(8,128)(2,1)S(1)} %get-tuple-element.15), channel_id=1, source_target_pairs={{0,12},{4,8},{8,4},{12,0},{1,13},{5,9},{9,5},{13,1},{2,14},{6,10},... | collective-permute-start | bytes 442376 | tf_op jit(solution)/shard_map/ppermute | solution.py:375
  16.5 12.7 %collective-permute-start.4 = (bf16[288,256]{1,0:T(8,128)(2,1)S(1)}, bf16[288,256]{1,0:T(8,128)(2,1)S(1)}, u32[]{:S(2)}, u32[]{:S(2)}) collective-permute-start(bf16[288,256]{1,0:T(8,128)(2,1)S(1)} %get-tuple-element.16), channel_id=1, source_target_pairs={{0,8},{4,12},{8,0},{12,4},{1,9},{5,13},{9,1},{13,5},{2,10},{6,14},... | collective-permute-start | bytes 442376 | tf_op jit(solution)/shard_map/ppermute | solution.py:375
  16.6 12.6 %collective-permute-start.5 = (bf16[288,256]{1,0:T(8,128)(2,1)S(1)}, bf16[288,256]{1,0:T(8,128)(2,1)S(1)}, u32[]{:S(2)}, u32[]{:S(2)}) collective-permute-start(bf16[288,256]{1,0:T(8,128)(2,1)S(1)} %get-tuple-element.17), channel_id=1, source_target_pairs={{0,4},{4,0},{8,12},{12,8},{1,5},{5,1},{9,13},{13,9},{2,6},{6,2},{1... | collective-permute-start | bytes 442376 | tf_op jit(solution)/shard_map/ppermute | solution.py:375
  20.9 8.8 %collective-permute-start.10 = (bf16[288,256]{1,0:T(8,128)(2,1)S(1)}, bf16[288,256]{1,0:T(8,128)(2,1)S(1)}, u32[]{:S(2)}, u32[]{:S(2)}) collective-permute-start(bf16[288,256]{1,0:T(8,128)(2,1)S(1)} %get-tuple-element.18.refs_0_), channel_id=1, source_target_pairs={{0,1},{1,0},{2,3},{3,2},{4,5},{5,4},{6,7},{7,6},{8,9},{9,8},{10,11... | collective-permute-start | bytes 442376 | tf_op jit(solution)/shard_map/ppermute | solution.py:374
  25.0 15.8 %collective-permute-start.6 = (bf16[288,256]{1,0:T(8,128)(2,1)S(1)}, bf16[288,256]{1,0:T(8,128)(2,1)S(1)}, u32[]{:S(2)}, u32[]{:S(2)}) collective-permute-start(bf16[288,256]{1,0:T(8,128)(2,1)S(1)} %collective-permute-done.3.refs_0_), channel_id=1, source_target_pairs={{0,1},{1,0},{2,3},{3,2},{4,5},{5,4},{6,7},{7,6},{8,9},{9,8},{10,11... | collective-permute-start | bytes 442376 | tf_op jit(solution)/shard_map/ppermute | solution.py:374
  29.2 11.6 %collective-permute-start.7 = (bf16[288,256]{1,0:T(8,128)(2,1)S(1)}, bf16[288,256]{1,0:T(8,128)(2,1)S(1)}, u32[]{:S(2)}, u32[]{:S(2)}) collective-permute-start(bf16[288,256]{1,0:T(8,128)(2,1)S(1)} %collective-permute-done.4.refs_1_), channel_id=1, source_target_pairs={{0,1},{1,0},{2,3},{3,2},{4,5},{5,4},{6,7},{7,6},{8,9},{9,8},{10,11... | collective-permute-start | bytes 442376 | tf_op jit(solution)/shard_map/ppermute | solution.py:374
  29.2 11.6 %collective-permute-start.8 = (bf16[288,256]{1,0:T(8,128)(2,1)S(1)}, bf16[288,256]{1,0:T(8,128)(2,1)S(1)}, u32[]{:S(2)}, u32[]{:S(2)}) collective-permute-start(bf16[288,256]{1,0:T(8,128)(2,1)S(1)} %collective-permute-done.5.refs_2_), channel_id=1, source_target_pairs={{0,1},{1,0},{2,3},{3,2},{4,5},{5,4},{6,7},{7,6},{8,9},{9,8},{10,11... | collective-permute-start | bytes 442376 | tf_op jit(solution)/shard_map/ppermute | solution.py:374
  54.6 1.9 %collective-permute-start.11 = (bf16[128,2048]{1,0:T(8,128)(2,1)S(1)}, bf16[128,2048]{1,0:T(8,128)(2,1)S(1)}, u32[]{:S(2)}, u32[]{:S(2)}) collective-permute-start(bf16[128,2048]{1,0:T(8,128)(2,1)S(1)} %get-tuple-element.22), channel_id=1, source_target_pairs={{0,1},{1,0},{2,3},{3,2},{4,5},{5,4},{6,7},{7,6},{8,9},{9,8},{10,11... | collective-permute-start | bytes 1572872 | tf_op jit(solution)/shard_map/ppermute | solution.py:374

commit v4 on v2

v4 whole, which is shorter than its diff:
```python
import functools
import math

import jax
import jax.numpy as jnp
from jax import lax
from jax.experimental import pallas as pl
from jax.experimental.pallas import tpu as pltpu
from jax.sharding import PartitionSpec as P


NOPE = 128
ROPE = 64
VDIM = 128
CAP = 2
LANES = 128
HIDE = -1e30


def pack_kernel(n, blocks, pool_local, lists, slots_ref, len_ref, pool_ref, rope_ref, outs, where_ref,
                index_ref, count_ref, lat_sem, rope_sem):
    me = lax.axis_index("req")
    sub = lax.axis_index("sub")
    block = pool_ref.shape[1]
    width = pool_ref.shape[2]
    for i in range(n * CAP):
        index_ref[i] = 0
        where_ref[i] = -1
    where_ref[n * CAP] = len_ref[0]
    for i in range(n):
        count_ref[i] = 0
    for k in range(n):
        found = jnp.int32(0)
        for p in range(blocks):
            physical = slots_ref[lists[k][0, p]]
            owner = physical // pool_local
            mine = owner == me

            @pl.when(mine)
            def _():
                index_ref[k * CAP + found] = physical - owner * pool_local

            found = found + mine.astype(jnp.int32)
            if k == 0:
                step = jnp.bitwise_xor(me, owner)
                earlier = count_ref[step]
                where_ref[step * CAP + earlier] = p
                count_ref[step] = earlier + 1
    parts = width // block
    rows = ROPE // parts
    copies = []
    for k in range(n):
        for c in range(CAP):
            copies.append(pltpu.make_async_copy(
                pool_ref.at[index_ref[k * CAP + c]],
                outs[k].at[pl.ds(c * block, block)],
                lat_sem.at[k * CAP + c],
            ))
        for i in range(parts):
            copies.append(pltpu.make_async_copy(
                rope_ref.at[index_ref[k * CAP + sub], pl.ds(i * rows, rows)],
                outs[k].at[pl.ds(CAP * block, rows), pl.ds(i * block, block)],
                rope_sem.at[k * parts + i],
            ))
    for copy in copies:
        copy.start()
    for copy in copies:
        copy.wait()


def pack(n, lists, block_slot, prefix_len, pool_latent, rope_turned):
    pool_local, block, width = pool_latent.shape
    blocks = lists[0].shape[1]
    rows = CAP * block + block * ROPE // width
    vmem = pl.BlockSpec(memory_space=pltpu.VMEM)
    smem = pl.BlockSpec(memory_space=pltpu.SMEM)

    def body(*refs):
        pack_kernel(
            n, blocks, pool_local, refs[:n], *refs[n : n + 4],
            refs[n + 4 : 2 * n + 4], *refs[2 * n + 4 :],
        )

    out = pl.pallas_call(
        body,
        out_shape=[jax.ShapeDtypeStruct((rows, width), jnp.bfloat16)] * n
        + [jax.ShapeDtypeStruct((n * CAP + 1,), jnp.int32)],
        in_specs=[smem] * (n + 2) + [pl.BlockSpec(memory_space=pl.ANY)] * 2,
        out_specs=[vmem] * n + [smem],
        scratch_shapes=[
            pltpu.SMEM((n * CAP,), jnp.int32),
            pltpu.SMEM((n,), jnp.int32),
            pltpu.SemaphoreType.DMA((n * CAP,)),
            pltpu.SemaphoreType.DMA((n * width // block,)),
        ],
        compiler_params=pltpu.CompilerParams(vmem_limit_bytes=16 << 20),
        cost_estimate=pl.CostEstimate(flops=0, bytes_accessed=4 * n * rows * width, transcendentals=0),
        name="pack",
    )(*lists, block_slot, prefix_len, pool_latent, rope_turned)
    return out[:n], out[n]


def prepare_kernel(lat_ref, qn_ref, qr_ref, rope_ref, out_ref, sem):
    there = 1 - lax.axis_index("sub")
    latent = lat_ref.shape[1]
    half = qn_ref.shape[1] // 2
    rope_half = qr_ref.shape[1] // 2
    tail = latent + half + rope_half
    copies = [
        pltpu.make_async_copy(lat_ref, out_ref.at[:, pl.ds(0, latent)], sem.at[0]),
        pltpu.make_async_copy(
            qn_ref.at[:, pl.ds(pl.multiple_of(there * half, LANES), half)],
            out_ref.at[:, pl.ds(latent, half)],
            sem.at[1],
        ),
        pltpu.make_async_copy(
            qr_ref.at[:, pl.ds(pl.multiple_of(there * rope_half, LANES), rope_half)],
            out_ref.at[:, pl.ds(latent + half, rope_half)],
            sem.at[2],
        ),
        pltpu.make_async_copy(
            rope_ref, out_ref.at[pl.ds(0, ROPE), pl.ds(tail, rope_ref.shape[1])], sem.at[3]
        ),
    ]
    for copy in copies:
        copy.start()
    for copy in copies:
        copy.wait()


def prepare(new_latent, q_nope, q_rope, rope_turned):
    rows, latent = new_latent.shape
    width = latent + q_nope.shape[1] // 2 + q_rope.shape[1] // 2 + rows
    return pl.pallas_call(
        prepare_kernel,
        out_shape=jax.ShapeDtypeStruct((rows, width), jnp.bfloat16),
        in_specs=[pl.BlockSpec(memory_space=pl.ANY)] * 4,
        out_specs=pl.BlockSpec(memory_space=pltpu.VMEM),
        scratch_shapes=[pltpu.SemaphoreType.DMA((4,))],
        compiler_params=pltpu.CompilerParams(vmem_limit_bytes=16 << 20),
        cost_estimate=pl.CostEstimate(flops=0, bytes_accessed=4 * rows * width, transcendentals=0),
        name="prepare",
    )(new_latent, q_nope, q_rope, rope_turned)


RATE = math.log2(math.e) / math.sqrt(NOPE + ROPE)


def attend_kernel(steps, fresh, halves, sub_ref, where_ref, *refs):
    count = len(steps)
    mine = refs[:count]
    theirs = refs[count : 2 * count]
    refs = refs[2 * count :]
    if fresh:
        lat_a, rope_a, lat_b, rope_b, *refs = refs
    lead, odd, even = refs[:6], refs[6:12], refs[12:18]
    if fresh:
        acc_ref, stat_ref, lat, kc, vt, score, weight, peak, bias = refs[18:]
    else:
        acc_ref, stat_ref, out_ref, send_ref, lat, kc, vt, score, weight, peak = refs[18:]
    sub = sub_ref[0]
    block = lead[0].shape[0]
    chunk = CAP * block
    first = chunk if fresh else 0
    queries = 2 * block
    keys = lat.shape[0]
    t = pl.program_id(0)
    head = lambda j: slice(j * LANES, (j + 1) * LANES)

    def build():
        def put_tails(base, rope, mask):
            kc[0, base : base + block, NOPE:] = jnp.concatenate([rope, mask], axis=1)
            kc[1, base : base + block, NOPE:] = jnp.concatenate([mask, rope], axis=1)

        lane = lax.broadcasted_iota(jnp.int32, (block, ROPE), 1)
        row = lax.broadcasted_iota(jnp.int32, (block, ROPE), 0)
        length = where_ref[where_ref.shape[0] - 1]
        vt[:, :, VDIM:, :] = jnp.ones((2, 2, 16, keys), jnp.bfloat16)
        for i, k in enumerate(steps):
            width = mine[i].shape[1]
            here = pl.multiple_of(sub * width, width)
            there = pl.multiple_of((1 - sub) * width, width)
            base = first + i * chunk
            lat[base : base + chunk, pl.ds(here, width)] = mine[i][:chunk, :]
            lat[base : base + chunk, pl.ds(there, width)] = theirs[i][:chunk, :]
            for c in range(CAP):
                packed = jnp.where(sub == c, mine[i][chunk:, :], theirs[i][chunk:, :])
                rope = jnp.concatenate(
                    [packed[:, j * block : (j + 1) * block] for j in range(width // block)], axis=0
                )
                p = where_ref[k * CAP + c]
                hidden = (lane == 0) & ((p < 0) | (p * block + row >= length))
                put_tails(
                    base + c * block, rope.T, jnp.where(hidden, HIDE, 0.0).astype(jnp.bfloat16)
                )
        if fresh:
            plain = jnp.zeros((block, ROPE), jnp.bfloat16)
            lat[:block, :] = lat_a[...]
            lat[block:chunk, :] = lat_b[...]
            put_tails(0, rope_a[...].T, plain)
            put_tails(block, rope_b[:ROPE, :].T, plain)
            i = lax.broadcasted_iota(jnp.int32, (queries, queries), 0)
            j = lax.broadcasted_iota(jnp.int32, (queries, queries), 1)
            flip = sub * block
            seen = jnp.bitwise_xor(i, flip) <= jnp.bitwise_xor(j, flip)
            bias[...] = jnp.where(seen, 0.0, HIDE)

    def form_keys(role):
        k2 = jnp.dot(lat[...], role[4][...], preferred_element_type=jnp.float32)
        for j in range(2):
            kc[j, :, :NOPE] = k2[:, head(j)].astype(jnp.bfloat16)

    def form_values(role, slot):
        v2 = lax.dot_general(
            role[5][...], lat[...], (((0,), (1,)), ((), ())), preferred_element_type=jnp.float32
        )
        for j in range(2):
            vt[slot, j, :VDIM, :] = v2[j * VDIM : (j + 1) * VDIM].astype(jnp.bfloat16)

    def form_scores(role, slot, j):
        qn_a, qr_a, qn_b, qr_b = role[:4]
        lane = lax.broadcasted_iota(jnp.int32, (queries, LANES), 1)
        qn = jnp.concatenate([qn_a[:, head(j)], qn_b[:, head(j)]], axis=0)
        qr = jnp.concatenate([qr_a[...], qr_b[...]], axis=0)
        fill = jnp.where(lane == (1 - j) * ROPE, 1.0, 0.0).astype(jnp.bfloat16)
        own = (lane >= ROPE) if j else (lane < ROPE)
        qc = jnp.concatenate([qn, jnp.where(own, qr, fill)], axis=1)
        s = lax.dot_general(
            kc[j], qc, (((1,), (1,)), ((), ())), preferred_element_type=jnp.float32
        )
        if fresh:
            s = jnp.concatenate([s[:queries] + bias[...], s[queries:]], axis=0)
        score[slot, j] = s
        most = jnp.max(s, axis=0, keepdims=True)
        peak[slot, j] = jnp.broadcast_to(most, (8, queries))

    def before(slot, j):
        rows = slice((slot * 2 + j) * 8, (slot * 2 + j) * 8 + 1)
        return stat_ref[rows, :]

    def form_weights(slot, j):
        most = peak[slot, j, :1, :]
        if not fresh:
            most = jnp.maximum(most, before(slot, j))
        weight[slot, j] = jnp.exp2((score[slot, j] - most) * RATE).astype(jnp.bfloat16)

    def form_output(slot, j):
        o = jnp.dot(vt[slot, j], weight[slot, j], preferred_element_type=jnp.float32)
        o, norm = o[:VDIM], o[VDIM : VDIM + 1]
        index = slot * 2 + j
        if fresh:
            acc_ref[index * VDIM : (index + 1) * VDIM, :] = o
            row = lax.broadcasted_iota(jnp.int32, (8, queries), 0)
            stat_ref[index * 8 : (index + 1) * 8, :] = jnp.where(row == 0, peak[slot, j], norm)
        else:
            old = before(slot, j)
            most = jnp.maximum(peak[slot, j, :1, :], old)
            keep = jnp.exp2((old - most) * RATE)
            norm = norm + keep * stat_ref[index * 8 + 1 : index * 8 + 2, :]
            o = (o + keep * acc_ref[index * VDIM : (index + 1) * VDIM, :]) / norm
            o = o.T.astype(jnp.bfloat16)
            out_ref[:, head(index)] = o[:block]
            send_ref[:, head(index)] = o[block:]

    def both(slot, role):
        form_weights(slot, 0)
        form_weights(slot, 1)
        if role is not None:
            form_keys(role)
            form_values(role, 1 - slot)
        for j in range(2):
            form_output(slot, j)
            if role is not None:
                form_scores(role, 1 - slot, j)

    @pl.when(t == 0)
    def _():
        build()
        form_keys(lead)
        form_values(lead, 0)
        for j in range(2):
            form_scores(lead, 0, j)

    @pl.when(t < halves - 1)
    def _():
        both(0, odd)
        both(1, even)

    @pl.when(t == halves - 1)
    def _():
        both(0, odd)
        both(1, None)


def attend(steps, sub, where, mine, theirs, new_latent, rope_turned, q_nope, q_rope,
           other, w_uk, w_uv, state):
    fresh = state is None
    block, latent = new_latent.shape
    heads = w_uk.shape[1] // NOPE // 2
    pairs = heads // 2
    halves = pairs // 2
    keys = (len(steps) + (1 if fresh else 0)) * CAP * block
    whole = lambda a: pl.BlockSpec(a.shape, lambda t, *_: (0,) * a.ndim)
    nope_at = latent
    rope_at = nope_at + heads * NOPE
    tail_at = rope_at + heads * ROPE

    def at(width, first):
        return pl.BlockSpec((block, width), lambda t, *_: (0, first // width))

    def follow(width, first, pair):
        return pl.BlockSpec((block, width), lambda t, *_: (0, first // width + pair(t)))

    def ours(rows, width, pair):
        return pl.BlockSpec((rows, width), lambda t, s, *_: (0, s[0] * pairs + pair(t)))

    specs = [whole(a) for a in mine] + [whole(a) for a in theirs]
    args = [*mine, *theirs]
    if fresh:
        specs += [whole(new_latent), whole(rope_turned), at(latent, 0), at(LANES, tail_at)]
        args += [new_latent, rope_turned, other, other]
    for pair in (
        lambda t: 0 * t,
        lambda t: 2 * t + 1,
        lambda t: jnp.minimum(2 * t + 2, pairs - 1),
    ):
        specs += [
            ours(block, 2 * NOPE, pair),
            ours(block, 2 * ROPE, pair),
            follow(2 * NOPE, nope_at, pair),
            follow(2 * ROPE, rope_at, pair),
            ours(latent, 2 * NOPE, pair),
            ours(latent, 2 * VDIM, pair),
        ]
        args += [q_nope, q_rope, other, other, w_uk, w_uv]
    tall = lambda rows: pl.BlockSpec((rows, 2 * block), lambda t, *_: (t, 0))
    state_specs = [tall(4 * VDIM), tall(32)]
    scratch = [
        pltpu.VMEM((keys, latent), jnp.bfloat16),
        pltpu.VMEM((2, keys, NOPE + LANES), jnp.bfloat16),
        pltpu.VMEM((2, 2, VDIM + 16, keys), jnp.bfloat16),
        pltpu.VMEM((2, 2, keys, 2 * block), jnp.float32),
        pltpu.VMEM((2, 2, keys, 2 * block), jnp.bfloat16),
        pltpu.VMEM((2, 2, 8, 2 * block), jnp.float32),
    ]
    if fresh:
        out_specs = state_specs
        out_shape = [
            jax.ShapeDtypeStruct((heads * VDIM, 2 * block), jnp.float32),
            jax.ShapeDtypeStruct((heads * 8, 2 * block), jnp.float32),
        ]
        scratch.append(pltpu.VMEM((2 * block, 2 * block), jnp.float32))
    else:
        specs += state_specs
        args += state
        out_specs = [
            pl.BlockSpec((block, 4 * VDIM), lambda t, s, *_: (0, s[0] * halves + t)),
            pl.BlockSpec((block, 4 * VDIM), lambda t, *_: (0, t)),
        ]
        out_shape = [
            jax.ShapeDtypeStruct((block, 2 * heads * VDIM), jnp.bfloat16),
            jax.ShapeDtypeStruct((block, heads * VDIM), jnp.bfloat16),
        ]
    return pl.pallas_call(
        functools.partial(attend_kernel, steps, fresh, halves),
        grid_spec=pltpu.PrefetchScalarGridSpec(
            num_scalar_prefetch=2,
            grid=(halves,),
            in_specs=specs,
            out_specs=out_specs,
            scratch_shapes=scratch,
        ),
        out_shape=out_shape,
        compiler_params=pltpu.CompilerParams(vmem_limit_bytes=(40 if len(steps) < 8 else 60) << 20),
        cost_estimate=pl.CostEstimate(
            flops=4 * keys * latent * heads * NOPE + 8 * block * keys * heads * 256,
            bytes_accessed=8 * 1024 * 1024,
            transcendentals=2 * block * keys * heads,
        ),
        name="attend_new" if fresh else "attend_prefix",
    )(sub, where, *args)


def shards(
    q_nope,
    q_rope,
    new_latent,
    new_rope,
    pool_latent,
    pool_rope,
    w_uk,
    w_uv,
    block_list,
    prefix_len,
    block_slot,
):
    n = lax.axis_size("req")
    sub = lax.axis_index("sub")
    half = q_nope.shape[1] // 2
    swap = lambda a: lax.ppermute(a, "sub", [(0, 1), (1, 0)])
    cross = lambda a, k: lax.ppermute(a, "req", [(i, i ^ k) for i in range(n)])
    far = list(range(n - 1, 0, -1))
    keep = lambda a: pltpu.with_memory_space_constraint(a, pltpu.HBM)
    q_nope, q_rope, new_latent, w_uk, w_uv = map(keep, (q_nope, q_rope, new_latent, w_uk, w_uv))
    pool_latent = keep(pool_latent)
    slots = keep(block_slot)
    pool_turned = keep(pool_rope.swapaxes(1, 2))
    rope_turned = keep(new_rope.T)
    got = {k: cross(block_list, k) for k in far}
    lists = [keep(block_list)] + [got[k] for k in range(1, n)]
    other = prepare(new_latent, q_nope, q_rope, rope_turned)
    other = swap(other)
    sent, where = pack(n, lists, slots, prefix_len, pool_latent, pool_turned)
    local = swap(sent[0])
    mine = [cross(sent[k], k) for k in far]
    theirs = [swap(a) for a in mine]
    common = (new_latent, rope_turned, q_nope, q_rope, other, w_uk, w_uv)
    state = attend([0], sub.reshape(1), where, [sent[0]], [local], *common, None)
    kept, gone = attend(far, sub.reshape(1), where, mine, theirs, *common, state)
    back = swap(gone)
    return lax.dynamic_update_slice_in_dim(kept, back, (1 - sub) * half, 1)


def solution(mesh):
    placed = (
        P(("groups", "req", "sub"), "head"),
        P(("groups", "req", "sub"), "head"),
        P(("groups", "req", "sub"), None),
        P(("groups", "req", "sub"), None),
        P(("groups", "req"), None, "sub"),
        P(("groups", "req"), None, None),
        P(None, "head"),
        P(None, "head"),
        P(("groups", "req"), None),
        P(("groups", "req")),
        P("groups"),
    )
    return jax.shard_map(
        shards,
        mesh=mesh,
        in_specs=placed,
        out_specs=P(("groups", "req", "sub"), "head"),
        check_vma=False,
    )
```

time: 62.9 us -> 52.2 us (0.83)
  Pallas kernels: 33.9 us -> 24.6 us
  local copies, waits for them, and re-layouts: 2.14 us -> 0.83 us
    pallas_call x2, Pallas kernels: 30.1 us -> 20.7 us  [attend(): pl.pallas_call(functools.partial(attend_kernel, steps, fresh, halves), gr...]
    unnamed x4 -> x0, local copies, waits for them, and re-layouts: 1.31 us -> none
  transfers between devices with their start and end apart: 12 -> 12, of which waited for: 5 -> 5; matrix products, arithmetic and copies ran while one was open for 0% -> 0% of each run, Pallas kernels for 24% -> 22%
where the time goes in v4:
time: 52.2 us; the launch traced here: 52 us
  Pallas kernels  24.6 us (47%)
  waiting for transfers between devices  15 us (29%)
  starting transfers between devices  10.8 us (21%)
  local copies, waits for them, and re-layouts  0.83 us (2%)
  between operations  0.72 us (1%)
    pallas_call x2, Pallas kernels, attend(): pl.pallas_call(functools.partial(attend_kernel, steps, fresh, halves), gr...  20.7 us
    ppermute x6, waiting for transfers between devices, shards(): cross = lambda a, k: lax.ppermute(a, 'req', [(i, i ^ k) for i in range(n)])  13.2 us
    ppermute x6, starting transfers between devices, shards(): cross = lambda a, k: lax.ppermute(a, 'req', [(i, i ^ k) for i in range(n)])  9.68 us
    pallas_call x1, Pallas kernels, pack(): pl.pallas_call(body, out_shape=[jax.ShapeDtypeStruct((rows, width), jnp.b...  2.72 us
    ppermute x6, waiting for transfers between devices, shards(): swap = lambda a: lax.ppermute(a, 'sub', [(0, 1), (1, 0)])  1.88 us
    pallas_call x1, Pallas kernels, prepare(): pl.pallas_call(prepare_kernel, out_shape=jax.ShapeDtypeStruct((rows, widt...  1.21 us
    ppermute x6, starting transfers between devices, shards(): swap = lambda a: lax.ppermute(a, 'sub', [(0, 1), (1, 0)])  1.11 us
  transfers between devices with their start and end apart: 12, of which 5 were waited for; matrix products, arithmetic and copies ran while one was open for 0% of the time, Pallas kernels for 22%

profile of v4, /device:TPU:0, one launch (start us, length us, event | category | flops | bytes accessed | tf_op | source)
XLA Modules:
  0.0 52.0 jit_solution(1924964314728625858)
XLA Ops:
  0.0 1.2 %prepare.1 = bf16[128,3712]{1,0:T(8,128)(2,1)S(1)} custom-call(bf16[128,512]{1,0:T(8,128)(2,1)} %refs_2_.1, bf16[128,4096]{1,0:T(8,128)(2,1)} %refs_18_.3, bf16[128,2048]{1,0:T(8,128)(2,1)} %refs_19_.3, bf16[64,128]{1,0:T(8,128)(2,1)} %bitcast.4), custom_call_target="tpu_custom_call" | custom-call | bytes 1900544 | tf_op jit(solution)/shard_map/prepare/pallas_call | solution.py:134
  1.2 0.6 %collective-permute-start.9 = (bf16[128,3712]{1,0:T(8,128)(2,1)S(1)}, bf16[128,3712]{1,0:T(8,128)(2,1)S(1)}, u32[]{:S(2)}, u32[]{:S(2)}) collective-permute-start(bf16[128,3712]{1,0:T(8,128)(2,1)S(1)} %prepare.1), channel_id=1, source_target_pairs={{0,1},{1,0},{2,3},{3,2},{4,5},{5,4},{6,7},{7,6},{8,9},{9,8},{10,11... | collective-permute-start | bytes 2850824 | tf_op jit(solution)/shard_map/ppermute | solution.py:400
  1.8 2.6 %collective-permute-start = (s32[1,6]{1,0:T(1,128)}, s32[1,6]{1,0:T(1,128)S(1)}, u32[]{:S(2)}, u32[]{:S(2)}) collective-permute-start(s32[1,6]{1,0:T(1,128)} %refs_0_.1), channel_id=1, source_target_pairs={{0,4},{4,0},{8,12},{12,8},{1,5},{5,1},{9,13},{13,9},{2,6},{6,2},{1... | collective-permute-start | bytes 80 | tf_op jit(solution)/shard_map/ppermute | solution.py:401
  4.4 2.6 %collective-permute-start.1 = (s32[1,6]{1,0:T(1,128)}, s32[1,6]{1,0:T(1,128)S(1)}, u32[]{:S(2)}, u32[]{:S(2)}) collective-permute-start(s32[1,6]{1,0:T(1,128)} %refs_0_.1), channel_id=1, source_target_pairs={{0,8},{4,12},{8,0},{12,4},{1,9},{5,13},{9,1},{13,5},{2,10},{6,14},... | collective-permute-start | bytes 80 | tf_op jit(solution)/shard_map/ppermute | solution.py:401
  7.7 1.3 %collective-permute-done.1.refs_2_ = s32[1,6]{1,0:T(1,128)S(1)} collective-permute-done((s32[1,6]{1,0:T(1,128)}, s32[1,6]{1,0:T(1,128)S(1)}, u32[]{:S(2)}, u32[]{:S(2)}) %collective-permute-start.1) | collective-permute-done | bytes 56 | tf_op jit(solution)/shard_map/ppermute | solution.py:401
  9.0 3.5 %collective-permute-done.2.refs_3_ = s32[1,6]{1,0:T(1,128)S(1)} collective-permute-done((s32[1,6]{1,0:T(1,128)}, s32[1,6]{1,0:T(1,128)S(1)}, u32[]{:S(2)}, u32[]{:S(2)}) %collective-permute-start.2) | collective-permute-done | bytes 56 | tf_op jit(solution)/shard_map/ppermute | solution.py:401
  12.5 2.7 %pack.1 = (bf16[288,256]{1,0:T(8,128)(2,1)S(1)}, bf16[288,256]{1,0:T(8,128)(2,1)S(1)}, bf16[288,256]{1,0:T(8,128)(2,1)S(1)}, bf16[288,256]{1,0:T(8,128)(2,1)S(1)}, s32[9]{0:T(128)S(1)}) custom-call(s32[1,6]{1,0:T(1,128)} %refs_0_.1, s32[1,6]{1,0:T(1,128)S(1)} %collective-permute-done.refs_1_, s32[1,6]{1,0:T(1,128)S(1)} %collective-permute-done.1.refs_2_, ...), custom_call_target="tpu_custom_call" | custom-call | bytes 1179648 | tf_op jit(solution)/shard_map/pack/pallas_call | solution.py:84
  15.2 0.1 collective-permute-start.3
  15.3 0.1 collective-permute-start.4
  15.4 4.3 %collective-permute-start.5 = (bf16[288,256]{1,0:T(8,128)(2,1)S(1)}, bf16[288,256]{1,0:T(8,128)(2,1)S(1)}, u32[]{:S(2)}, u32[]{:S(2)}) collective-permute-start(bf16[288,256]{1,0:T(8,128)(2,1)S(1)} %get-tuple-element.17), channel_id=1, source_target_pairs={{0,4},{4,0},{8,12},{12,8},{1,5},{5,1},{9,13},{13,9},{2,6},{6,2},{1... | collective-permute-start | bytes 442376 | tf_op jit(solution)/shard_map/ppermute | solution.py:401
  19.7 0.0 collective-permute-start.10
  19.7 4.1 %collective-permute-done.3.refs_0_ = bf16[288,256]{1,0:T(8,128)(2,1)S(1)} collective-permute-done((bf16[288,256]{1,0:T(8,128)(2,1)S(1)}, bf16[288,256]{1,0:T(8,128)(2,1)S(1)}, u32[]{:S(2)}, u32[]{:S(2)}) %collective-permute-start.3) | collective-permute-done | bytes 147488 | tf_op jit(solution)/shard_map/ppermute | solution.py:401
  23.8 0.0 collective-permute-start.6
  23.8 4.2 %collective-permute-done.4.refs_1_ = bf16[288,256]{1,0:T(8,128)(2,1)S(1)} collective-permute-done((bf16[288,256]{1,0:T(8,128)(2,1)S(1)}, bf16[288,256]{1,0:T(8,128)(2,1)S(1)}, u32[]{:S(2)}, u32[]{:S(2)}) %collective-permute-start.4) | collective-permute-done | bytes 147488 | tf_op jit(solution)/shard_map/ppermute | solution.py:401
  28.0 0.0 collective-permute-start.7
  28.0 0.0 collective-permute-done.5.refs_2_
  28.0 0.5 collective-permute-start.8
  28.5 8.9 %attend_new.1 = (f32[2048,256]{1,0:T(8,128)S(1)}, f32[128,256]{1,0:T(8,128)S(1)}) custom-call(s32[1]{0:T(128)} %bitcast.sub_ref, s32[9]{0:T(128)S(1)} %get-tuple-element.14.where_ref, bf16[288,256]{1,0:T(8,128)(2,1)S(1)} %get-tuple-element.18.refs_0_, bf16[288,256]{1,0:T(8,128)(2,1)S(1)} %collective-permute-done.10.refs_1_, bf16[128,512]{1,0:T(8,128)(2,1)} %refs_2_.1, ...), custom_call_target="tpu_custom_call" | custom-call | flops 4294967296 | bytes 8388608 | tf_op jit(solution)/shard_map/attend_new/pallas_call | solution.py:364
  37.5 0.0 collective-permute-done.6.refs_3_
  37.5 0.0 collective-permute-done.7.refs_4_
  37.5 11.7 %attend_prefix.1 = (bf16[128,4096]{1,0:T(8,128)(2,1)}, bf16[128,2048]{1,0:T(8,128)(2,1)S(1)}) custom-call(s32[1]{0:T(128)} %bitcast.sub_ref, s32[9]{0:T(128)S(1)} %get-tuple-element.14.where_ref, bf16[288,256]{1,0:T(8,128)(2,1)S(1)} %collective-permute-done.3.refs_0_, bf16[288,256]{1,0:T(8,128)(2,1)S(1)} %collective-permute-done.4.refs_1_, ...), custom_call_target="tpu_custom_call" | custom-call | flops 6442450944 | bytes 8388608 | tf_op jit(solution)/shard_map/attend_prefix/pallas_call | solution.py:364
  49.3 0.0 collective-permute-start.11
  49.3 1.9 %collective-permute-done.11 = bf16[128,2048]{1,0:T(8,128)(2,1)S(1)} collective-permute-done((bf16[128,2048]{1,0:T(8,128)(2,1)S(1)}, bf16[128,2048]{1,0:T(8,128)(2,1)S(1)}, u32[]{:S(2)}, u32[]{:S(2)}) %collective-permute-start.11) | collective-permute-done | bytes 524320 | tf_op jit(solution)/shard_map/ppermute | solution.py:400
  51.2 0.8 %constant_dynamic-update-slice_fusion = bf16[128,4096]{1,0:T(8,128)(2,1)} fusion(bf16[128,4096]{1,0:T(8,128)(2,1)} %get-tuple-element.21, bf16[128,2048]{1,0:T(8,128)(2,1)S(1)} %collective-permute-done.11, s32[]{:T(128)S(6)} %select_n.3), kind=kLoop, calls=%fused_computation | loop fusion | bytes 1048580 | tf_op jit(solution)/shard_map/dynamic_update_slice | solution.py:421
  (5 shorter events, 0.0 us)
Async XLA Ops:
  1.2 27.3 %collective-permute-start.9 = (bf16[128,3712]{1,0:T(8,128)(2,1)S(1)}, bf16[128,3712]{1,0:T(8,128)(2,1)S(1)}, u32[]{:S(2)}, u32[]{:S(2)}) collective-permute-start(bf16[128,3712]{1,0:T(8,128)(2,1)S(1)} %prepare.1), channel_id=1, source_target_pairs={{0,1},{1,0},{2,3},{3,2},{4,5},{5,4},{6,7},{7,6},{8,9},{9,8},{10,11... | collective-permute-start | bytes 2850824 | tf_op jit(solution)/shard_map/ppermute | solution.py:400
  1.8 5.9 %collective-permute-start = (s32[1,6]{1,0:T(1,128)}, s32[1,6]{1,0:T(1,128)S(1)}, u32[]{:S(2)}, u32[]{:S(2)}) collective-permute-start(s32[1,6]{1,0:T(1,128)} %refs_0_.1), channel_id=1, source_target_pairs={{0,4},{4,0},{8,12},{12,8},{1,5},{5,1},{9,13},{13,9},{2,6},{6,2},{1... | collective-permute-start | bytes 80 | tf_op jit(solution)/shard_map/ppermute | solution.py:401
  4.4 4.6 %collective-permute-start.1 = (s32[1,6]{1,0:T(1,128)}, s32[1,6]{1,0:T(1,128)S(1)}, u32[]{:S(2)}, u32[]{:S(2)}) collective-permute-start(s32[1,6]{1,0:T(1,128)} %refs_0_.1), channel_id=1, source_target_pairs={{0,8},{4,12},{8,0},{12,4},{1,9},{5,13},{9,1},{13,5},{2,10},{6,14},... | collective-permute-start | bytes 80 | tf_op jit(solution)/shard_map/ppermute | solution.py:401
  7.0 5.5 %collective-permute-start.2 = (s32[1,6]{1,0:T(1,128)}, s32[1,6]{1,0:T(1,128)S(1)}, u32[]{:S(2)}, u32[]{:S(2)}) collective-permute-start(s32[1,6]{1,0:T(1,128)} %refs_0_.1), channel_id=1, source_target_pairs={{0,12},{4,8},{8,4},{12,0},{1,13},{5,9},{9,5},{13,1},{2,14},{6,10},... | collective-permute-start | bytes 80 | tf_op jit(solution)/shard_map/ppermute | solution.py:401
  15.2 8.6 %collective-permute-start.3 = (bf16[288,256]{1,0:T(8,128)(2,1)S(1)}, bf16[288,256]{1,0:T(8,128)(2,1)S(1)}, u32[]{:S(2)}, u32[]{:S(2)}) collective-permute-start(bf16[288,256]{1,0:T(8,128)(2,1)S(1)} %get-tuple-element.15), channel_id=1, source_target_pairs={{0,12},{4,8},{8,4},{12,0},{1,13},{5,9},{9,5},{13,1},{2,14},{6,10},... | collective-permute-start | bytes 442376 | tf_op jit(solution)/shard_map/ppermute | solution.py:401
  15.3 12.7 %collective-permute-start.4 = (bf16[288,256]{1,0:T(8,128)(2,1)S(1)}, bf16[288,256]{1,0:T(8,128)(2,1)S(1)}, u32[]{:S(2)}, u32[]{:S(2)}) collective-permute-start(bf16[288,256]{1,0:T(8,128)(2,1)S(1)} %get-tuple-element.16), channel_id=1, source_target_pairs={{0,8},{4,12},{8,0},{12,4},{1,9},{5,13},{9,1},{13,5},{2,10},{6,14},... | collective-permute-start | bytes 442376 | tf_op jit(solution)/shard_map/ppermute | solution.py:401
  15.4 12.6 %collective-permute-start.5 = (bf16[288,256]{1,0:T(8,128)(2,1)S(1)}, bf16[288,256]{1,0:T(8,128)(2,1)S(1)}, u32[]{:S(2)}, u32[]{:S(2)}) collective-permute-start(bf16[288,256]{1,0:T(8,128)(2,1)S(1)} %get-tuple-element.17), channel_id=1, source_target_pairs={{0,4},{4,0},{8,12},{12,8},{1,5},{5,1},{9,13},{13,9},{2,6},{6,2},{1... | collective-permute-start | bytes 442376 | tf_op jit(solution)/shard_map/ppermute | solution.py:401
  19.7 8.8 %collective-permute-start.10 = (bf16[288,256]{1,0:T(8,128)(2,1)S(1)}, bf16[288,256]{1,0:T(8,128)(2,1)S(1)}, u32[]{:S(2)}, u32[]{:S(2)}) collective-permute-start(bf16[288,256]{1,0:T(8,128)(2,1)S(1)} %get-tuple-element.18.refs_0_), channel_id=1, source_target_pairs={{0,1},{1,0},{2,3},{3,2},{4,5},{5,4},{6,7},{7,6},{8,9},{9,8},{10,11... | collective-permute-start | bytes 442376 | tf_op jit(solution)/shard_map/ppermute | solution.py:400
  23.8 13.7 %collective-permute-start.6 = (bf16[288,256]{1,0:T(8,128)(2,1)S(1)}, bf16[288,256]{1,0:T(8,128)(2,1)S(1)}, u32[]{:S(2)}, u32[]{:S(2)}) collective-permute-start(bf16[288,256]{1,0:T(8,128)(2,1)S(1)} %collective-permute-done.3.refs_0_), channel_id=1, source_target_pairs={{0,1},{1,0},{2,3},{3,2},{4,5},{5,4},{6,7},{7,6},{8,9},{9,8},{10,11... | collective-permute-start | bytes 442376 | tf_op jit(solution)/shard_map/ppermute | solution.py:400
  28.0 9.5 %collective-permute-start.7 = (bf16[288,256]{1,0:T(8,128)(2,1)S(1)}, bf16[288,256]{1,0:T(8,128)(2,1)S(1)}, u32[]{:S(2)}, u32[]{:S(2)}) collective-permute-start(bf16[288,256]{1,0:T(8,128)(2,1)S(1)} %collective-permute-done.4.refs_1_), channel_id=1, source_target_pairs={{0,1},{1,0},{2,3},{3,2},{4,5},{5,4},{6,7},{7,6},{8,9},{9,8},{10,11... | collective-permute-start | bytes 442376 | tf_op jit(solution)/shard_map/ppermute | solution.py:400
  28.0 9.5 %collective-permute-start.8 = (bf16[288,256]{1,0:T(8,128)(2,1)S(1)}, bf16[288,256]{1,0:T(8,128)(2,1)S(1)}, u32[]{:S(2)}, u32[]{:S(2)}) collective-permute-start(bf16[288,256]{1,0:T(8,128)(2,1)S(1)} %collective-permute-done.5.refs_2_), channel_id=1, source_target_pairs={{0,1},{1,0},{2,3},{3,2},{4,5},{5,4},{6,7},{7,6},{8,9},{9,8},{10,11... | collective-permute-start | bytes 442376 | tf_op jit(solution)/shard_map/ppermute | solution.py:400
  49.3 1.9 %collective-permute-start.11 = (bf16[128,2048]{1,0:T(8,128)(2,1)S(1)}, bf16[128,2048]{1,0:T(8,128)(2,1)S(1)}, u32[]{:S(2)}, u32[]{:S(2)}) collective-permute-start(bf16[128,2048]{1,0:T(8,128)(2,1)S(1)} %get-tuple-element.22), channel_id=1, source_target_pairs={{0,1},{1,0},{2,3},{3,2},{4,5},{5,4},{6,7},{7,6},{8,9},{9,8},{10,11... | collective-permute-start | bytes 1572872 | tf_op jit(solution)/shard_map/ppermute | solution.py:400

commit v5 on v4

--- a/solution.py
+++ b/solution.py
@@ -29,7 +29,10 @@
     where_ref[n * CAP] = len_ref[0]
     for i in range(n):
         count_ref[i] = 0
-    for k in range(n):
+    parts = width // block
+    rows = ROPE // parts
+    copies = []
+    for k in [*range(1, n), 0]:
         found = jnp.int32(0)
         for p in range(blocks):
             physical = slots_ref[lists[k][0, p]]
@@ -46,24 +49,24 @@
                 earlier = count_ref[step]
                 where_ref[step * CAP + earlier] = p
                 count_ref[step] = earlier + 1
-    parts = width // block
-    rows = ROPE // parts
-    copies = []
-    for k in range(n):
-        for c in range(CAP):
-            copies.append(pltpu.make_async_copy(
+        batch = [
+            pltpu.make_async_copy(
                 pool_ref.at[index_ref[k * CAP + c]],
                 outs[k].at[pl.ds(c * block, block)],
                 lat_sem.at[k * CAP + c],
-            ))
-        for i in range(parts):
-            copies.append(pltpu.make_async_copy(
+            )
+            for c in range(CAP)
+        ] + [
+            pltpu.make_async_copy(
                 rope_ref.at[index_ref[k * CAP + sub], pl.ds(i * rows, rows)],
                 outs[k].at[pl.ds(CAP * block, rows), pl.ds(i * block, block)],
                 rope_sem.at[k * parts + i],
-            ))
-    for copy in copies:
-        copy.start()
+            )
+            for i in range(parts)
+        ]
+        for copy in batch:
+            copy.start()
+        copies += batch
     for copy in copies:
         copy.wait()
 
@@ -100,7 +103,8 @@
     return out[:n], out[n]
 
 
-def prepare_kernel(lat_ref, qn_ref, qr_ref, rope_ref, out_ref, sem):
+def prepare_kernel(len_ref, lat_ref, qn_ref, qr_ref, rope_ref, out_ref, kept_ref, sem):
+    kept_ref[0] = len_ref[0]
     there = 1 - lax.axis_index("sub")
     latent = lat_ref.shape[1]
     half = qn_ref.shape[1] // 2
@@ -128,19 +132,22 @@
         copy.wait()
 
 
-def prepare(new_latent, q_nope, q_rope, rope_turned):
+def prepare(prefix_len, new_latent, q_nope, q_rope, rope_turned):
     rows, latent = new_latent.shape
     width = latent + q_nope.shape[1] // 2 + q_rope.shape[1] // 2 + rows
     return pl.pallas_call(
         prepare_kernel,
-        out_shape=jax.ShapeDtypeStruct((rows, width), jnp.bfloat16),
-        in_specs=[pl.BlockSpec(memory_space=pl.ANY)] * 4,
-        out_specs=pl.BlockSpec(memory_space=pltpu.VMEM),
+        out_shape=[
+            jax.ShapeDtypeStruct((rows, width), jnp.bfloat16),
+            jax.ShapeDtypeStruct((1,), jnp.int32),
+        ],
+        in_specs=[pl.BlockSpec(memory_space=pltpu.SMEM)] + [pl.BlockSpec(memory_space=pl.ANY)] * 4,
+        out_specs=[pl.BlockSpec(memory_space=pltpu.VMEM), pl.BlockSpec(memory_space=pltpu.SMEM)],
         scratch_shapes=[pltpu.SemaphoreType.DMA((4,))],
         compiler_params=pltpu.CompilerParams(vmem_limit_bytes=16 << 20),
         cost_estimate=pl.CostEstimate(flops=0, bytes_accessed=4 * rows * width, transcendentals=0),
         name="prepare",
-    )(new_latent, q_nope, q_rope, rope_turned)
+    )(prefix_len, new_latent, q_nope, q_rope, rope_turned)
 
 
 RATE = math.log2(math.e) / math.sqrt(NOPE + ROPE)
@@ -206,9 +213,11 @@
             bias[...] = jnp.where(seen, 0.0, HIDE)
 
     def form_keys(role):
-        k2 = jnp.dot(lat[...], role[4][...], preferred_element_type=jnp.float32)
-        for j in range(2):
-            kc[j, :, :NOPE] = k2[:, head(j)].astype(jnp.bfloat16)
+        for r in range(0, keys, chunk):
+            rows = slice(r, r + chunk)
+            k2 = jnp.dot(lat[rows, :], role[4][...], preferred_element_type=jnp.float32)
+            for j in range(2):
+                kc[j, rows, :NOPE] = k2[:, head(j)].astype(jnp.bfloat16)
 
     def form_values(role, slot):
         v2 = lax.dot_general(
@@ -314,7 +323,7 @@
     def ours(rows, width, pair):
         return pl.BlockSpec((rows, width), lambda t, s, *_: (0, s[0] * pairs + pair(t)))
 
-    specs = [whole(a) for a in mine] + [whole(a) for a in theirs]
+    specs = [pl.BlockSpec(memory_space=pltpu.VMEM)] * (2 * len(steps))
     args = [*mine, *theirs]
     if fresh:
         specs += [whole(new_latent), whole(rope_turned), at(latent, 0), at(LANES, tail_at)]
@@ -381,6 +390,29 @@
     )(sub, where, *args)
 
 
+def join_kernel(kept_ref, back_ref, out_ref, sem):
+    there = 1 - lax.axis_index("sub")
+    half = back_ref.shape[1]
+    copy = pltpu.make_async_copy(
+        back_ref, out_ref.at[:, pl.ds(pl.multiple_of(there * half, LANES), half)], sem
+    )
+    copy.start()
+    copy.wait()
+
+
+def join(kept, back):
+    return pl.pallas_call(
+        join_kernel,
+        out_shape=jax.ShapeDtypeStruct(kept.shape, kept.dtype),
+        in_specs=[pl.BlockSpec(memory_space=pl.ANY)] * 2,
+        out_specs=pl.BlockSpec(memory_space=pl.ANY),
+        scratch_shapes=[pltpu.SemaphoreType.DMA(())],
+        input_output_aliases={0: 0},
+        compiler_params=pltpu.CompilerParams(vmem_limit_bytes=1 << 20),
+        name="join",
+    )(kept, back)
+
+
 def shards(
     q_nope,
     q_rope,
@@ -396,7 +428,6 @@
 ):
     n = lax.axis_size("req")
     sub = lax.axis_index("sub")
-    half = q_nope.shape[1] // 2
     swap = lambda a: lax.ppermute(a, "sub", [(0, 1), (1, 0)])
     cross = lambda a, k: lax.ppermute(a, "req", [(i, i ^ k) for i in range(n)])
     far = list(range(n - 1, 0, -1))
@@ -406,19 +437,25 @@
     slots = keep(block_slot)
     pool_turned = keep(pool_rope.swapaxes(1, 2))
     rope_turned = keep(new_rope.T)
-    got = {k: cross(block_list, k) for k in far}
+    got = {}
+    for k in far:
+        got[k] = cross(block_list, k)
     lists = [keep(block_list)] + [got[k] for k in range(1, n)]
-    other = prepare(new_latent, q_nope, q_rope, rope_turned)
+    other, length = prepare(prefix_len, new_latent, q_nope, q_rope, rope_turned)
     other = swap(other)
-    sent, where = pack(n, lists, slots, prefix_len, pool_latent, pool_turned)
+    sent, where = pack(n, lists, slots, length, pool_latent, pool_turned)
     local = swap(sent[0])
-    mine = [cross(sent[k], k) for k in far]
-    theirs = [swap(a) for a in mine]
+    mine = []
+    for k in far:
+        mine.append(cross(sent[k], k))
+    theirs = []
+    for k, a in zip(far, mine):
+        theirs.append(swap(a))
     common = (new_latent, rope_turned, q_nope, q_rope, other, w_uk, w_uv)
     state = attend([0], sub.reshape(1), where, [sent[0]], [local], *common, None)
     kept, gone = attend(far, sub.reshape(1), where, mine, theirs, *common, state)
     back = swap(gone)
-    return lax.dynamic_update_slice_in_dim(kept, back, (1 - sub) * half, 1)
+    return join(kept, back)
 
 
 def solution(mesh):

time: 52.2 us -> 53.9 us (1.033)
  Pallas kernels: 24.6 us -> 26.5 us
  local copies, waits for them, and re-layouts: 0.83 us -> 0 us
  waiting for transfers between devices: 15 us -> 15.7 us
    pallas_call x1 -> x2, Pallas kernels: 1.21 us -> 2.54 us  [the longest x1 1.74 us: prepare(): pl.pallas_call(prepare_kernel, out_shape=[jax.ShapeDtypeStruct((rows, wid...]
    dynamic_update_slice x1 -> x0, local copies, waits for them, and re-layouts: 0.83 us -> none  [shards(): return lax.dynamic_update_slice_in_dim(kept, back, (1 - sub) * half, 1)]
    ppermute x6, waiting for transfers between devices: 13.2 us -> 13.8 us  [shards(): cross = lambda a, k: lax.ppermute(a, 'req', [(i, i ^ k) for i in range(n)])]
    pallas_call x1, Pallas kernels: 2.72 us -> 3.32 us  [pack(): pl.pallas_call(body, out_shape=[jax.ShapeDtypeStruct((rows, width), jnp.b...]
  transfers between devices with their start and end apart: 12 -> 12, of which waited for: 5 -> 6; matrix products, arithmetic and copies ran while one was open for 0% -> 0% of each run, Pallas kernels for 22% -> 23%
where the time goes in v5:
time: 53.9 us; the launch traced here: 53.7 us
  Pallas kernels  26.5 us (49%)
  waiting for transfers between devices  15.7 us (29%)
  starting transfers between devices  10.8 us (20%)
  between operations  0.71 us (1%)
    pallas_call x2, Pallas kernels, attend(): pl.pallas_call(functools.partial(attend_kernel, steps, fresh, halves), gr...  20.6 us
    ppermute x6, waiting for transfers between devices, shards(): cross = lambda a, k: lax.ppermute(a, 'req', [(i, i ^ k) for i in range(n)])  13.8 us
    ppermute x6, starting transfers between devices, shards(): cross = lambda a, k: lax.ppermute(a, 'req', [(i, i ^ k) for i in range(n)])  9.68 us
    pallas_call x1, Pallas kernels, pack(): pl.pallas_call(body, out_shape=[jax.ShapeDtypeStruct((rows, width), jnp.b...  3.32 us
    ppermute x6, waiting for transfers between devices, shards(): swap = lambda a: lax.ppermute(a, 'sub', [(0, 1), (1, 0)])  1.88 us
    pallas_call x1, Pallas kernels, prepare(): pl.pallas_call(prepare_kernel, out_shape=[jax.ShapeDtypeStruct((rows, wid...  1.74 us
    ppermute x6, starting transfers between devices, shards(): swap = lambda a: lax.ppermute(a, 'sub', [(0, 1), (1, 0)])  1.12 us
  transfers between devices with their start and end apart: 12, of which 6 were waited for; matrix products, arithmetic and copies ran while one was open for 0% of the time, Pallas kernels for 23%

profile of v5, /device:TPU:0, one launch (start us, length us, event | category | flops | bytes accessed | tf_op | source)
XLA Modules:
  0.0 53.7 jit_solution(5145366035786060983)
XLA Ops:
  0.7 1.7 %prepare.1 = (bf16[128,3712]{1,0:T(8,128)(2,1)S(1)}, s32[1]{0:T(128)}) custom-call(s32[1]{0:T(128)S(6)} %copy.14.len_ref, bf16[128,512]{1,0:T(8,128)(2,1)} %refs_2_.1, bf16[128,4096]{1,0:T(8,128)(2,1)} %refs_18_.3, bf16[128,2048]{1,0:T(8,128)(2,1)} %refs_19_.3, bf16[64,128]{1,0:T(8,128)(2,1)} %bitcast.4), custom_call_target="tpu_custom_call" | custom-call | bytes 1900544 | tf_op jit(solution)/shard_map/prepare/pallas_call | solution.py:138
  2.4 0.6 %collective-permute-start.9 = (bf16[128,3712]{1,0:T(8,128)(2,1)S(1)}, bf16[128,3712]{1,0:T(8,128)(2,1)S(1)}, u32[]{:S(2)}, u32[]{:S(2)}) collective-permute-start(bf16[128,3712]{1,0:T(8,128)(2,1)S(1)} %get-tuple-element.21), channel_id=1, source_target_pairs={{0,1},{1,0},{2,3},{3,2},{4,5},{5,4},{6,7},{7,6},{8,9},{9,8},{10,11... | collective-permute-start | bytes 2850824 | tf_op jit(solution)/shard_map/ppermute | solution.py:431
  3.0 3.7 %collective-permute-start.1 = (s32[1,6]{1,0:T(1,128)}, s32[1,6]{1,0:T(1,128)S(1)}, u32[]{:S(2)}, u32[]{:S(2)}) collective-permute-start(s32[1,6]{1,0:T(1,128)} %refs_0_.1), channel_id=1, source_target_pairs={{0,8},{4,12},{8,0},{12,4},{1,9},{5,13},{9,1},{13,5},{2,10},{6,14},... | collective-permute-start | bytes 80 | tf_op jit(solution)/shard_map/ppermute | solution.py:432
  6.6 1.6 %collective-permute-start = (s32[1,6]{1,0:T(1,128)}, s32[1,6]{1,0:T(1,128)S(1)}, u32[]{:S(2)}, u32[]{:S(2)}) collective-permute-start(s32[1,6]{1,0:T(1,128)} %refs_0_.1), channel_id=1, source_target_pairs={{0,4},{4,0},{8,12},{12,8},{1,5},{5,1},{9,13},{13,9},{2,6},{6,2},{1... | collective-permute-start | bytes 80 | tf_op jit(solution)/shard_map/ppermute | solution.py:432
  8.2 0.1 collective-permute-done.1.refs_2_
  8.3 2.0 %collective-permute-done.refs_1_ = s32[1,6]{1,0:T(1,128)S(1)} collective-permute-done((s32[1,6]{1,0:T(1,128)}, s32[1,6]{1,0:T(1,128)S(1)}, u32[]{:S(2)}, u32[]{:S(2)}) %collective-permute-start) | collective-permute-done | bytes 56 | tf_op jit(solution)/shard_map/ppermute | solution.py:432
  10.3 3.4 %collective-permute-done.2.refs_3_ = s32[1,6]{1,0:T(1,128)S(1)} collective-permute-done((s32[1,6]{1,0:T(1,128)}, s32[1,6]{1,0:T(1,128)S(1)}, u32[]{:S(2)}, u32[]{:S(2)}) %collective-permute-start.2) | collective-permute-done | bytes 56 | tf_op jit(solution)/shard_map/ppermute | solution.py:432
  13.7 3.3 %pack.1 = (bf16[288,256]{1,0:T(8,128)(2,1)S(1)}, bf16[288,256]{1,0:T(8,128)(2,1)S(1)}, bf16[288,256]{1,0:T(8,128)(2,1)S(1)}, bf16[288,256]{1,0:T(8,128)(2,1)S(1)}, s32[9]{0:T(128)S(1)}) custom-call(s32[1,6]{1,0:T(1,128)} %refs_0_.1, s32[1,6]{1,0:T(1,128)S(1)} %collective-permute-done.refs_1_, s32[1,6]{1,0:T(1,128)S(1)} %collective-permute-done.1.refs_2_, ...), custom_call_target="tpu_custom_call" | custom-call | bytes 1179648 | tf_op jit(solution)/shard_map/pack/pallas_call | solution.py:87
  17.0 0.1 collective-permute-start.3
  17.1 0.1 collective-permute-start.4
  17.2 4.3 %collective-permute-start.5 = (bf16[288,256]{1,0:T(8,128)(2,1)S(1)}, bf16[288,256]{1,0:T(8,128)(2,1)S(1)}, u32[]{:S(2)}, u32[]{:S(2)}) collective-permute-start(bf16[288,256]{1,0:T(8,128)(2,1)S(1)} %get-tuple-element.20), channel_id=1, source_target_pairs={{0,4},{4,0},{8,12},{12,8},{1,5},{5,1},{9,13},{13,9},{2,6},{6,2},{1... | collective-permute-start | bytes 442376 | tf_op jit(solution)/shard_map/ppermute | solution.py:432
  21.5 0.0 collective-permute-start.10
  21.5 4.1 %collective-permute-done.3.refs_0_ = bf16[288,256]{1,0:T(8,128)(2,1)S(1)} collective-permute-done((bf16[288,256]{1,0:T(8,128)(2,1)S(1)}, bf16[288,256]{1,0:T(8,128)(2,1)S(1)}, u32[]{:S(2)}, u32[]{:S(2)}) %collective-permute-start.3) | collective-permute-done | bytes 147488 | tf_op jit(solution)/shard_map/ppermute | solution.py:432
  25.6 0.0 collective-permute-start.6
  25.6 4.2 %collective-permute-done.4.refs_1_ = bf16[288,256]{1,0:T(8,128)(2,1)S(1)} collective-permute-done((bf16[288,256]{1,0:T(8,128)(2,1)S(1)}, bf16[288,256]{1,0:T(8,128)(2,1)S(1)}, u32[]{:S(2)}, u32[]{:S(2)}) %collective-permute-start.4) | collective-permute-done | bytes 147488 | tf_op jit(solution)/shard_map/ppermute | solution.py:432
  29.8 0.5 collective-permute-start.8
  30.3 0.0 collective-permute-done.9.refs_4_.refs_5_.refs_8_.refs_9_.refs_14_.refs_15_.refs_20_.refs_21_
  30.3 8.8 %attend_new.1 = (f32[2048,256]{1,0:T(8,128)S(1)}, f32[128,256]{1,0:T(8,128)S(1)}) custom-call(s32[1]{0:T(128)} %bitcast.sub_ref, s32[9]{0:T(128)S(1)} %get-tuple-element.17.where_ref, bf16[288,256]{1,0:T(8,128)(2,1)S(1)} %get-tuple-element.22.refs_0_, bf16[288,256]{1,0:T(8,128)(2,1)S(1)} %collective-permute-done.10.refs_1_, bf16[128,512]{1,0:T(8,128)(2,1)} %refs_2_.1, ...), custom_call_target="tpu_custom_call" | custom-call | flops 4294967296 | bytes 8388608 | tf_op jit(solution)/shard_map/attend_new/pallas_call | solution.py:373
  39.1 0.0 collective-permute-done.6.refs_3_
  39.1 0.0 collective-permute-done.7.refs_4_
  39.2 11.8 %attend_prefix.1 = (bf16[128,4096]{1,0:T(8,128)(2,1)}, bf16[128,2048]{1,0:T(8,128)(2,1)S(1)}) custom-call(s32[1]{0:T(128)} %bitcast.sub_ref, s32[9]{0:T(128)S(1)} %get-tuple-element.17.where_ref, bf16[288,256]{1,0:T(8,128)(2,1)S(1)} %collective-permute-done.3.refs_0_, bf16[288,256]{1,0:T(8,128)(2,1)S(1)} %collective-permute-done.4.refs_1_, ...), custom_call_target="tpu_custom_call" | custom-call | flops 6442450944 | bytes 8388608 | tf_op jit(solution)/shard_map/attend_prefix/pallas_call | solution.py:373
  51.0 0.0 collective-permute-start.11
  51.0 1.9 %collective-permute-done.11.back_ref = bf16[128,2048]{1,0:T(8,128)(2,1)S(1)} collective-permute-done((bf16[128,2048]{1,0:T(8,128)(2,1)S(1)}, bf16[128,2048]{1,0:T(8,128)(2,1)S(1)}, u32[]{:S(2)}, u32[]{:S(2)}) %collective-permute-start.11) | collective-permute-done | bytes 524320 | tf_op jit(solution)/shard_map/ppermute | solution.py:431
  52.9 0.8 %join.1 = bf16[128,4096]{1,0:T(8,128)(2,1)} custom-call(bf16[128,4096]{1,0:T(8,128)(2,1)} %get-tuple-element.25.kept_ref, bf16[128,2048]{1,0:T(8,128)(2,1)S(1)} %collective-permute-done.11.back_ref), custom_call_target="tpu_custom_call", output_to_operand_aliasing={{}: (0, {})} | custom-call | tf_op jit(solution)/shard_map/join/pallas_call | solution.py:404
  (5 shorter events, 0.0 us)
Async XLA Ops:
  2.4 27.9 %collective-permute-start.9 = (bf16[128,3712]{1,0:T(8,128)(2,1)S(1)}, bf16[128,3712]{1,0:T(8,128)(2,1)S(1)}, u32[]{:S(2)}, u32[]{:S(2)}) collective-permute-start(bf16[128,3712]{1,0:T(8,128)(2,1)S(1)} %get-tuple-element.21), channel_id=1, source_target_pairs={{0,1},{1,0},{2,3},{3,2},{4,5},{5,4},{6,7},{7,6},{8,9},{9,8},{10,11... | collective-permute-start | bytes 2850824 | tf_op jit(solution)/shard_map/ppermute | solution.py:431
  3.0 5.3 %collective-permute-start.1 = (s32[1,6]{1,0:T(1,128)}, s32[1,6]{1,0:T(1,128)S(1)}, u32[]{:S(2)}, u32[]{:S(2)}) collective-permute-start(s32[1,6]{1,0:T(1,128)} %refs_0_.1), channel_id=1, source_target_pairs={{0,8},{4,12},{8,0},{12,4},{1,9},{5,13},{9,1},{13,5},{2,10},{6,14},... | collective-permute-start | bytes 80 | tf_op jit(solution)/shard_map/ppermute | solution.py:432
  6.6 3.7 %collective-permute-start = (s32[1,6]{1,0:T(1,128)}, s32[1,6]{1,0:T(1,128)S(1)}, u32[]{:S(2)}, u32[]{:S(2)}) collective-permute-start(s32[1,6]{1,0:T(1,128)} %refs_0_.1), channel_id=1, source_target_pairs={{0,4},{4,0},{8,12},{12,8},{1,5},{5,1},{9,13},{13,9},{2,6},{6,2},{1... | collective-permute-start | bytes 80 | tf_op jit(solution)/shard_map/ppermute | solution.py:432
  8.2 5.5 %collective-permute-start.2 = (s32[1,6]{1,0:T(1,128)}, s32[1,6]{1,0:T(1,128)S(1)}, u32[]{:S(2)}, u32[]{:S(2)}) collective-permute-start(s32[1,6]{1,0:T(1,128)} %refs_0_.1), channel_id=1, source_target_pairs={{0,12},{4,8},{8,4},{12,0},{1,13},{5,9},{9,5},{13,1},{2,14},{6,10},... | collective-permute-start | bytes 80 | tf_op jit(solution)/shard_map/ppermute | solution.py:432
  17.0 8.6 %collective-permute-start.3 = (bf16[288,256]{1,0:T(8,128)(2,1)S(1)}, bf16[288,256]{1,0:T(8,128)(2,1)S(1)}, u32[]{:S(2)}, u32[]{:S(2)}) collective-permute-start(bf16[288,256]{1,0:T(8,128)(2,1)S(1)} %get-tuple-element.18), channel_id=1, source_target_pairs={{0,12},{4,8},{8,4},{12,0},{1,13},{5,9},{9,5},{13,1},{2,14},{6,10},... | collective-permute-start | bytes 442376 | tf_op jit(solution)/shard_map/ppermute | solution.py:432
  17.1 12.7 %collective-permute-start.4 = (bf16[288,256]{1,0:T(8,128)(2,1)S(1)}, bf16[288,256]{1,0:T(8,128)(2,1)S(1)}, u32[]{:S(2)}, u32[]{:S(2)}) collective-permute-start(bf16[288,256]{1,0:T(8,128)(2,1)S(1)} %get-tuple-element.19), channel_id=1, source_target_pairs={{0,8},{4,12},{8,0},{12,4},{1,9},{5,13},{9,1},{13,5},{2,10},{6,14},... | collective-permute-start | bytes 442376 | tf_op jit(solution)/shard_map/ppermute | solution.py:432
  17.2 12.6 %collective-permute-start.5 = (bf16[288,256]{1,0:T(8,128)(2,1)S(1)}, bf16[288,256]{1,0:T(8,128)(2,1)S(1)}, u32[]{:S(2)}, u32[]{:S(2)}) collective-permute-start(bf16[288,256]{1,0:T(8,128)(2,1)S(1)} %get-tuple-element.20), channel_id=1, source_target_pairs={{0,4},{4,0},{8,12},{12,8},{1,5},{5,1},{9,13},{13,9},{2,6},{6,2},{1... | collective-permute-start | bytes 442376 | tf_op jit(solution)/shard_map/ppermute | solution.py:432
  21.5 8.8 %collective-permute-start.10 = (bf16[288,256]{1,0:T(8,128)(2,1)S(1)}, bf16[288,256]{1,0:T(8,128)(2,1)S(1)}, u32[]{:S(2)}, u32[]{:S(2)}) collective-permute-start(bf16[288,256]{1,0:T(8,128)(2,1)S(1)} %get-tuple-element.22.refs_0_), channel_id=1, source_target_pairs={{0,1},{1,0},{2,3},{3,2},{4,5},{5,4},{6,7},{7,6},{8,9},{9,8},{10,11... | collective-permute-start | bytes 442376 | tf_op jit(solution)/shard_map/ppermute | solution.py:431
  25.6 13.5 %collective-permute-start.6 = (bf16[288,256]{1,0:T(8,128)(2,1)S(1)}, bf16[288,256]{1,0:T(8,128)(2,1)S(1)}, u32[]{:S(2)}, u32[]{:S(2)}) collective-permute-start(bf16[288,256]{1,0:T(8,128)(2,1)S(1)} %collective-permute-done.3.refs_0_), channel_id=1, source_target_pairs={{0,1},{1,0},{2,3},{3,2},{4,5},{5,4},{6,7},{7,6},{8,9},{9,8},{10,11... | collective-permute-start | bytes 442376 | tf_op jit(solution)/shard_map/ppermute | solution.py:431
  29.8 9.3 %collective-permute-start.7 = (bf16[288,256]{1,0:T(8,128)(2,1)S(1)}, bf16[288,256]{1,0:T(8,128)(2,1)S(1)}, u32[]{:S(2)}, u32[]{:S(2)}) collective-permute-start(bf16[288,256]{1,0:T(8,128)(2,1)S(1)} %collective-permute-done.4.refs_1_), channel_id=1, source_target_pairs={{0,1},{1,0},{2,3},{3,2},{4,5},{5,4},{6,7},{7,6},{8,9},{9,8},{10,11... | collective-permute-start | bytes 442376 | tf_op jit(solution)/shard_map/ppermute | solution.py:431
  29.8 9.3 %collective-permute-start.8 = (bf16[288,256]{1,0:T(8,128)(2,1)S(1)}, bf16[288,256]{1,0:T(8,128)(2,1)S(1)}, u32[]{:S(2)}, u32[]{:S(2)}) collective-permute-start(bf16[288,256]{1,0:T(8,128)(2,1)S(1)} %collective-permute-done.5.refs_2_), channel_id=1, source_target_pairs={{0,1},{1,0},{2,3},{3,2},{4,5},{5,4},{6,7},{7,6},{8,9},{9,8},{10,11... | collective-permute-start | bytes 442376 | tf_op jit(solution)/shard_map/ppermute | solution.py:431
  51.0 1.9 %collective-permute-start.11 = (bf16[128,2048]{1,0:T(8,128)(2,1)S(1)}, bf16[128,2048]{1,0:T(8,128)(2,1)S(1)}, u32[]{:S(2)}, u32[]{:S(2)}) collective-permute-start(bf16[128,2048]{1,0:T(8,128)(2,1)S(1)} %get-tuple-element.26), channel_id=1, source_target_pairs={{0,1},{1,0},{2,3},{3,2},{4,5},{5,4},{6,7},{7,6},{8,9},{9,8},{10,11... | collective-permute-start | bytes 1572872 | tf_op jit(solution)/shard_map/ppermute | solution.py:431

commit v6 on v5

v6 whole, which is shorter than its diff:
```python
import functools
import math

import jax
import jax.numpy as jnp
from jax import lax
from jax.experimental import pallas as pl
from jax.experimental.pallas import tpu as pltpu
from jax.sharding import PartitionSpec as P


NOPE = 128
ROPE = 64
VDIM = 128
CAP = 2
LANES = 128
HIDE = -1e30


def pack_kernel(n, blocks, pool_local, lists, slots_ref, len_ref, pool_ref, rope_ref, outs, where_ref,
                index_ref, count_ref, lat_sem, rope_sem):
    me = lax.axis_index("req")
    sub = lax.axis_index("sub")
    block = pool_ref.shape[1]
    width = pool_ref.shape[2]
    for i in range(n * CAP):
        index_ref[i] = 0
        where_ref[i] = -1
    where_ref[n * CAP] = len_ref[0]
    for i in range(n):
        count_ref[i] = 0
    for k in range(n):
        found = jnp.int32(0)
        for p in range(blocks):
            physical = slots_ref[lists[k][0, p]]
            owner = physical // pool_local
            mine = owner == me

            @pl.when(mine)
            def _():
                index_ref[k * CAP + found] = physical - owner * pool_local

            found = found + mine.astype(jnp.int32)
            if k == 0:
                step = jnp.bitwise_xor(me, owner)
                earlier = count_ref[step]
                where_ref[step * CAP + earlier] = p
                count_ref[step] = earlier + 1
    parts = width // block
    rows = ROPE // parts
    copies = []
    for k in range(n):
        for c in range(CAP):
            copies.append(pltpu.make_async_copy(
                pool_ref.at[index_ref[k * CAP + c]],
                outs[k].at[pl.ds(c * block, block)],
                lat_sem.at[k * CAP + c],
            ))
        for i in range(parts):
            copies.append(pltpu.make_async_copy(
                rope_ref.at[index_ref[k * CAP + sub], pl.ds(i * rows, rows)],
                outs[k].at[pl.ds(CAP * block, rows), pl.ds(i * block, block)],
                rope_sem.at[k * parts + i],
            ))
    for copy in copies:
        copy.start()
    for copy in copies:
        copy.wait()


def pack(n, lists, block_slot, prefix_len, pool_latent, rope_turned):
    pool_local, block, width = pool_latent.shape
    blocks = lists[0].shape[1]
    rows = CAP * block + block * ROPE // width
    vmem = pl.BlockSpec(memory_space=pltpu.VMEM)
    smem = pl.BlockSpec(memory_space=pltpu.SMEM)

    def body(*refs):
        pack_kernel(
            n, blocks, pool_local, refs[:n], *refs[n : n + 4],
            refs[n + 4 : 2 * n + 4], *refs[2 * n + 4 :],
        )

    out = pl.pallas_call(
        body,
        out_shape=[jax.ShapeDtypeStruct((rows, width), jnp.bfloat16)] * n
        + [jax.ShapeDtypeStruct((n * CAP + 1,), jnp.int32)],
        in_specs=[smem] * (n + 2) + [pl.BlockSpec(memory_space=pl.ANY)] * 2,
        out_specs=[vmem] * n + [smem],
        scratch_shapes=[
            pltpu.SMEM((n * CAP,), jnp.int32),
            pltpu.SMEM((n,), jnp.int32),
            pltpu.SemaphoreType.DMA((n * CAP,)),
            pltpu.SemaphoreType.DMA((n * width // block,)),
        ],
        compiler_params=pltpu.CompilerParams(vmem_limit_bytes=16 << 20),
        cost_estimate=pl.CostEstimate(flops=0, bytes_accessed=4 * n * rows * width, transcendentals=0),
        name="pack",
    )(*lists, block_slot, prefix_len, pool_latent, rope_turned)
    return out[:n], out[n]


def prepare_kernel(len_ref, lat_ref, qn_ref, qr_ref, rope_ref, wk_ref, wv_ref,
                   out_ref, qn_out, qr_out, wk_out, wv_out, kept_ref, sem):
    kept_ref[0] = len_ref[0]
    sub = lax.axis_index("sub")
    latent = lat_ref.shape[1]
    tail = out_ref.shape[1] - rope_ref.shape[1]

    def part(ref, which):
        half = ref.shape[1] // 2
        return ref.at[:, pl.ds(pl.multiple_of(which * half, LANES), half)]

    half = qn_out.shape[1]
    rope_half = qr_out.shape[1]
    moves = [
        (lat_ref, out_ref.at[:, pl.ds(0, latent)]),
        (part(qn_ref, 1 - sub), out_ref.at[:, pl.ds(latent, half)]),
        (part(qr_ref, 1 - sub), out_ref.at[:, pl.ds(latent + half, rope_half)]),
        (rope_ref, out_ref.at[pl.ds(0, ROPE), pl.ds(tail, rope_ref.shape[1])]),
        (part(qn_ref, sub), qn_out),
        (part(qr_ref, sub), qr_out),
        (part(wk_ref, sub), wk_out),
        (part(wv_ref, sub), wv_out),
    ]
    copies = [pltpu.make_async_copy(*move, sem.at[i]) for i, move in enumerate(moves)]
    for copy in copies:
        copy.start()
    for copy in copies:
        copy.wait()


def prepare(prefix_len, new_latent, q_nope, q_rope, rope_turned, w_uk, w_uv):
    rows, latent = new_latent.shape
    half = q_nope.shape[1] // 2
    rope_half = q_rope.shape[1] // 2
    shapes = [
        (rows, latent + half + rope_half + rows),
        (rows, half),
        (rows, rope_half),
        (latent, half),
        (latent, half),
    ]
    return pl.pallas_call(
        prepare_kernel,
        out_shape=[jax.ShapeDtypeStruct(shape, jnp.bfloat16) for shape in shapes]
        + [jax.ShapeDtypeStruct((1,), jnp.int32)],
        in_specs=[pl.BlockSpec(memory_space=pltpu.SMEM)] + [pl.BlockSpec(memory_space=pl.ANY)] * 6,
        out_specs=[pl.BlockSpec(memory_space=pltpu.VMEM)] * 5
        + [pl.BlockSpec(memory_space=pltpu.SMEM)],
        scratch_shapes=[pltpu.SemaphoreType.DMA((8,))],
        compiler_params=pltpu.CompilerParams(vmem_limit_bytes=16 << 20),
        cost_estimate=pl.CostEstimate(
            flops=0, bytes_accessed=4 * sum(math.prod(shape) for shape in shapes), transcendentals=0
        ),
        name="prepare",
    )(prefix_len, new_latent, q_nope, q_rope, rope_turned, w_uk, w_uv)


RATE = math.log2(math.e) / math.sqrt(NOPE + ROPE)


def attend_kernel(steps, fresh, *refs):
    count = len(steps)
    where_ref, lat_a, rope_a, other, qn_ref, qr_ref, wk_ref, wv_ref, *refs = refs
    mine = refs[:count]
    theirs = refs[count : 2 * count]
    refs = refs[2 * count :]
    if fresh:
        acc_ref, stat_ref, lat, kc, vt, score, weight, peak, bias = refs
    else:
        (acc_ref, stat_ref, out_ref, send_ref, lat, kc, vt, score, weight, peak, result,
         sem) = refs
    sub = lax.axis_index("sub")
    block, latent = lat_a.shape
    chunk = CAP * block
    first = chunk if fresh else 0
    queries = 2 * block
    keys = lat.shape[0]
    half = qn_ref.shape[1]
    halves = half // (4 * NOPE)
    nope_at = latent
    rope_at = nope_at + half
    tail_at = rope_at + qr_ref.shape[1]
    head = lambda j: slice(j * LANES, (j + 1) * LANES)
    at = lambda start, size: pl.ds(pl.multiple_of(start, size), size)

    def build():
        def put_tails(base, rope, mask):
            kc[0, base : base + block, NOPE:] = jnp.concatenate([rope, mask], axis=1)
            kc[1, base : base + block, NOPE:] = jnp.concatenate([mask, rope], axis=1)

        lane = lax.broadcasted_iota(jnp.int32, (block, ROPE), 1)
        row = lax.broadcasted_iota(jnp.int32, (block, ROPE), 0)
        length = where_ref[where_ref.shape[0] - 1]
        vt[:, :, VDIM:, :] = jnp.ones((2, 2, 16, keys), jnp.bfloat16)
        for i, k in enumerate(steps):
            width = mine[i].shape[1]
            here = pl.multiple_of(sub * width, width)
            there = pl.multiple_of((1 - sub) * width, width)
            base = first + i * chunk
            lat[base : base + chunk, pl.ds(here, width)] = mine[i][:chunk, :]
            lat[base : base + chunk, pl.ds(there, width)] = theirs[i][:chunk, :]
            for c in range(CAP):
                packed = jnp.where(sub == c, mine[i][chunk:, :], theirs[i][chunk:, :])
                rope = jnp.concatenate(
                    [packed[:, j * block : (j + 1) * block] for j in range(width // block)], axis=0
                )
                p = where_ref[k * CAP + c]
                hidden = (lane == 0) & ((p < 0) | (p * block + row >= length))
                put_tails(
                    base + c * block, rope.T, jnp.where(hidden, HIDE, 0.0).astype(jnp.bfloat16)
                )
        if fresh:
            plain = jnp.zeros((block, ROPE), jnp.bfloat16)
            lat[:block, :] = lat_a[...]
            lat[block:chunk, :] = other[:, :latent]
            put_tails(0, rope_a[...].T, plain)
            put_tails(block, other[:ROPE, tail_at:].T, plain)
            i = lax.broadcasted_iota(jnp.int32, (queries, queries), 0)
            j = lax.broadcasted_iota(jnp.int32, (queries, queries), 1)
            flip = sub * block
            seen = jnp.bitwise_xor(i, flip) <= jnp.bitwise_xor(j, flip)
            bias[...] = jnp.where(seen, 0.0, HIDE)

    def form_keys(pair):
        columns = at(pair * 2 * NOPE, 2 * NOPE)
        for r in range(0, keys, chunk):
            rows = slice(r, r + chunk)
            k2 = jnp.dot(lat[rows, :], wk_ref[:, columns], preferred_element_type=jnp.float32)
            for j in range(2):
                kc[j, rows, :NOPE] = k2[:, head(j)].astype(jnp.bfloat16)

    def form_values(pair, slot):
        v2 = lax.dot_general(
            wv_ref[:, at(pair * 2 * VDIM, 2 * VDIM)], lat[...], (((0,), (1,)), ((), ())),
            preferred_element_type=jnp.float32,
        )
        for j in range(2):
            vt[slot, j, :VDIM, :] = v2[j * VDIM : (j + 1) * VDIM].astype(jnp.bfloat16)

    def form_scores(pair, slot, j):
        lane = lax.broadcasted_iota(jnp.int32, (queries, LANES), 1)
        nope = pair * 2 * NOPE + j * NOPE
        qn = jnp.concatenate(
            [qn_ref[:, at(nope, NOPE)], other[:, at(nope_at + nope, NOPE)]], axis=0
        )
        rope = pair * LANES
        qr = jnp.concatenate(
            [qr_ref[:, at(rope, LANES)], other[:, at(rope_at + rope, LANES)]], axis=0
        )
        fill = jnp.where(lane == (1 - j) * ROPE, 1.0, 0.0).astype(jnp.bfloat16)
        own = (lane >= ROPE) if j else (lane < ROPE)
        qc = jnp.concatenate([qn, jnp.where(own, qr, fill)], axis=1)
        s = lax.dot_general(
            kc[j], qc, (((1,), (1,)), ((), ())), preferred_element_type=jnp.float32
        )
        if fresh:
            s = jnp.concatenate([s[:queries] + bias[...], s[queries:]], axis=0)
        score[slot, j] = s
        most = jnp.max(s, axis=0, keepdims=True)
        peak[slot, j] = jnp.broadcast_to(most, (8, queries))

    def form_weights(pair, slot, j):
        most = peak[slot, j, :1, :]
        if not fresh:
            most = jnp.maximum(most, stat_ref[at((2 * pair + j) * 8, 8), :][:1])
        weight[slot, j] = jnp.exp2((score[slot, j] - most) * RATE).astype(jnp.bfloat16)

    def form_output(pair, slot, j):
        o = jnp.dot(vt[slot, j], weight[slot, j], preferred_element_type=jnp.float32)
        o, norm = o[:VDIM], o[VDIM : VDIM + 1]
        rows = at((2 * pair + j) * VDIM, VDIM)
        stat_rows = at((2 * pair + j) * 8, 8)
        if fresh:
            acc_ref[rows, :] = o
            row = lax.broadcasted_iota(jnp.int32, (8, queries), 0)
            stat_ref[stat_rows, :] = jnp.where(row == 0, peak[slot, j], norm)
        else:
            stat = stat_ref[stat_rows, :]
            old = stat[:1]
            most = jnp.maximum(peak[slot, j, :1, :], old)
            keep = jnp.exp2((old - most) * RATE)
            norm = norm + keep * stat[1:2]
            o = (o + keep * acc_ref[rows, :]) / norm
            o = o.T.astype(jnp.bfloat16)
            columns = at((2 * pair + j) * VDIM, VDIM)
            result[:, columns] = o[:block]
            send_ref[:, columns] = o[block:]

    def both(pair, slot, more=True):
        form_weights(pair, slot, 0)
        form_weights(pair, slot, 1)
        if more:
            form_keys(pair + 1)
            form_values(pair + 1, 1 - slot)
        for j in range(2):
            form_output(pair, slot, j)
            if more:
                form_scores(pair + 1, 1 - slot, j)

    def deliver(t):
        width = 4 * VDIM
        return pltpu.make_async_copy(
            result.at[:, at(t * width, width)],
            out_ref.at[:, at(sub * half + t * width, width)],
            sem.at[t],
        )

    build()
    form_keys(0)
    form_values(0, 0)
    for j in range(2):
        form_scores(0, 0, j)

    def body(t, carry):
        both(2 * t, 0)
        both(2 * t + 1, 1)
        if not fresh:
            deliver(t).start()
        return carry

    if halves > 1:
        lax.fori_loop(0, halves - 1, body, 0)
    both(2 * halves - 2, 0)
    both(2 * halves - 1, 1, False)
    if not fresh:
        deliver(halves - 1).start()
        for t in range(halves):
            deliver(t).wait()


def attend(steps, where, mine, theirs, new_latent, rope_turned, other, qn, qr, wk, wv, state):
    fresh = state is None
    block, latent = new_latent.shape
    heads = wk.shape[1] // NOPE
    keys = (len(steps) + (1 if fresh else 0)) * CAP * block
    vmem = pl.BlockSpec(memory_space=pltpu.VMEM)
    args = [where, new_latent, rope_turned, other, qn, qr, wk, wv, *mine, *theirs]
    specs = [pl.BlockSpec(memory_space=pltpu.SMEM)] + [vmem] * (len(args) - 1)
    scratch = [
        pltpu.VMEM((keys, latent), jnp.bfloat16),
        pltpu.VMEM((2, keys, NOPE + LANES), jnp.bfloat16),
        pltpu.VMEM((2, 2, VDIM + 16, keys), jnp.bfloat16),
        pltpu.VMEM((2, 2, keys, 2 * block), jnp.float32),
        pltpu.VMEM((2, 2, keys, 2 * block), jnp.bfloat16),
        pltpu.VMEM((2, 2, 8, 2 * block), jnp.float32),
    ]
    if fresh:
        out_specs = [vmem, vmem]
        out_shape = [
            jax.ShapeDtypeStruct((heads * VDIM, 2 * block), jnp.float32),
            jax.ShapeDtypeStruct((heads * 8, 2 * block), jnp.float32),
        ]
        scratch.append(pltpu.VMEM((2 * block, 2 * block), jnp.float32))
    else:
        specs += [vmem, vmem]
        args += state
        out_specs = [pl.BlockSpec(memory_space=pl.ANY), vmem]
        out_shape = [
            jax.ShapeDtypeStruct((block, 2 * heads * VDIM), jnp.bfloat16),
            jax.ShapeDtypeStruct((block, heads * VDIM), jnp.bfloat16),
        ]
        scratch += [
            pltpu.VMEM((block, heads * VDIM), jnp.bfloat16),
            pltpu.SemaphoreType.DMA((heads // 4,)),
        ]
    return pl.pallas_call(
        functools.partial(attend_kernel, steps, fresh),
        in_specs=specs,
        out_specs=out_specs,
        scratch_shapes=scratch,
        out_shape=out_shape,
        compiler_params=pltpu.CompilerParams(vmem_limit_bytes=(36 if len(steps) < 8 else 48) << 20),
        cost_estimate=pl.CostEstimate(
            flops=4 * keys * latent * heads * NOPE + 8 * block * keys * heads * 256,
            bytes_accessed=8 * 1024 * 1024,
            transcendentals=2 * block * keys * heads,
        ),
        name="attend_new" if fresh else "attend_prefix",
    )(*args)


def join_kernel(kept_ref, back_ref, out_ref, sem):
    there = 1 - lax.axis_index("sub")
    half = back_ref.shape[1]
    copy = pltpu.make_async_copy(
        back_ref, out_ref.at[:, pl.ds(pl.multiple_of(there * half, LANES), half)], sem
    )
    copy.start()
    copy.wait()


def join(kept, back):
    return pl.pallas_call(
        join_kernel,
        out_shape=jax.ShapeDtypeStruct(kept.shape, kept.dtype),
        in_specs=[pl.BlockSpec(memory_space=pl.ANY)] * 2,
        out_specs=pl.BlockSpec(memory_space=pl.ANY),
        scratch_shapes=[pltpu.SemaphoreType.DMA(())],
        input_output_aliases={0: 0},
        compiler_params=pltpu.CompilerParams(vmem_limit_bytes=1 << 20),
        name="join",
    )(kept, back)


def shards(
    q_nope,
    q_rope,
    new_latent,
    new_rope,
    pool_latent,
    pool_rope,
    w_uk,
    w_uv,
    block_list,
    prefix_len,
    block_slot,
):
    n = lax.axis_size("req")
    swap = lambda a: lax.ppermute(a, "sub", [(0, 1), (1, 0)])
    cross = lambda a, k: lax.ppermute(a, "req", [(i, i ^ k) for i in range(n)])
    far = list(range(n - 1, 0, -1))
    keep = lambda a: pltpu.with_memory_space_constraint(a, pltpu.HBM)
    q_nope, q_rope, new_latent, w_uk, w_uv = map(keep, (q_nope, q_rope, new_latent, w_uk, w_uv))
    pool_latent = keep(pool_latent)
    slots = keep(block_slot)
    pool_turned = keep(pool_rope.swapaxes(1, 2))
    rope_turned = keep(new_rope.T)
    got = {}
    for k in far:
        got[k] = cross(block_list, k)
    lists = [keep(block_list)] + [got[k] for k in range(1, n)]
    other, qn, qr, wk, wv, length = prepare(
        prefix_len, new_latent, q_nope, q_rope, rope_turned, w_uk, w_uv
    )
    other = swap(other)
    sent, where = pack(n, lists, slots, length, pool_latent, pool_turned)
    local = swap(sent[0])
    mine = []
    for k in far:
        mine.append(cross(sent[k], k))
    theirs = []
    for k, a in zip(far, mine):
        theirs.append(swap(a))
    common = (new_latent, rope_turned, other, qn, qr, wk, wv)
    state = attend([0], where, [sent[0]], [local], *common, None)
    kept, gone = attend(far, where, mine, theirs, *common, state)
    back = swap(gone)
    return join(kept, back)


def solution(mesh):
    placed = (
        P(("groups", "req", "sub"), "head"),
        P(("groups", "req", "sub"), "head"),
        P(("groups", "req", "sub"), None),
        P(("groups", "req", "sub"), None),
        P(("groups", "req"), None, "sub"),
        P(("groups", "req"), None, None),
        P(None, "head"),
        P(None, "head"),
        P(("groups", "req"), None),
        P(("groups", "req")),
        P("groups"),
    )
    return jax.shard_map(
        shards,
        mesh=mesh,
        in_specs=placed,
        out_specs=P(("groups", "req", "sub"), "head"),
        check_vma=False,
    )
```

time: 53.9 us -> 51.7 us (0.959)
  Pallas kernels: 26.5 us -> 24.3 us
    pallas_call x3, Pallas kernels: 22.4 us -> 20.1 us  [the longest x2 16.7 us: attend(): pl.pallas_call(functools.partial(attend_kernel, steps, fresh), in_specs=s...]
  transfers between devices with their start and end apart: 12 -> 12, of which waited for: 6 -> 5; matrix products, arithmetic and copies ran while one was open for 0% -> 0% of each run, Pallas kernels for 23% -> 20%
where the time goes in v6:
time: 51.7 us; the launch traced here: 51.4 us
  Pallas kernels  24.3 us (47%)
  waiting for transfers between devices  15.6 us (30%)
  starting transfers between devices  10.9 us (21%)
  between operations  0.73 us (1%)
    pallas_call x2, Pallas kernels, attend(): pl.pallas_call(functools.partial(attend_kernel, steps, fresh), in_specs=s...  16.7 us
    ppermute x6, waiting for transfers between devices, shards(): cross = lambda a, k: lax.ppermute(a, 'req', [(i, i ^ k) for i in range(n)])  13.7 us
    ppermute x6, starting transfers between devices, shards(): cross = lambda a, k: lax.ppermute(a, 'req', [(i, i ^ k) for i in range(n)])  9.68 us
    pallas_call x1, Pallas kernels, prepare(): pl.pallas_call(prepare_kernel, out_shape=[jax.ShapeDtypeStruct(shape, jnp...  3.39 us
    pallas_call x1, Pallas kernels, pack(): pl.pallas_call(body, out_shape=[jax.ShapeDtypeStruct((rows, width), jnp.b...  3.37 us
    ppermute x6, waiting for transfers between devices, shards(): swap = lambda a: lax.ppermute(a, 'sub', [(0, 1), (1, 0)])  1.89 us
    ppermute x6, starting transfers between devices, shards(): swap = lambda a: lax.ppermute(a, 'sub', [(0, 1), (1, 0)])  1.17 us
  transfers between devices with their start and end apart: 12, of which 5 were waited for; matrix products, arithmetic and copies ran while one was open for 0% of the time, Pallas kernels for 20%

profile of v6, /device:TPU:0, one launch (start us, length us, event | category | flops | bytes accessed | tf_op | source)
XLA Modules:
  0.0 51.4 jit_solution(3169330623036755597)
XLA Ops:
  0.7 0.0 copy-start
  0.7 3.4 %prepare.1 = (bf16[128,3712]{1,0:T(8,128)(2,1)S(1)}, bf16[128,2048]{1,0:T(8,128)(2,1)S(1)}, bf16[128,1024]{1,0:T(8,128)(2,1)S(1)}, bf16[512,2048]{1,0:T(8,128)(2...) custom-call(s32[1]{0:T(128)S(6)} %copy.14.len_ref, bf16[128,512]{1,0:T(8,128)(2,1)} %refs_1_.3, ...), custom_call_target="tpu_custom_call" | custom-call | bytes 11862016 | tf_op jit(solution)/shard_map/prepare/pallas_call | solution.py:144
  4.1 0.6 %collective-permute-start.3 = (bf16[128,3712]{1,0:T(8,128)(2,1)S(1)}, bf16[128,3712]{1,0:T(8,128)(2,1)S(1)}, u32[]{:S(2)}, u32[]{:S(2)}) collective-permute-start(bf16[128,3712]{1,0:T(8,128)(2,1)S(1)} %get-tuple-element.22), channel_id=1, source_target_pairs={{0,1},{1,0},{2,3},{3,2},{4,5},{5,4},{6,7},{7,6},{8,9},{9,8},{10,11... | collective-permute-start | bytes 2850824 | tf_op jit(solution)/shard_map/ppermute | solution.py:421
  4.6 3.7 %collective-permute-start.1 = (s32[1,6]{1,0:T(1,128)S(1)}, s32[1,6]{1,0:T(1,128)S(1)}, u32[]{:S(2)}, u32[]{:S(2)}) collective-permute-start(s32[1,6]{1,0:T(1,128)S(1)} %copy-done), channel_id=1, source_target_pairs={{0,8},{4,12},{8,0},{12,4},{1,9},{5,13},{9,1},{13,5},{2,10},{6,14},... | collective-permute-start | bytes 80 | tf_op jit(solution)/shard_map/ppermute | solution.py:422
  8.3 1.6 %collective-permute-start = (s32[1,6]{1,0:T(1,128)S(1)}, s32[1,6]{1,0:T(1,128)S(1)}, u32[]{:S(2)}, u32[]{:S(2)}) collective-permute-start(s32[1,6]{1,0:T(1,128)S(1)} %copy-done), channel_id=1, source_target_pairs={{0,4},{4,0},{8,12},{12,8},{1,5},{5,1},{9,13},{13,9},{2,6},{6,2},{1... | collective-permute-start | bytes 80 | tf_op jit(solution)/shard_map/ppermute | solution.py:422
  9.9 2.0 %collective-permute-done.refs_1_ = s32[1,6]{1,0:T(1,128)S(1)} collective-permute-done((s32[1,6]{1,0:T(1,128)S(1)}, s32[1,6]{1,0:T(1,128)S(1)}, u32[]{:S(2)}, u32[]{:S(2)}) %collective-permute-start) | collective-permute-done | bytes 56 | tf_op jit(solution)/shard_map/ppermute | solution.py:422
  11.9 3.4 %collective-permute-done.2.refs_3_ = s32[1,6]{1,0:T(1,128)S(1)} collective-permute-done((s32[1,6]{1,0:T(1,128)S(1)}, s32[1,6]{1,0:T(1,128)S(1)}, u32[]{:S(2)}, u32[]{:S(2)}) %collective-permute-start.2) | collective-permute-done | bytes 56 | tf_op jit(solution)/shard_map/ppermute | solution.py:422
  15.2 3.4 %pack.1 = (bf16[288,256]{1,0:T(8,128)(2,1)S(1)}, bf16[288,256]{1,0:T(8,128)(2,1)S(1)}, bf16[288,256]{1,0:T(8,128)(2,1)S(1)}, bf16[288,256]{1,0:T(8,128)(2,1)S(1)}, s32[9]{0:T(128)S(1)}) custom-call(s32[1,6]{1,0:T(1,128)} %refs_0_.1, s32[1,6]{1,0:T(1,128)S(1)} %collective-permute-done.refs_1_, s32[1,6]{1,0:T(1,128)S(1)} %collective-permute-done.1.refs_2_, ...), custom_call_target="tpu_custom_call" | custom-call | bytes 1179648 | tf_op jit(solution)/shard_map/pack/pallas_call | solution.py:84
  18.6 0.1 collective-permute-start.4
  18.7 0.1 collective-permute-start.5
  18.8 4.3 %collective-permute-start.6 = (bf16[288,256]{1,0:T(8,128)(2,1)S(1)}, bf16[288,256]{1,0:T(8,128)(2,1)S(1)}, u32[]{:S(2)}, u32[]{:S(2)}) collective-permute-start(bf16[288,256]{1,0:T(8,128)(2,1)S(1)} %get-tuple-element.29), channel_id=1, source_target_pairs={{0,4},{4,0},{8,12},{12,8},{1,5},{5,1},{9,13},{13,9},{2,6},{6,2},{1... | collective-permute-start | bytes 442376 | tf_op jit(solution)/shard_map/ppermute | solution.py:422
  23.1 0.0 collective-permute-start.10
  23.1 4.1 %collective-permute-done.4.refs_8_ = bf16[288,256]{1,0:T(8,128)(2,1)S(1)} collective-permute-done((bf16[288,256]{1,0:T(8,128)(2,1)S(1)}, bf16[288,256]{1,0:T(8,128)(2,1)S(1)}, u32[]{:S(2)}, u32[]{:S(2)}) %collective-permute-start.4) | collective-permute-done | bytes 147488 | tf_op jit(solution)/shard_map/ppermute | solution.py:422
  27.2 0.0 collective-permute-start.7
  27.2 4.2 %collective-permute-done.5.refs_9_ = bf16[288,256]{1,0:T(8,128)(2,1)S(1)} collective-permute-done((bf16[288,256]{1,0:T(8,128)(2,1)S(1)}, bf16[288,256]{1,0:T(8,128)(2,1)S(1)}, u32[]{:S(2)}, u32[]{:S(2)}) %collective-permute-start.5) | collective-permute-done | bytes 147488 | tf_op jit(solution)/shard_map/ppermute | solution.py:422
  31.4 0.5 collective-permute-start.9
  31.9 0.0 collective-permute-done.10.refs_9_
  31.9 0.0 collective-permute-done.3.refs_3_
  31.9 6.8 %attend_new.1 = (f32[2048,256]{1,0:T(8,128)S(1)}, f32[128,256]{1,0:T(8,128)S(1)}) custom-call(s32[9]{0:T(128)S(1)} %get-tuple-element.21.refs_0_, bf16[128,512]{1,0:T(8,128)(2,1)} %refs_1_.3, bf16[64,128]{1,0:T(8,128)(2,1)} %bitcast.4, bf16[128,3712]{1,0:T(8,128)(2,1)S(1)} %collective-permute-done.3.refs_3_, ...), custom_call_target="tpu_custom_call" | custom-call | flops 4294967296 | bytes 8388608 | tf_op jit(solution)/shard_map/attend_new/pallas_call | solution.py:368
  38.7 0.0 collective-permute-done.9.refs_13_
  38.7 9.9 %attend_prefix.1 = (bf16[128,4096]{1,0:T(8,128)(2,1)}, bf16[128,2048]{1,0:T(8,128)(2,1)S(1)}) custom-call(s32[9]{0:T(128)S(1)} %get-tuple-element.21.refs_0_, bf16[128,512]{1,0:T(8,128)(2,1)} %refs_1_.3, bf16[64,128]{1,0:T(8,128)(2,1)} %bitcast.5, bf16[128,3712]{1,0:T(8,128)(2,1)S(1)} %collective-permute-done.3.refs_3_, ...), custom_call_target="tpu_custom_call" | custom-call | flops 6442450944 | bytes 8388608 | tf_op jit(solution)/shard_map/attend_prefix/pallas_call | solution.py:368
  48.6 0.1 collective-permute-start.11
  48.7 1.9 %collective-permute-done.11.back_ref = bf16[128,2048]{1,0:T(8,128)(2,1)S(1)} collective-permute-done((bf16[128,2048]{1,0:T(8,128)(2,1)S(1)}, bf16[128,2048]{1,0:T(8,128)(2,1)S(1)}, u32[]{:S(2)}, u32[]{:S(2)}) %collective-permute-start.11) | collective-permute-done | bytes 524320 | tf_op jit(solution)/shard_map/ppermute | solution.py:421
  50.6 0.8 %join.1 = bf16[128,4096]{1,0:T(8,128)(2,1)} custom-call(bf16[128,4096]{1,0:T(8,128)(2,1)} %get-tuple-element.33.kept_ref, bf16[128,2048]{1,0:T(8,128)(2,1)S(1)} %collective-permute-done.11.back_ref), custom_call_target="tpu_custom_call", output_to_operand_aliasing={{}: (0, {})} | custom-call | tf_op jit(solution)/shard_map/join/pallas_call | solution.py:395
  (7 shorter events, 0.0 us)
Async XLA Ops:
  0.7 4.0 %copy-start = (s32[1,6]{1,0:T(1,128)S(1)}, s32[1,6]{1,0:T(1,128)}, u32[]{:S(2)}) copy-start(s32[1,6]{1,0:T(1,128)} %refs_0_.1) | copy-start | bytes 76
  4.1 27.8 %collective-permute-start.3 = (bf16[128,3712]{1,0:T(8,128)(2,1)S(1)}, bf16[128,3712]{1,0:T(8,128)(2,1)S(1)}, u32[]{:S(2)}, u32[]{:S(2)}) collective-permute-start(bf16[128,3712]{1,0:T(8,128)(2,1)S(1)} %get-tuple-element.22), channel_id=1, source_target_pairs={{0,1},{1,0},{2,3},{3,2},{4,5},{5,4},{6,7},{7,6},{8,9},{9,8},{10,11... | collective-permute-start | bytes 2850824 | tf_op jit(solution)/shard_map/ppermute | solution.py:421
  4.6 5.2 %collective-permute-start.1 = (s32[1,6]{1,0:T(1,128)S(1)}, s32[1,6]{1,0:T(1,128)S(1)}, u32[]{:S(2)}, u32[]{:S(2)}) collective-permute-start(s32[1,6]{1,0:T(1,128)S(1)} %copy-done), channel_id=1, source_target_pairs={{0,8},{4,12},{8,0},{12,4},{1,9},{5,13},{9,1},{13,5},{2,10},{6,14},... | collective-permute-start | bytes 80 | tf_op jit(solution)/shard_map/ppermute | solution.py:422
  8.3 3.6 %collective-permute-start = (s32[1,6]{1,0:T(1,128)S(1)}, s32[1,6]{1,0:T(1,128)S(1)}, u32[]{:S(2)}, u32[]{:S(2)}) collective-permute-start(s32[1,6]{1,0:T(1,128)S(1)} %copy-done), channel_id=1, source_target_pairs={{0,4},{4,0},{8,12},{12,8},{1,5},{5,1},{9,13},{13,9},{2,6},{6,2},{1... | collective-permute-start | bytes 80 | tf_op jit(solution)/shard_map/ppermute | solution.py:422
  9.9 5.4 %collective-permute-start.2 = (s32[1,6]{1,0:T(1,128)S(1)}, s32[1,6]{1,0:T(1,128)S(1)}, u32[]{:S(2)}, u32[]{:S(2)}) collective-permute-start(s32[1,6]{1,0:T(1,128)S(1)} %copy-done), channel_id=1, source_target_pairs={{0,12},{4,8},{8,4},{12,0},{1,13},{5,9},{9,5},{13,1},{2,14},{6,10},... | collective-permute-start | bytes 80 | tf_op jit(solution)/shard_map/ppermute | solution.py:422
  18.6 8.6 %collective-permute-start.4 = (bf16[288,256]{1,0:T(8,128)(2,1)S(1)}, bf16[288,256]{1,0:T(8,128)(2,1)S(1)}, u32[]{:S(2)}, u32[]{:S(2)}) collective-permute-start(bf16[288,256]{1,0:T(8,128)(2,1)S(1)} %get-tuple-element.27), channel_id=1, source_target_pairs={{0,12},{4,8},{8,4},{12,0},{1,13},{5,9},{9,5},{13,1},{2,14},{6,10},... | collective-permute-start | bytes 442376 | tf_op jit(solution)/shard_map/ppermute | solution.py:422
  18.7 12.7 %collective-permute-start.5 = (bf16[288,256]{1,0:T(8,128)(2,1)S(1)}, bf16[288,256]{1,0:T(8,128)(2,1)S(1)}, u32[]{:S(2)}, u32[]{:S(2)}) collective-permute-start(bf16[288,256]{1,0:T(8,128)(2,1)S(1)} %get-tuple-element.28), channel_id=1, source_target_pairs={{0,8},{4,12},{8,0},{12,4},{1,9},{5,13},{9,1},{13,5},{2,10},{6,14},... | collective-permute-start | bytes 442376 | tf_op jit(solution)/shard_map/ppermute | solution.py:422
  18.8 12.6 %collective-permute-start.6 = (bf16[288,256]{1,0:T(8,128)(2,1)S(1)}, bf16[288,256]{1,0:T(8,128)(2,1)S(1)}, u32[]{:S(2)}, u32[]{:S(2)}) collective-permute-start(bf16[288,256]{1,0:T(8,128)(2,1)S(1)} %get-tuple-element.29), channel_id=1, source_target_pairs={{0,4},{4,0},{8,12},{12,8},{1,5},{5,1},{9,13},{13,9},{2,6},{6,2},{1... | collective-permute-start | bytes 442376 | tf_op jit(solution)/shard_map/ppermute | solution.py:422
  23.1 8.8 %collective-permute-start.10 = (bf16[288,256]{1,0:T(8,128)(2,1)S(1)}, bf16[288,256]{1,0:T(8,128)(2,1)S(1)}, u32[]{:S(2)}, u32[]{:S(2)}) collective-permute-start(bf16[288,256]{1,0:T(8,128)(2,1)S(1)} %get-tuple-element.30.refs_8_), channel_id=1, source_target_pairs={{0,1},{1,0},{2,3},{3,2},{4,5},{5,4},{6,7},{7,6},{8,9},{9,8},{10,11... | collective-permute-start | bytes 442376 | tf_op jit(solution)/shard_map/ppermute | solution.py:421
  27.2 11.5 %collective-permute-start.7 = (bf16[288,256]{1,0:T(8,128)(2,1)S(1)}, bf16[288,256]{1,0:T(8,128)(2,1)S(1)}, u32[]{:S(2)}, u32[]{:S(2)}) collective-permute-start(bf16[288,256]{1,0:T(8,128)(2,1)S(1)} %collective-permute-done.4.refs_8_), channel_id=1, source_target_pairs={{0,1},{1,0},{2,3},{3,2},{4,5},{5,4},{6,7},{7,6},{8,9},{9,8},{10,11... | collective-permute-start | bytes 442376 | tf_op jit(solution)/shard_map/ppermute | solution.py:421
  31.4 7.3 %collective-permute-start.8 = (bf16[288,256]{1,0:T(8,128)(2,1)S(1)}, bf16[288,256]{1,0:T(8,128)(2,1)S(1)}, u32[]{:S(2)}, u32[]{:S(2)}) collective-permute-start(bf16[288,256]{1,0:T(8,128)(2,1)S(1)} %collective-permute-done.5.refs_9_), channel_id=1, source_target_pairs={{0,1},{1,0},{2,3},{3,2},{4,5},{5,4},{6,7},{7,6},{8,9},{9,8},{10,11... | collective-permute-start | bytes 442376 | tf_op jit(solution)/shard_map/ppermute | solution.py:421
  31.4 7.3 %collective-permute-start.9 = (bf16[288,256]{1,0:T(8,128)(2,1)S(1)}, bf16[288,256]{1,0:T(8,128)(2,1)S(1)}, u32[]{:S(2)}, u32[]{:S(2)}) collective-permute-start(bf16[288,256]{1,0:T(8,128)(2,1)S(1)} %collective-permute-done.6.refs_10_), channel_id=1, source_target_pairs={{0,1},{1,0},{2,3},{3,2},{4,5},{5,4},{6,7},{7,6},{8,9},{9,8},{10,11... | collective-permute-start | bytes 442376 | tf_op jit(solution)/shard_map/ppermute | solution.py:421
  48.6 2.0 %collective-permute-start.11 = (bf16[128,2048]{1,0:T(8,128)(2,1)S(1)}, bf16[128,2048]{1,0:T(8,128)(2,1)S(1)}, u32[]{:S(2)}, u32[]{:S(2)}) collective-permute-start(bf16[128,2048]{1,0:T(8,128)(2,1)S(1)} %get-tuple-element.34), channel_id=1, source_target_pairs={{0,1},{1,0},{2,3},{3,2},{4,5},{5,4},{6,7},{7,6},{8,9},{9,8},{10,11... | collective-permute-start | bytes 1572872 | tf_op jit(solution)/shard_map/ppermute | solution.py:421

commit v7 on v6

--- a/solution.py
+++ b/solution.py
@@ -17,7 +17,7 @@
 HIDE = -1e30
 
 
-def pack_kernel(n, blocks, pool_local, lists, slots_ref, len_ref, pool_ref, rope_ref, outs, where_ref,
+def pack_kernel(n, blocks, pool_local, lists, slots_ref, pool_ref, rope_ref, outs, where_ref,
                 index_ref, count_ref, lat_sem, rope_sem):
     me = lax.axis_index("req")
     sub = lax.axis_index("sub")
@@ -26,7 +26,6 @@
     for i in range(n * CAP):
         index_ref[i] = 0
         where_ref[i] = -1
-    where_ref[n * CAP] = len_ref[0]
     for i in range(n):
         count_ref[i] = 0
     for k in range(n):
@@ -68,7 +67,7 @@
         copy.wait()
 
 
-def pack(n, lists, block_slot, prefix_len, pool_latent, rope_turned):
+def pack(n, lists, block_slot, pool_latent, rope_turned):
     pool_local, block, width = pool_latent.shape
     blocks = lists[0].shape[1]
     rows = CAP * block + block * ROPE // width
@@ -77,15 +76,15 @@
 
     def body(*refs):
         pack_kernel(
-            n, blocks, pool_local, refs[:n], *refs[n : n + 4],
-            refs[n + 4 : 2 * n + 4], *refs[2 * n + 4 :],
+            n, blocks, pool_local, refs[:n], *refs[n : n + 3],
+            refs[n + 3 : 2 * n + 3], *refs[2 * n + 3 :],
         )
 
     out = pl.pallas_call(
         body,
         out_shape=[jax.ShapeDtypeStruct((rows, width), jnp.bfloat16)] * n
-        + [jax.ShapeDtypeStruct((n * CAP + 1,), jnp.int32)],
-        in_specs=[smem] * (n + 2) + [pl.BlockSpec(memory_space=pl.ANY)] * 2,
+        + [jax.ShapeDtypeStruct((n * CAP,), jnp.int32)],
+        in_specs=[smem] * (n + 1) + [pl.BlockSpec(memory_space=pl.ANY)] * 2,
         out_specs=[vmem] * n + [smem],
         scratch_shapes=[
             pltpu.SMEM((n * CAP,), jnp.int32),
@@ -96,65 +95,70 @@
         compiler_params=pltpu.CompilerParams(vmem_limit_bytes=16 << 20),
         cost_estimate=pl.CostEstimate(flops=0, bytes_accessed=4 * n * rows * width, transcendentals=0),
         name="pack",
-    )(*lists, block_slot, prefix_len, pool_latent, rope_turned)
+    )(*lists, block_slot, pool_latent, rope_turned)
     return out[:n], out[n]
 
 
-def prepare_kernel(len_ref, lat_ref, qn_ref, qr_ref, rope_ref, wk_ref, wv_ref,
-                   out_ref, qn_out, qr_out, wk_out, wv_out, kept_ref, sem):
-    kept_ref[0] = len_ref[0]
-    sub = lax.axis_index("sub")
-    latent = lat_ref.shape[1]
-    tail = out_ref.shape[1] - rope_ref.shape[1]
-
-    def part(ref, which):
-        half = ref.shape[1] // 2
-        return ref.at[:, pl.ds(pl.multiple_of(which * half, LANES), half)]
-
-    half = qn_out.shape[1]
-    rope_half = qr_out.shape[1]
-    moves = [
-        (lat_ref, out_ref.at[:, pl.ds(0, latent)]),
-        (part(qn_ref, 1 - sub), out_ref.at[:, pl.ds(latent, half)]),
-        (part(qr_ref, 1 - sub), out_ref.at[:, pl.ds(latent + half, rope_half)]),
-        (rope_ref, out_ref.at[pl.ds(0, ROPE), pl.ds(tail, rope_ref.shape[1])]),
-        (part(qn_ref, sub), qn_out),
-        (part(qr_ref, sub), qr_out),
-        (part(wk_ref, sub), wk_out),
-        (part(wv_ref, sub), wv_out),
-    ]
-    copies = [pltpu.make_async_copy(*move, sem.at[i]) for i, move in enumerate(moves)]
+def half_of(ref, which):
+    half = ref.shape[1] // 2
+    return ref.at[:, pl.ds(pl.multiple_of(which * half, LANES), half)]
+
+
+def move(moves, sem):
+    copies = [pltpu.make_async_copy(*pair, sem.at[i]) for i, pair in enumerate(moves)]
     for copy in copies:
         copy.start()
     for copy in copies:
         copy.wait()
 
 
-def prepare(prefix_len, new_latent, q_nope, q_rope, rope_turned, w_uk, w_uv):
-    rows, latent = new_latent.shape
-    half = q_nope.shape[1] // 2
-    rope_half = q_rope.shape[1] // 2
-    shapes = [
-        (rows, latent + half + rope_half + rows),
-        (rows, half),
-        (rows, rope_half),
-        (latent, half),
-        (latent, half),
-    ]
+def prepare_kernel(lat_ref, qn_ref, qr_ref, rope_ref, out_ref, sem):
+    there = 1 - lax.axis_index("sub")
+    latent = lat_ref.shape[1]
+    half = qn_ref.shape[1] // 2
+    rope_half = qr_ref.shape[1] // 2
+    tail = latent + half + rope_half
+    move(
+        [
+            (lat_ref, out_ref.at[:, pl.ds(0, latent)]),
+            (half_of(qn_ref, there), out_ref.at[:, pl.ds(latent, half)]),
+            (half_of(qr_ref, there), out_ref.at[:, pl.ds(latent + half, rope_half)]),
+            (rope_ref, out_ref.at[pl.ds(0, ROPE), pl.ds(tail, rope_ref.shape[1])]),
+        ],
+        sem,
+    )
+
+
+def load_kernel(*refs):
+    sub = lax.axis_index("sub")
+    *refs, sem = refs
+    count = len(refs) // 2
+    move([(half_of(a, sub), b) for a, b in zip(refs[:count], refs[count:])], sem)
+
+
+def gather_call(kernel, args, shapes):
     return pl.pallas_call(
-        prepare_kernel,
-        out_shape=[jax.ShapeDtypeStruct(shape, jnp.bfloat16) for shape in shapes]
-        + [jax.ShapeDtypeStruct((1,), jnp.int32)],
-        in_specs=[pl.BlockSpec(memory_space=pltpu.SMEM)] + [pl.BlockSpec(memory_space=pl.ANY)] * 6,
-        out_specs=[pl.BlockSpec(memory_space=pltpu.VMEM)] * 5
-        + [pl.BlockSpec(memory_space=pltpu.SMEM)],
-        scratch_shapes=[pltpu.SemaphoreType.DMA((8,))],
+        kernel,
+        out_shape=[jax.ShapeDtypeStruct(shape, jnp.bfloat16) for shape in shapes],
+        in_specs=[pl.BlockSpec(memory_space=pl.ANY)] * len(args),
+        out_specs=[pl.BlockSpec(memory_space=pltpu.VMEM)] * len(shapes),
+        scratch_shapes=[pltpu.SemaphoreType.DMA((len(args),))],
         compiler_params=pltpu.CompilerParams(vmem_limit_bytes=16 << 20),
         cost_estimate=pl.CostEstimate(
             flops=0, bytes_accessed=4 * sum(math.prod(shape) for shape in shapes), transcendentals=0
         ),
-        name="prepare",
-    )(prefix_len, new_latent, q_nope, q_rope, rope_turned, w_uk, w_uv)
+    )(*args)
+
+
+def prepare(new_latent, q_nope, q_rope, rope_turned):
+    rows, latent = new_latent.shape
+    width = latent + q_nope.shape[1] // 2 + q_rope.shape[1] // 2 + rows
+    args = (new_latent, q_nope, q_rope, rope_turned)
+    return gather_call(prepare_kernel, args, [(rows, width)])[0]
+
+
+def load(*args):
+    return gather_call(load_kernel, args, [(a.shape[0], a.shape[1] // 2) for a in args])
 
 
 RATE = math.log2(math.e) / math.sqrt(NOPE + ROPE)
@@ -162,7 +166,7 @@
 
 def attend_kernel(steps, fresh, *refs):
     count = len(steps)
-    where_ref, lat_a, rope_a, other, qn_ref, qr_ref, wk_ref, wv_ref, *refs = refs
+    where_ref, len_ref, lat_a, rope_a, other, qn_ref, qr_ref, wk_ref, wv_ref, *refs = refs
     mine = refs[:count]
     theirs = refs[count : 2 * count]
     refs = refs[2 * count :]
@@ -192,7 +196,7 @@
 
         lane = lax.broadcasted_iota(jnp.int32, (block, ROPE), 1)
         row = lax.broadcasted_iota(jnp.int32, (block, ROPE), 0)
-        length = where_ref[where_ref.shape[0] - 1]
+        length = jnp.broadcast_to(len_ref[:1, :ROPE], (block, ROPE)) + lane
         vt[:, :, VDIM:, :] = jnp.ones((2, 2, 16, keys), jnp.bfloat16)
         for i, k in enumerate(steps):
             width = mine[i].shape[1]
@@ -330,13 +334,13 @@
             deliver(t).wait()
 
 
-def attend(steps, where, mine, theirs, new_latent, rope_turned, other, qn, qr, wk, wv, state):
+def attend(steps, where, length, mine, theirs, new_latent, rope_turned, other, qn, qr, wk, wv, state):
     fresh = state is None
     block, latent = new_latent.shape
     heads = wk.shape[1] // NOPE
     keys = (len(steps) + (1 if fresh else 0)) * CAP * block
     vmem = pl.BlockSpec(memory_space=pltpu.VMEM)
-    args = [where, new_latent, rope_turned, other, qn, qr, wk, wv, *mine, *theirs]
+    args = [where, length, new_latent, rope_turned, other, qn, qr, wk, wv, *mine, *theirs]
     specs = [pl.BlockSpec(memory_space=pltpu.SMEM)] + [vmem] * (len(args) - 1)
     scratch = [
         pltpu.VMEM((keys, latent), jnp.bfloat16),
@@ -431,21 +435,21 @@
     for k in far:
         got[k] = cross(block_list, k)
     lists = [keep(block_list)] + [got[k] for k in range(1, n)]
-    other, qn, qr, wk, wv, length = prepare(
-        prefix_len, new_latent, q_nope, q_rope, rope_turned, w_uk, w_uv
-    )
+    other = prepare(new_latent, q_nope, q_rope, rope_turned)
     other = swap(other)
-    sent, where = pack(n, lists, slots, length, pool_latent, pool_turned)
+    sent, where = pack(n, lists, slots, pool_latent, pool_turned)
     local = swap(sent[0])
+    length = prefix_len - lax.broadcasted_iota(jnp.int32, (8, LANES), 1)
     mine = []
     for k in far:
         mine.append(cross(sent[k], k))
     theirs = []
     for k, a in zip(far, mine):
         theirs.append(swap(a))
-    common = (new_latent, rope_turned, other, qn, qr, wk, wv)
-    state = attend([0], where, [sent[0]], [local], *common, None)
-    kept, gone = attend(far, where, mine, theirs, *common, state)
+    loaded = load(q_nope, q_rope, w_uk, w_uv)
+    common = (new_latent, rope_turned, other, *loaded)
+    state = attend([0], where, length, [sent[0]], [local], *common, None)
+    kept, gone = attend(far, where, length, mine, theirs, *common, state)
     back = swap(gone)
     return join(kept, back)
 

time: 51.7 us -> 48.2 us (0.932)
  waiting for transfers between devices: 15.6 us -> 12.4 us
    ppermute x6, waiting for transfers between devices: 13.7 us -> 10.5 us  [shards(): cross = lambda a, k: lax.ppermute(a, 'req', [(i, i ^ k) for i in range(n)])]
    pallas_call x1, Pallas kernels: 3.37 us -> 2.72 us  [pack(): pl.pallas_call(body, out_shape=[jax.ShapeDtypeStruct((rows, width), jnp.b...]
    pallas_call x1 -> x2, Pallas kernels: 3.39 us -> 3.75 us  [gather_call(): pl.pallas_call(kernel, out_shape=[jax.ShapeDtypeStruct(shape, jnp.bfloat1...]
  transfers between devices with their start and end apart: 12 -> 12, of which waited for: 5 -> 5; matrix products, arithmetic and copies ran while one was open for 0% -> 0% of each run, Pallas kernels for 20% -> 25%
where the time goes in v7:
time: 48.2 us; the launch traced here: 48 us
  Pallas kernels  24 us (50%)
  waiting for transfers between devices  12.4 us (26%)
  starting transfers between devices  10.8 us (22%)
  between operations  0.74 us (2%)
    pallas_call x2, Pallas kernels, attend(): pl.pallas_call(functools.partial(attend_kernel, steps, fresh), in_specs=s...  16.7 us
    ppermute x6, waiting for transfers between devices, shards(): cross = lambda a, k: lax.ppermute(a, 'req', [(i, i ^ k) for i in range(n)])  10.5 us
    ppermute x6, starting transfers between devices, shards(): cross = lambda a, k: lax.ppermute(a, 'req', [(i, i ^ k) for i in range(n)])  9.68 us
    pallas_call x2, Pallas kernels, gather_call(): pl.pallas_call(kernel, out_shape=[jax.ShapeDtypeStruct(shape, jnp.bfloat1...  3.75 us
    pallas_call x1, Pallas kernels, pack(): pl.pallas_call(body, out_shape=[jax.ShapeDtypeStruct((rows, width), jnp.b...  2.72 us
    ppermute x6, waiting for transfers between devices, shards(): swap = lambda a: lax.ppermute(a, 'sub', [(0, 1), (1, 0)])  1.9 us
    ppermute x6, starting transfers between devices, shards(): swap = lambda a: lax.ppermute(a, 'sub', [(0, 1), (1, 0)])  1.16 us
  transfers between devices with their start and end apart: 12, of which 5 were waited for; matrix products, arithmetic and copies ran while one was open for 0% of the time, Pallas kernels for 25%

profile of v7, /device:TPU:0, one launch (start us, length us, event | category | flops | bytes accessed | tf_op | source)
XLA Modules:
  0.0 48.0 jit_solution(9415076691362399915)
XLA Ops:
  0.0 1.2 %shard_map.109 = bf16[128,3712]{1,0:T(8,128)(2,1)S(1)} custom-call(bf16[128,512]{1,0:T(8,128)(2,1)} %refs_2_.5, bf16[128,4096]{1,0:T(8,128)(2,1)} %refs_0_.3, bf16[128,2048]{1,0:T(8,128)(2,1)} %refs_1_.1, bf16[64,128]{1,0:T(8,128)(2,1)} %bitcast.5), custom_call_target="tpu_custom_call" | custom-call | bytes 1900544 | tf_op jit(solution)/shard_map/pallas_call | solution.py:140
  1.2 0.6 %collective-permute-start.3 = (bf16[128,3712]{1,0:T(8,128)(2,1)S(1)}, bf16[128,3712]{1,0:T(8,128)(2,1)S(1)}, u32[]{:S(2)}, u32[]{:S(2)}) collective-permute-start(bf16[128,3712]{1,0:T(8,128)(2,1)S(1)} %shard_map.109), channel_id=1, source_target_pairs={{0,1},{1,0},{2,3},{3,2},{4,5},{5,4},{6,7},{7,6},{8,9},{9,8},{10,11... | collective-permute-start | bytes 2850824 | tf_op jit(solution)/shard_map/ppermute | solution.py:425
  1.8 3.7 %collective-permute-start.1 = (s32[1,6]{1,0:T(1,128)S(1)}, s32[1,6]{1,0:T(1,128)S(1)}, u32[]{:S(2)}, u32[]{:S(2)}) collective-permute-start(s32[1,6]{1,0:T(1,128)S(1)} %copy-done), channel_id=1, source_target_pairs={{0,8},{4,12},{8,0},{12,4},{1,9},{5,13},{9,1},{13,5},{2,10},{6,14},... | collective-permute-start | bytes 80 | tf_op jit(solution)/shard_map/ppermute | solution.py:426
  5.5 1.6 %collective-permute-start = (s32[1,6]{1,0:T(1,128)S(1)}, s32[1,6]{1,0:T(1,128)S(1)}, u32[]{:S(2)}, u32[]{:S(2)}) collective-permute-start(s32[1,6]{1,0:T(1,128)S(1)} %copy-done), channel_id=1, source_target_pairs={{0,4},{4,0},{8,12},{12,8},{1,5},{5,1},{9,13},{13,9},{2,6},{6,2},{1... | collective-permute-start | bytes 80 | tf_op jit(solution)/shard_map/ppermute | solution.py:426
  7.0 2.0 %collective-permute-done.refs_1_ = s32[1,6]{1,0:T(1,128)S(1)} collective-permute-done((s32[1,6]{1,0:T(1,128)S(1)}, s32[1,6]{1,0:T(1,128)S(1)}, u32[]{:S(2)}, u32[]{:S(2)}) %collective-permute-start) | collective-permute-done | bytes 56 | tf_op jit(solution)/shard_map/ppermute | solution.py:426
  9.0 3.4 %collective-permute-done.2.refs_3_ = s32[1,6]{1,0:T(1,128)S(1)} collective-permute-done((s32[1,6]{1,0:T(1,128)S(1)}, s32[1,6]{1,0:T(1,128)S(1)}, u32[]{:S(2)}, u32[]{:S(2)}) %collective-permute-start.2) | collective-permute-done | bytes 56 | tf_op jit(solution)/shard_map/ppermute | solution.py:426
  12.4 2.7 %pack.1 = (bf16[288,256]{1,0:T(8,128)(2,1)S(1)}, bf16[288,256]{1,0:T(8,128)(2,1)S(1)}, bf16[288,256]{1,0:T(8,128)(2,1)S(1)}, bf16[288,256]{1,0:T(8,128)(2,1)S(1)}, s32[8]{0:T(128)S(1)}) custom-call(s32[1,6]{1,0:T(1,128)} %refs_0_.2, s32[1,6]{1,0:T(1,128)S(1)} %collective-permute-done.refs_1_, s32[1,6]{1,0:T(1,128)S(1)} %collective-permute-done.1.refs_2_, ...), custom_call_target="tpu_custom_call" | custom-call | bytes 1179648 | tf_op jit(solution)/shard_map/pack/pallas_call | solution.py:83
  15.1 0.1 collective-permute-start.4
  15.2 0.1 collective-permute-start.5
  15.3 4.3 %collective-permute-start.6 = (bf16[288,256]{1,0:T(8,128)(2,1)S(1)}, bf16[288,256]{1,0:T(8,128)(2,1)S(1)}, u32[]{:S(2)}, u32[]{:S(2)}) collective-permute-start(bf16[288,256]{1,0:T(8,128)(2,1)S(1)} %get-tuple-element.25), channel_id=1, source_target_pairs={{0,4},{4,0},{8,12},{12,8},{1,5},{5,1},{9,13},{13,9},{2,6},{6,2},{1... | collective-permute-start | bytes 442376 | tf_op jit(solution)/shard_map/ppermute | solution.py:426
  20.2 2.5 %shard_map.110 = (bf16[128,2048]{1,0:T(8,128)(2,1)S(1)}, bf16[128,1024]{1,0:T(8,128)(2,1)S(1)}, bf16[512,2048]{1,0:T(8,128)(2,1)S(1)}, bf16[512,2048]{1,0:T(8,128)(2,1)S(1)}) custom-call(bf16[128,4096]{1,0:T(8,128)(2,1)} %refs_0_.3, bf16[128,2048]{1,0:T(8,128)(2,1)} %refs_1_.1, bf16[512,4096]{1,0:T(8,128)(2,1)} %refs_2_.3, bf16[512,4096]{1,0:T(8,128)(2,1)} %refs_3_.1), custom_call_target="tpu_custom_call" | custom-call | bytes 9961472 | tf_op jit(solution)/shard_map/pallas_call | solution.py:140
  22.8 0.9 %collective-permute-done.4.refs_9_ = bf16[288,256]{1,0:T(8,128)(2,1)S(1)} collective-permute-done((bf16[288,256]{1,0:T(8,128)(2,1)S(1)}, bf16[288,256]{1,0:T(8,128)(2,1)S(1)}, u32[]{:S(2)}, u32[]{:S(2)}) %collective-permute-start.4) | collective-permute-done | bytes 147488 | tf_op jit(solution)/shard_map/ppermute | solution.py:426
  23.7 4.2 %collective-permute-done.5.refs_10_ = bf16[288,256]{1,0:T(8,128)(2,1)S(1)} collective-permute-done((bf16[288,256]{1,0:T(8,128)(2,1)S(1)}, bf16[288,256]{1,0:T(8,128)(2,1)S(1)}, u32[]{:S(2)}, u32[]{:S(2)}) %collective-permute-start.5) | collective-permute-done | bytes 147488 | tf_op jit(solution)/shard_map/ppermute | solution.py:426
  27.9 0.0 collective-permute-start.8
  27.9 0.0 collective-permute-done.6.refs_11_
  27.9 0.5 %collective-permute-start.9 = (bf16[288,256]{1,0:T(8,128)(2,1)S(1)}, bf16[288,256]{1,0:T(8,128)(2,1)S(1)}, u32[]{:S(2)}, u32[]{:S(2)}) collective-permute-start(bf16[288,256]{1,0:T(8,128)(2,1)S(1)} %collective-permute-done.6.refs_11_), channel_id=1, source_target_pairs={{0,1},{1,0},{2,3},{3,2},{4,5},{5,4},{6,7},{7,6},{8,9},{9,8},{10,11... | collective-permute-start | bytes 442376 | tf_op jit(solution)/shard_map/ppermute | solution.py:425
  28.4 0.0 collective-permute-done.10.refs_10_
  28.4 0.0 collective-permute-done.3.refs_4_
  28.4 6.8 %attend_new.1 = (f32[2048,256]{1,0:T(8,128)S(1)}, f32[128,256]{1,0:T(8,128)S(1)}) custom-call(s32[8]{0:T(128)S(1)} %get-tuple-element.18.refs_0_, s32[8,128]{1,0:T(8,128)S(1)} %iota.7.refs_1_, bf16[128,512]{1,0:T(8,128)(2,1)} %refs_2_.5, bf16[64,128]{1,0:T(8,128)(2,1)} %bitcast.6, bf16[128,3712]{1,0:T(8,128)(2,1)S(1)} %collective-permute-done.3.refs_4_, ...), custom_call_target="tpu_custom_call" | custom-call | flops 4294967296 | bytes 8388608 | tf_op jit(solution)/shard_map/attend_new/pallas_call | solution.py:372
  35.2 0.0 collective-permute-done.8.refs_13_
  35.3 9.9 %attend_prefix.1 = (bf16[128,4096]{1,0:T(8,128)(2,1)}, bf16[128,2048]{1,0:T(8,128)(2,1)S(1)}) custom-call(s32[8]{0:T(128)S(1)} %get-tuple-element.18.refs_0_, s32[8,128]{1,0:T(8,128)S(1)} %iota.7.refs_1_, bf16[128,512]{1,0:T(8,128)(2,1)} %refs_2_.5, bf16[64,128]{1,0:T(8,128)(2,1)} %bitcast.7, bf16[128,3712]{1,0:T(8,128)(2,1)S(1)} %collective-permute-done.3.refs_4_, ...), custom_call_target="tpu_custom_call" | custom-call | flops 6442450944 | bytes 8388608 | tf_op jit(solution)/shard_map/attend_prefix/pallas_call | solution.py:372
  45.2 0.1 collective-permute-start.11
  45.3 1.9 %collective-permute-done.11.back_ref = bf16[128,2048]{1,0:T(8,128)(2,1)S(1)} collective-permute-done((bf16[128,2048]{1,0:T(8,128)(2,1)S(1)}, bf16[128,2048]{1,0:T(8,128)(2,1)S(1)}, u32[]{:S(2)}, u32[]{:S(2)}) %collective-permute-start.11) | collective-permute-done | bytes 524320 | tf_op jit(solution)/shard_map/ppermute | solution.py:425
  47.2 0.8 %join.1 = bf16[128,4096]{1,0:T(8,128)(2,1)} custom-call(bf16[128,4096]{1,0:T(8,128)(2,1)} %get-tuple-element.29.kept_ref, bf16[128,2048]{1,0:T(8,128)(2,1)S(1)} %collective-permute-done.11.back_ref), custom_call_target="tpu_custom_call", output_to_operand_aliasing={{}: (0, {})} | custom-call | tf_op jit(solution)/shard_map/join/pallas_call | solution.py:399
  (10 shorter events, 0.0 us)
Async XLA Ops:
  0.0 1.8 %copy-start = (s32[1,6]{1,0:T(1,128)S(1)}, s32[1,6]{1,0:T(1,128)}, u32[]{:S(2)}) copy-start(s32[1,6]{1,0:T(1,128)} %refs_0_.2) | copy-start | bytes 76
  1.2 27.2 %collective-permute-start.3 = (bf16[128,3712]{1,0:T(8,128)(2,1)S(1)}, bf16[128,3712]{1,0:T(8,128)(2,1)S(1)}, u32[]{:S(2)}, u32[]{:S(2)}) collective-permute-start(bf16[128,3712]{1,0:T(8,128)(2,1)S(1)} %shard_map.109), channel_id=1, source_target_pairs={{0,1},{1,0},{2,3},{3,2},{4,5},{5,4},{6,7},{7,6},{8,9},{9,8},{10,11... | collective-permute-start | bytes 2850824 | tf_op jit(solution)/shard_map/ppermute | solution.py:425
  1.8 5.2 %collective-permute-start.1 = (s32[1,6]{1,0:T(1,128)S(1)}, s32[1,6]{1,0:T(1,128)S(1)}, u32[]{:S(2)}, u32[]{:S(2)}) collective-permute-start(s32[1,6]{1,0:T(1,128)S(1)} %copy-done), channel_id=1, source_target_pairs={{0,8},{4,12},{8,0},{12,4},{1,9},{5,13},{9,1},{13,5},{2,10},{6,14},... | collective-permute-start | bytes 80 | tf_op jit(solution)/shard_map/ppermute | solution.py:426
  5.5 3.6 %collective-permute-start = (s32[1,6]{1,0:T(1,128)S(1)}, s32[1,6]{1,0:T(1,128)S(1)}, u32[]{:S(2)}, u32[]{:S(2)}) collective-permute-start(s32[1,6]{1,0:T(1,128)S(1)} %copy-done), channel_id=1, source_target_pairs={{0,4},{4,0},{8,12},{12,8},{1,5},{5,1},{9,13},{13,9},{2,6},{6,2},{1... | collective-permute-start | bytes 80 | tf_op jit(solution)/shard_map/ppermute | solution.py:426
  7.0 5.4 %collective-permute-start.2 = (s32[1,6]{1,0:T(1,128)S(1)}, s32[1,6]{1,0:T(1,128)S(1)}, u32[]{:S(2)}, u32[]{:S(2)}) collective-permute-start(s32[1,6]{1,0:T(1,128)S(1)} %copy-done), channel_id=1, source_target_pairs={{0,12},{4,8},{8,4},{12,0},{1,13},{5,9},{9,5},{13,1},{2,14},{6,10},... | collective-permute-start | bytes 80 | tf_op jit(solution)/shard_map/ppermute | solution.py:426
  15.1 8.6 %collective-permute-start.4 = (bf16[288,256]{1,0:T(8,128)(2,1)S(1)}, bf16[288,256]{1,0:T(8,128)(2,1)S(1)}, u32[]{:S(2)}, u32[]{:S(2)}) collective-permute-start(bf16[288,256]{1,0:T(8,128)(2,1)S(1)} %get-tuple-element.23), channel_id=1, source_target_pairs={{0,12},{4,8},{8,4},{12,0},{1,13},{5,9},{9,5},{13,1},{2,14},{6,10},... | collective-permute-start | bytes 442376 | tf_op jit(solution)/shard_map/ppermute | solution.py:426
  15.2 12.7 %collective-permute-start.5 = (bf16[288,256]{1,0:T(8,128)(2,1)S(1)}, bf16[288,256]{1,0:T(8,128)(2,1)S(1)}, u32[]{:S(2)}, u32[]{:S(2)}) collective-permute-start(bf16[288,256]{1,0:T(8,128)(2,1)S(1)} %get-tuple-element.24), channel_id=1, source_target_pairs={{0,8},{4,12},{8,0},{12,4},{1,9},{5,13},{9,1},{13,5},{2,10},{6,14},... | collective-permute-start | bytes 442376 | tf_op jit(solution)/shard_map/ppermute | solution.py:426
  15.3 12.6 %collective-permute-start.6 = (bf16[288,256]{1,0:T(8,128)(2,1)S(1)}, bf16[288,256]{1,0:T(8,128)(2,1)S(1)}, u32[]{:S(2)}, u32[]{:S(2)}) collective-permute-start(bf16[288,256]{1,0:T(8,128)(2,1)S(1)} %get-tuple-element.25), channel_id=1, source_target_pairs={{0,4},{4,0},{8,12},{12,8},{1,5},{5,1},{9,13},{13,9},{2,6},{6,2},{1... | collective-permute-start | bytes 442376 | tf_op jit(solution)/shard_map/ppermute | solution.py:426
  19.6 8.8 %collective-permute-start.10 = (bf16[288,256]{1,0:T(8,128)(2,1)S(1)}, bf16[288,256]{1,0:T(8,128)(2,1)S(1)}, u32[]{:S(2)}, u32[]{:S(2)}) collective-permute-start(bf16[288,256]{1,0:T(8,128)(2,1)S(1)} %get-tuple-element.26.refs_9_), channel_id=1, source_target_pairs={{0,1},{1,0},{2,3},{3,2},{4,5},{5,4},{6,7},{7,6},{8,9},{9,8},{10,11... | collective-permute-start | bytes 442376 | tf_op jit(solution)/shard_map/ppermute | solution.py:425
  23.7 11.5 %collective-permute-start.7 = (bf16[288,256]{1,0:T(8,128)(2,1)S(1)}, bf16[288,256]{1,0:T(8,128)(2,1)S(1)}, u32[]{:S(2)}, u32[]{:S(2)}) collective-permute-start(bf16[288,256]{1,0:T(8,128)(2,1)S(1)} %collective-permute-done.4.refs_9_), channel_id=1, source_target_pairs={{0,1},{1,0},{2,3},{3,2},{4,5},{5,4},{6,7},{7,6},{8,9},{9,8},{10,11... | collective-permute-start | bytes 442376 | tf_op jit(solution)/shard_map/ppermute | solution.py:425
  27.9 7.3 %collective-permute-start.8 = (bf16[288,256]{1,0:T(8,128)(2,1)S(1)}, bf16[288,256]{1,0:T(8,128)(2,1)S(1)}, u32[]{:S(2)}, u32[]{:S(2)}) collective-permute-start(bf16[288,256]{1,0:T(8,128)(2,1)S(1)} %collective-permute-done.5.refs_10_), channel_id=1, source_target_pairs={{0,1},{1,0},{2,3},{3,2},{4,5},{5,4},{6,7},{7,6},{8,9},{9,8},{10,11... | collective-permute-start | bytes 442376 | tf_op jit(solution)/shard_map/ppermute | solution.py:425
  27.9 7.3 %collective-permute-start.9 = (bf16[288,256]{1,0:T(8,128)(2,1)S(1)}, bf16[288,256]{1,0:T(8,128)(2,1)S(1)}, u32[]{:S(2)}, u32[]{:S(2)}) collective-permute-start(bf16[288,256]{1,0:T(8,128)(2,1)S(1)} %collective-permute-done.6.refs_11_), channel_id=1, source_target_pairs={{0,1},{1,0},{2,3},{3,2},{4,5},{5,4},{6,7},{7,6},{8,9},{9,8},{10,11... | collective-permute-start | bytes 442376 | tf_op jit(solution)/shard_map/ppermute | solution.py:425
  45.2 2.0 %collective-permute-start.11 = (bf16[128,2048]{1,0:T(8,128)(2,1)S(1)}, bf16[128,2048]{1,0:T(8,128)(2,1)S(1)}, u32[]{:S(2)}, u32[]{:S(2)}) collective-permute-start(bf16[128,2048]{1,0:T(8,128)(2,1)S(1)} %get-tuple-element.30), channel_id=1, source_target_pairs={{0,1},{1,0},{2,3},{3,2},{4,5},{5,4},{6,7},{7,6},{8,9},{9,8},{10,11... | collective-permute-start | bytes 1572872 | tf_op jit(solution)/shard_map/ppermute | solution.py:425

commit v8 on v7

--- a/solution.py
+++ b/solution.py
@@ -112,7 +112,8 @@
         copy.wait()
 
 
-def prepare_kernel(lat_ref, qn_ref, qr_ref, rope_ref, out_ref, sem):
+def prepare_kernel(lat_ref, qn_ref, qr_ref, rope_ref, pool_ref, pool_rope_ref,
+                   out_ref, pool_out, pool_rope_out, sem):
     there = 1 - lax.axis_index("sub")
     latent = lat_ref.shape[1]
     half = qn_ref.shape[1] // 2
@@ -124,6 +125,8 @@
             (half_of(qn_ref, there), out_ref.at[:, pl.ds(latent, half)]),
             (half_of(qr_ref, there), out_ref.at[:, pl.ds(latent + half, rope_half)]),
             (rope_ref, out_ref.at[pl.ds(0, ROPE), pl.ds(tail, rope_ref.shape[1])]),
+            (pool_ref, pool_out),
+            (pool_rope_ref, pool_rope_out),
         ],
         sem,
     )
@@ -150,11 +153,12 @@
     )(*args)
 
 
-def prepare(new_latent, q_nope, q_rope, rope_turned):
+def prepare(new_latent, q_nope, q_rope, rope_turned, pool_latent, pool_turned):
     rows, latent = new_latent.shape
     width = latent + q_nope.shape[1] // 2 + q_rope.shape[1] // 2 + rows
-    args = (new_latent, q_nope, q_rope, rope_turned)
-    return gather_call(prepare_kernel, args, [(rows, width)])[0]
+    args = (new_latent, q_nope, q_rope, rope_turned, pool_latent, pool_turned)
+    shapes = [(rows, width), pool_latent.shape, pool_turned.shape]
+    return gather_call(prepare_kernel, args, shapes)
 
 
 def load(*args):
@@ -171,9 +175,9 @@
     theirs = refs[count : 2 * count]
     refs = refs[2 * count :]
     if fresh:
-        acc_ref, stat_ref, lat, kc, vt, score, weight, peak, bias = refs
+        acc_ref, stat_ref, lat, kc, vt, score, weight, peak, norms, bias = refs
     else:
-        (acc_ref, stat_ref, out_ref, send_ref, lat, kc, vt, score, weight, peak, result,
+        (acc_ref, stat_ref, out_ref, send_ref, lat, kc, vt, score, weight, peak, norms, result,
          sem) = refs
     sub = lax.axis_index("sub")
     block, latent = lat_a.shape
@@ -197,7 +201,6 @@
         lane = lax.broadcasted_iota(jnp.int32, (block, ROPE), 1)
         row = lax.broadcasted_iota(jnp.int32, (block, ROPE), 0)
         length = jnp.broadcast_to(len_ref[:1, :ROPE], (block, ROPE)) + lane
-        vt[:, :, VDIM:, :] = jnp.ones((2, 2, 16, keys), jnp.bfloat16)
         for i, k in enumerate(steps):
             width = mine[i].shape[1]
             here = pl.multiple_of(sub * width, width)
@@ -241,7 +244,7 @@
             preferred_element_type=jnp.float32,
         )
         for j in range(2):
-            vt[slot, j, :VDIM, :] = v2[j * VDIM : (j + 1) * VDIM].astype(jnp.bfloat16)
+            vt[slot, j] = v2[j * VDIM : (j + 1) * VDIM].astype(jnp.bfloat16)
 
     def form_scores(pair, slot, j):
         lane = lax.broadcasted_iota(jnp.int32, (queries, LANES), 1)
@@ -269,11 +272,13 @@
         most = peak[slot, j, :1, :]
         if not fresh:
             most = jnp.maximum(most, stat_ref[at((2 * pair + j) * 8, 8), :][:1])
-        weight[slot, j] = jnp.exp2((score[slot, j] - most) * RATE).astype(jnp.bfloat16)
+        e = jnp.exp2((score[slot, j] - most) * RATE)
+        norms[slot, j] = jnp.broadcast_to(jnp.sum(e, axis=0, keepdims=True), (8, queries))
+        weight[slot, j] = e.astype(jnp.bfloat16)
 
     def form_output(pair, slot, j):
         o = jnp.dot(vt[slot, j], weight[slot, j], preferred_element_type=jnp.float32)
-        o, norm = o[:VDIM], o[VDIM : VDIM + 1]
+        norm = norms[slot, j, :1, :]
         rows = at((2 * pair + j) * VDIM, VDIM)
         stat_rows = at((2 * pair + j) * 8, 8)
         if fresh:
@@ -299,9 +304,12 @@
             form_keys(pair + 1)
             form_values(pair + 1, 1 - slot)
         for j in range(2):
-            form_output(pair, slot, j)
+            if not fresh:
+                form_output(pair, slot, j)
             if more:
                 form_scores(pair + 1, 1 - slot, j)
+            if fresh:
+                form_output(pair, slot, j)
 
     def deliver(t):
         width = 4 * VDIM
@@ -345,9 +353,10 @@
     scratch = [
         pltpu.VMEM((keys, latent), jnp.bfloat16),
         pltpu.VMEM((2, keys, NOPE + LANES), jnp.bfloat16),
-        pltpu.VMEM((2, 2, VDIM + 16, keys), jnp.bfloat16),
+        pltpu.VMEM((2, 2, VDIM, keys), jnp.bfloat16),
         pltpu.VMEM((2, 2, keys, 2 * block), jnp.float32),
         pltpu.VMEM((2, 2, keys, 2 * block), jnp.bfloat16),
+        pltpu.VMEM((2, 2, 8, 2 * block), jnp.float32),
         pltpu.VMEM((2, 2, 8, 2 * block), jnp.float32),
     ]
     if fresh:
@@ -435,7 +444,9 @@
     for k in far:
         got[k] = cross(block_list, k)
     lists = [keep(block_list)] + [got[k] for k in range(1, n)]
-    other = prepare(new_latent, q_nope, q_rope, rope_turned)
+    other, pool_latent, pool_turned = prepare(
+        new_latent, q_nope, q_rope, rope_turned, pool_latent, pool_turned
+    )
     other = swap(other)
     sent, where = pack(n, lists, slots, pool_latent, pool_turned)
     local = swap(sent[0])

time: 48.2 us -> 47.9 us (level)
  transfers between devices with their start and end apart: 12 -> 12, of which waited for: 5 -> 5; matrix products, arithmetic and copies ran while one was open for 0% -> 0% of each run, Pallas kernels for 25% -> 24%
where the time goes in v8:
time: 47.9 us; the launch traced here: 47.7 us
  Pallas kernels  23.8 us (50%)
  waiting for transfers between devices  12.4 us (26%)
  starting transfers between devices  10.8 us (23%)
  between operations  0.74 us (2%)
    pallas_call x2, Pallas kernels, attend(): pl.pallas_call(functools.partial(attend_kernel, steps, fresh), in_specs=s...  16.4 us
    ppermute x6, waiting for transfers between devices, shards(): cross = lambda a, k: lax.ppermute(a, 'req', [(i, i ^ k) for i in range(n)])  10.5 us
    ppermute x6, starting transfers between devices, shards(): cross = lambda a, k: lax.ppermute(a, 'req', [(i, i ^ k) for i in range(n)])  9.68 us
    pallas_call x2, Pallas kernels, gather_call(): pl.pallas_call(kernel, out_shape=[jax.ShapeDtypeStruct(shape, jnp.bfloat1...  4.17 us
    pallas_call x1, Pallas kernels, pack(): pl.pallas_call(body, out_shape=[jax.ShapeDtypeStruct((rows, width), jnp.b...  2.4 us
    ppermute x6, waiting for transfers between devices, shards(): swap = lambda a: lax.ppermute(a, 'sub', [(0, 1), (1, 0)])  1.91 us
    ppermute x6, starting transfers between devices, shards(): swap = lambda a: lax.ppermute(a, 'sub', [(0, 1), (1, 0)])  1.16 us
  transfers between devices with their start and end apart: 12, of which 5 were waited for; matrix products, arithmetic and copies ran while one was open for 0% of the time, Pallas kernels for 24%

profile of v8, /device:TPU:0, one launch (start us, length us, event | category | flops | bytes accessed | tf_op | source)
XLA Modules:
  0.0 47.7 jit_solution(4951193611841142962)
XLA Ops:
  0.0 1.6 %shard_map.109 = (bf16[128,3712]{1,0:T(8,128)(2,1)S(1)}, bf16[16,128,256]{2,1,0:T(8,128)(2,1)S(1)}, bf16[16,64,128]{2,1,0:T(8,128)(2,1)S(1)}) custom-call(bf16[128,512]{1,0:T(8,128)(2,1)} %refs_2_.5, bf16[128,4096]{1,0:T(8,128)(2,1)} %refs_0_.3, bf16[128,2048]{1,0:T(8,128)(2,1)} %refs_1_.1, bf16[64,128]{1,0:T(8,128)(2,1)} %bitcast.5, ...), custom_call_target="tpu_custom_call" | custom-call | bytes 4521984 | tf_op jit(solution)/shard_map/pallas_call | solution.py:143
  1.7 0.6 %collective-permute-start.3 = (bf16[128,3712]{1,0:T(8,128)(2,1)S(1)}, bf16[128,3712]{1,0:T(8,128)(2,1)S(1)}, u32[]{:S(2)}, u32[]{:S(2)}) collective-permute-start(bf16[128,3712]{1,0:T(8,128)(2,1)S(1)} %get-tuple-element.24), channel_id=1, source_target_pairs={{0,1},{1,0},{2,3},{3,2},{4,5},{5,4},{6,7},{7,6},{8,9},{9,8},{10,11... | collective-permute-start | bytes 2850824 | tf_op jit(solution)/shard_map/ppermute | solution.py:434
  2.2 3.7 %collective-permute-start.1 = (s32[1,6]{1,0:T(1,128)S(1)}, s32[1,6]{1,0:T(1,128)S(1)}, u32[]{:S(2)}, u32[]{:S(2)}) collective-permute-start(s32[1,6]{1,0:T(1,128)S(1)} %copy-done), channel_id=1, source_target_pairs={{0,8},{4,12},{8,0},{12,4},{1,9},{5,13},{9,1},{13,5},{2,10},{6,14},... | collective-permute-start | bytes 80 | tf_op jit(solution)/shard_map/ppermute | solution.py:435
  5.9 1.6 %collective-permute-start = (s32[1,6]{1,0:T(1,128)S(1)}, s32[1,6]{1,0:T(1,128)S(1)}, u32[]{:S(2)}, u32[]{:S(2)}) collective-permute-start(s32[1,6]{1,0:T(1,128)S(1)} %copy-done), channel_id=1, source_target_pairs={{0,4},{4,0},{8,12},{12,8},{1,5},{5,1},{9,13},{13,9},{2,6},{6,2},{1... | collective-permute-start | bytes 80 | tf_op jit(solution)/shard_map/ppermute | solution.py:435
  7.5 0.0 collective-permute-start.2
  7.5 0.0 collective-permute-done.1.refs_2_
  7.5 2.0 %collective-permute-done.refs_1_ = s32[1,6]{1,0:T(1,128)S(1)} collective-permute-done((s32[1,6]{1,0:T(1,128)S(1)}, s32[1,6]{1,0:T(1,128)S(1)}, u32[]{:S(2)}, u32[]{:S(2)}) %collective-permute-start) | collective-permute-done | bytes 56 | tf_op jit(solution)/shard_map/ppermute | solution.py:435
  9.4 3.4 %collective-permute-done.2.refs_3_ = s32[1,6]{1,0:T(1,128)S(1)} collective-permute-done((s32[1,6]{1,0:T(1,128)S(1)}, s32[1,6]{1,0:T(1,128)S(1)}, u32[]{:S(2)}, u32[]{:S(2)}) %collective-permute-start.2) | collective-permute-done | bytes 56 | tf_op jit(solution)/shard_map/ppermute | solution.py:435
  12.8 2.4 %pack.1 = (bf16[288,256]{1,0:T(8,128)(2,1)S(1)}, bf16[288,256]{1,0:T(8,128)(2,1)S(1)}, bf16[288,256]{1,0:T(8,128)(2,1)S(1)}, bf16[288,256]{1,0:T(8,128)(2,1)S(1)}, s32[8]{0:T(128)S(1)}) custom-call(s32[1,6]{1,0:T(1,128)} %refs_0_.2, s32[1,6]{1,0:T(1,128)S(1)} %collective-permute-done.refs_1_, s32[1,6]{1,0:T(1,128)S(1)} %collective-permute-done.1.refs_2_, ...), custom_call_target="tpu_custom_call" | custom-call | bytes 1179648 | tf_op jit(solution)/shard_map/pack/pallas_call | solution.py:83
  15.2 0.1 collective-permute-start.4
  15.3 0.1 collective-permute-start.5
  15.4 4.3 %collective-permute-start.6 = (bf16[288,256]{1,0:T(8,128)(2,1)S(1)}, bf16[288,256]{1,0:T(8,128)(2,1)S(1)}, u32[]{:S(2)}, u32[]{:S(2)}) collective-permute-start(bf16[288,256]{1,0:T(8,128)(2,1)S(1)} %get-tuple-element.31), channel_id=1, source_target_pairs={{0,4},{4,0},{8,12},{12,8},{1,5},{5,1},{9,13},{13,9},{2,6},{6,2},{1... | collective-permute-start | bytes 442376 | tf_op jit(solution)/shard_map/ppermute | solution.py:435
  20.3 2.5 %shard_map.110 = (bf16[128,2048]{1,0:T(8,128)(2,1)S(1)}, bf16[128,1024]{1,0:T(8,128)(2,1)S(1)}, bf16[512,2048]{1,0:T(8,128)(2,1)S(1)}, bf16[512,2048]{1,0:T(8,128)(2,1)S(1)}) custom-call(bf16[128,4096]{1,0:T(8,128)(2,1)} %refs_0_.3, bf16[128,2048]{1,0:T(8,128)(2,1)} %refs_1_.1, bf16[512,4096]{1,0:T(8,128)(2,1)} %refs_2_.3, bf16[512,4096]{1,0:T(8,128)(2,1)} %refs_3_.1), custom_call_target="tpu_custom_call" | custom-call | bytes 9961472 | tf_op jit(solution)/shard_map/pallas_call | solution.py:143
  22.9 0.9 %collective-permute-done.4.refs_9_ = bf16[288,256]{1,0:T(8,128)(2,1)S(1)} collective-permute-done((bf16[288,256]{1,0:T(8,128)(2,1)S(1)}, bf16[288,256]{1,0:T(8,128)(2,1)S(1)}, u32[]{:S(2)}, u32[]{:S(2)}) %collective-permute-start.4) | collective-permute-done | bytes 147488 | tf_op jit(solution)/shard_map/ppermute | solution.py:435
  23.8 4.2 %collective-permute-done.5.refs_10_ = bf16[288,256]{1,0:T(8,128)(2,1)S(1)} collective-permute-done((bf16[288,256]{1,0:T(8,128)(2,1)S(1)}, bf16[288,256]{1,0:T(8,128)(2,1)S(1)}, u32[]{:S(2)}, u32[]{:S(2)}) %collective-permute-start.5) | collective-permute-done | bytes 147488 | tf_op jit(solution)/shard_map/ppermute | solution.py:435
  28.0 0.0 collective-permute-start.8
  28.0 0.0 collective-permute-done.6.refs_11_
  28.0 0.5 %collective-permute-start.9 = (bf16[288,256]{1,0:T(8,128)(2,1)S(1)}, bf16[288,256]{1,0:T(8,128)(2,1)S(1)}, u32[]{:S(2)}, u32[]{:S(2)}) collective-permute-start(bf16[288,256]{1,0:T(8,128)(2,1)S(1)} %collective-permute-done.6.refs_11_), channel_id=1, source_target_pairs={{0,1},{1,0},{2,3},{3,2},{4,5},{5,4},{6,7},{7,6},{8,9},{9,8},{10,11... | collective-permute-start | bytes 442376 | tf_op jit(solution)/shard_map/ppermute | solution.py:434
  28.5 0.0 collective-permute-done.10.refs_10_
  28.5 6.6 %attend_new.1 = (f32[2048,256]{1,0:T(8,128)S(1)}, f32[128,256]{1,0:T(8,128)S(1)}) custom-call(s32[8]{0:T(128)S(1)} %get-tuple-element.23.refs_0_, s32[8,128]{1,0:T(8,128)S(1)} %iota.7.refs_1_, bf16[128,512]{1,0:T(8,128)(2,1)} %refs_2_.5, bf16[64,128]{1,0:T(8,128)(2,1)} %bitcast.6, bf16[128,3712]{1,0:T(8,128)(2,1)S(1)} %collective-permute-done.3.refs_4_, ...), custom_call_target="tpu_custom_call" | custom-call | flops 4294967296 | bytes 8388608 | tf_op jit(solution)/shard_map/attend_new/pallas_call | solution.py:381
  35.2 9.8 %attend_prefix.1 = (bf16[128,4096]{1,0:T(8,128)(2,1)}, bf16[128,2048]{1,0:T(8,128)(2,1)S(1)}) custom-call(s32[8]{0:T(128)S(1)} %get-tuple-element.23.refs_0_, s32[8,128]{1,0:T(8,128)S(1)} %iota.7.refs_1_, bf16[128,512]{1,0:T(8,128)(2,1)} %refs_2_.5, bf16[64,128]{1,0:T(8,128)(2,1)} %bitcast.7, bf16[128,3712]{1,0:T(8,128)(2,1)S(1)} %collective-permute-done.3.refs_4_, ...), custom_call_target="tpu_custom_call" | custom-call | flops 6442450944 | bytes 8388608 | tf_op jit(solution)/shard_map/attend_prefix/pallas_call | solution.py:381
  45.0 0.1 collective-permute-start.11
  45.1 1.9 %collective-permute-done.11.back_ref = bf16[128,2048]{1,0:T(8,128)(2,1)S(1)} collective-permute-done((bf16[128,2048]{1,0:T(8,128)(2,1)S(1)}, bf16[128,2048]{1,0:T(8,128)(2,1)S(1)}, u32[]{:S(2)}, u32[]{:S(2)}) %collective-permute-start.11) | collective-permute-done | bytes 524320 | tf_op jit(solution)/shard_map/ppermute | solution.py:434
  46.9 0.8 %join.1 = bf16[128,4096]{1,0:T(8,128)(2,1)} custom-call(bf16[128,4096]{1,0:T(8,128)(2,1)} %get-tuple-element.35.kept_ref, bf16[128,2048]{1,0:T(8,128)(2,1)S(1)} %collective-permute-done.11.back_ref), custom_call_target="tpu_custom_call", output_to_operand_aliasing={{}: (0, {})} | custom-call | tf_op jit(solution)/shard_map/join/pallas_call | solution.py:408
  (10 shorter events, 0.0 us)
Async XLA Ops:
  0.0 2.2 %copy-start = (s32[1,6]{1,0:T(1,128)S(1)}, s32[1,6]{1,0:T(1,128)}, u32[]{:S(2)}) copy-start(s32[1,6]{1,0:T(1,128)} %refs_0_.2) | copy-start | bytes 76
  1.7 26.9 %collective-permute-start.3 = (bf16[128,3712]{1,0:T(8,128)(2,1)S(1)}, bf16[128,3712]{1,0:T(8,128)(2,1)S(1)}, u32[]{:S(2)}, u32[]{:S(2)}) collective-permute-start(bf16[128,3712]{1,0:T(8,128)(2,1)S(1)} %get-tuple-element.24), channel_id=1, source_target_pairs={{0,1},{1,0},{2,3},{3,2},{4,5},{5,4},{6,7},{7,6},{8,9},{9,8},{10,11... | collective-permute-start | bytes 2850824 | tf_op jit(solution)/shard_map/ppermute | solution.py:434
  2.2 5.2 %collective-permute-start.1 = (s32[1,6]{1,0:T(1,128)S(1)}, s32[1,6]{1,0:T(1,128)S(1)}, u32[]{:S(2)}, u32[]{:S(2)}) collective-permute-start(s32[1,6]{1,0:T(1,128)S(1)} %copy-done), channel_id=1, source_target_pairs={{0,8},{4,12},{8,0},{12,4},{1,9},{5,13},{9,1},{13,5},{2,10},{6,14},... | collective-permute-start | bytes 80 | tf_op jit(solution)/shard_map/ppermute | solution.py:435
  5.9 3.6 %collective-permute-start = (s32[1,6]{1,0:T(1,128)S(1)}, s32[1,6]{1,0:T(1,128)S(1)}, u32[]{:S(2)}, u32[]{:S(2)}) collective-permute-start(s32[1,6]{1,0:T(1,128)S(1)} %copy-done), channel_id=1, source_target_pairs={{0,4},{4,0},{8,12},{12,8},{1,5},{5,1},{9,13},{13,9},{2,6},{6,2},{1... | collective-permute-start | bytes 80 | tf_op jit(solution)/shard_map/ppermute | solution.py:435
  7.5 5.4 %collective-permute-start.2 = (s32[1,6]{1,0:T(1,128)S(1)}, s32[1,6]{1,0:T(1,128)S(1)}, u32[]{:S(2)}, u32[]{:S(2)}) collective-permute-start(s32[1,6]{1,0:T(1,128)S(1)} %copy-done), channel_id=1, source_target_pairs={{0,12},{4,8},{8,4},{12,0},{1,13},{5,9},{9,5},{13,1},{2,14},{6,10},... | collective-permute-start | bytes 80 | tf_op jit(solution)/shard_map/ppermute | solution.py:435
  15.2 8.6 %collective-permute-start.4 = (bf16[288,256]{1,0:T(8,128)(2,1)S(1)}, bf16[288,256]{1,0:T(8,128)(2,1)S(1)}, u32[]{:S(2)}, u32[]{:S(2)}) collective-permute-start(bf16[288,256]{1,0:T(8,128)(2,1)S(1)} %get-tuple-element.29), channel_id=1, source_target_pairs={{0,12},{4,8},{8,4},{12,0},{1,13},{5,9},{9,5},{13,1},{2,14},{6,10},... | collective-permute-start | bytes 442376 | tf_op jit(solution)/shard_map/ppermute | solution.py:435
  15.3 12.7 %collective-permute-start.5 = (bf16[288,256]{1,0:T(8,128)(2,1)S(1)}, bf16[288,256]{1,0:T(8,128)(2,1)S(1)}, u32[]{:S(2)}, u32[]{:S(2)}) collective-permute-start(bf16[288,256]{1,0:T(8,128)(2,1)S(1)} %get-tuple-element.30), channel_id=1, source_target_pairs={{0,8},{4,12},{8,0},{12,4},{1,9},{5,13},{9,1},{13,5},{2,10},{6,14},... | collective-permute-start | bytes 442376 | tf_op jit(solution)/shard_map/ppermute | solution.py:435
  15.4 12.6 %collective-permute-start.6 = (bf16[288,256]{1,0:T(8,128)(2,1)S(1)}, bf16[288,256]{1,0:T(8,128)(2,1)S(1)}, u32[]{:S(2)}, u32[]{:S(2)}) collective-permute-start(bf16[288,256]{1,0:T(8,128)(2,1)S(1)} %get-tuple-element.31), channel_id=1, source_target_pairs={{0,4},{4,0},{8,12},{12,8},{1,5},{5,1},{9,13},{13,9},{2,6},{6,2},{1... | collective-permute-start | bytes 442376 | tf_op jit(solution)/shard_map/ppermute | solution.py:435
  19.7 8.8 %collective-permute-start.10 = (bf16[288,256]{1,0:T(8,128)(2,1)S(1)}, bf16[288,256]{1,0:T(8,128)(2,1)S(1)}, u32[]{:S(2)}, u32[]{:S(2)}) collective-permute-start(bf16[288,256]{1,0:T(8,128)(2,1)S(1)} %get-tuple-element.32.refs_9_), channel_id=1, source_target_pairs={{0,1},{1,0},{2,3},{3,2},{4,5},{5,4},{6,7},{7,6},{8,9},{9,8},{10,11... | collective-permute-start | bytes 442376 | tf_op jit(solution)/shard_map/ppermute | solution.py:434
  23.8 11.3 %collective-permute-start.7 = (bf16[288,256]{1,0:T(8,128)(2,1)S(1)}, bf16[288,256]{1,0:T(8,128)(2,1)S(1)}, u32[]{:S(2)}, u32[]{:S(2)}) collective-permute-start(bf16[288,256]{1,0:T(8,128)(2,1)S(1)} %collective-permute-done.4.refs_9_), channel_id=1, source_target_pairs={{0,1},{1,0},{2,3},{3,2},{4,5},{5,4},{6,7},{7,6},{8,9},{9,8},{10,11... | collective-permute-start | bytes 442376 | tf_op jit(solution)/shard_map/ppermute | solution.py:434
  28.0 7.2 %collective-permute-start.8 = (bf16[288,256]{1,0:T(8,128)(2,1)S(1)}, bf16[288,256]{1,0:T(8,128)(2,1)S(1)}, u32[]{:S(2)}, u32[]{:S(2)}) collective-permute-start(bf16[288,256]{1,0:T(8,128)(2,1)S(1)} %collective-permute-done.5.refs_10_), channel_id=1, source_target_pairs={{0,1},{1,0},{2,3},{3,2},{4,5},{5,4},{6,7},{7,6},{8,9},{9,8},{10,11... | collective-permute-start | bytes 442376 | tf_op jit(solution)/shard_map/ppermute | solution.py:434
  28.0 7.2 %collective-permute-start.9 = (bf16[288,256]{1,0:T(8,128)(2,1)S(1)}, bf16[288,256]{1,0:T(8,128)(2,1)S(1)}, u32[]{:S(2)}, u32[]{:S(2)}) collective-permute-start(bf16[288,256]{1,0:T(8,128)(2,1)S(1)} %collective-permute-done.6.refs_11_), channel_id=1, source_target_pairs={{0,1},{1,0},{2,3},{3,2},{4,5},{5,4},{6,7},{7,6},{8,9},{9,8},{10,11... | collective-permute-start | bytes 442376 | tf_op jit(solution)/shard_map/ppermute | solution.py:434
  45.0 2.0 %collective-permute-start.11 = (bf16[128,2048]{1,0:T(8,128)(2,1)S(1)}, bf16[128,2048]{1,0:T(8,128)(2,1)S(1)}, u32[]{:S(2)}, u32[]{:S(2)}) collective-permute-start(bf16[128,2048]{1,0:T(8,128)(2,1)S(1)} %get-tuple-element.36), channel_id=1, source_target_pairs={{0,1},{1,0},{2,3},{3,2},{4,5},{5,4},{6,7},{7,6},{8,9},{9,8},{10,11... | collective-permute-start | bytes 1572872 | tf_op jit(solution)/shard_map/ppermute | solution.py:434

commit v9 on v8

--- a/solution.py
+++ b/solution.py
@@ -17,27 +17,29 @@
 HIDE = -1e30
 
 
-def pack_kernel(n, blocks, pool_local, lists, slots_ref, pool_ref, rope_ref, outs, where_ref,
-                index_ref, count_ref, lat_sem, rope_sem):
+def pack_kernel(kinds, own, blocks, pool_local, lists, slots_ref, pool_ref, rope_ref, outs,
+                where_ref, index_ref, count_ref, lat_sem, rope_sem):
     me = lax.axis_index("req")
     sub = lax.axis_index("sub")
     block = pool_ref.shape[1]
     width = pool_ref.shape[2]
-    for i in range(n * CAP):
+    for i in range(len(kinds) * CAP):
         index_ref[i] = 0
-        where_ref[i] = -1
-    for i in range(n):
-        count_ref[i] = 0
-    for k in range(n):
+    if own:
+        for i in range(where_ref.shape[0]):
+            where_ref[i] = -1
+        for i in range(count_ref.shape[0]):
+            count_ref[i] = 0
+    for i, k in enumerate(kinds):
         found = jnp.int32(0)
         for p in range(blocks):
-            physical = slots_ref[lists[k][0, p]]
+            physical = slots_ref[lists[i][0, p]]
             owner = physical // pool_local
             mine = owner == me
 
             @pl.when(mine)
             def _():
-                index_ref[k * CAP + found] = physical - owner * pool_local
+                index_ref[i * CAP + found] = physical - owner * pool_local
 
             found = found + mine.astype(jnp.int32)
             if k == 0:
@@ -48,18 +50,18 @@
     parts = width // block
     rows = ROPE // parts
     copies = []
-    for k in range(n):
+    for i in range(len(kinds)):
         for c in range(CAP):
             copies.append(pltpu.make_async_copy(
-                pool_ref.at[index_ref[k * CAP + c]],
-                outs[k].at[pl.ds(c * block, block)],
-                lat_sem.at[k * CAP + c],
+                pool_ref.at[index_ref[i * CAP + c]],
+                outs[i].at[pl.ds(c * block, block)],
+                lat_sem.at[i * CAP + c],
             ))
-        for i in range(parts):
+        for j in range(parts):
             copies.append(pltpu.make_async_copy(
-                rope_ref.at[index_ref[k * CAP + sub], pl.ds(i * rows, rows)],
-                outs[k].at[pl.ds(CAP * block, rows), pl.ds(i * block, block)],
-                rope_sem.at[k * parts + i],
+                rope_ref.at[index_ref[i * CAP + sub], pl.ds(j * rows, rows)],
+                outs[i].at[pl.ds(CAP * block, rows), pl.ds(j * block, block)],
+                rope_sem.at[i * parts + j],
             ))
     for copy in copies:
         copy.start()
@@ -67,36 +69,39 @@
         copy.wait()
 
 
-def pack(n, lists, block_slot, pool_latent, rope_turned):
+def pack(n, kinds, lists, block_slot, pool_latent, rope_turned):
     pool_local, block, width = pool_latent.shape
     blocks = lists[0].shape[1]
     rows = CAP * block + block * ROPE // width
+    count = len(kinds)
+    own = 0 in kinds
     vmem = pl.BlockSpec(memory_space=pltpu.VMEM)
     smem = pl.BlockSpec(memory_space=pltpu.SMEM)
 
     def body(*refs):
-        pack_kernel(
-            n, blocks, pool_local, refs[:n], *refs[n : n + 3],
-            refs[n + 3 : 2 * n + 3], *refs[2 * n + 3 :],
-        )
-
-    out = pl.pallas_call(
+        ins, refs = refs[: count + 3], refs[count + 3 :]
+        outs, refs = refs[:count], refs[count:]
+        where_ref, refs = (refs[0], refs[1:]) if own else (None, refs)
+        pack_kernel(kinds, own, blocks, pool_local, ins[:count], *ins[count:], outs, where_ref, *refs)
+
+    return pl.pallas_call(
         body,
-        out_shape=[jax.ShapeDtypeStruct((rows, width), jnp.bfloat16)] * n
-        + [jax.ShapeDtypeStruct((n * CAP,), jnp.int32)],
-        in_specs=[smem] * (n + 1) + [pl.BlockSpec(memory_space=pl.ANY)] * 2,
-        out_specs=[vmem] * n + [smem],
+        out_shape=[jax.ShapeDtypeStruct((rows, width), jnp.bfloat16)] * count
+        + [jax.ShapeDtypeStruct((n * CAP,), jnp.int32)] * own,
+        in_specs=[smem] * (count + 1) + [pl.BlockSpec(memory_space=pl.ANY)] * 2,
+        out_specs=[vmem] * count + [smem] * own,
         scratch_shapes=[
-            pltpu.SMEM((n * CAP,), jnp.int32),
+            pltpu.SMEM((count * CAP,), jnp.int32),
             pltpu.SMEM((n,), jnp.int32),
-            pltpu.SemaphoreType.DMA((n * CAP,)),
-            pltpu.SemaphoreType.DMA((n * width // block,)),
+            pltpu.SemaphoreType.DMA((count * CAP,)),
+            pltpu.SemaphoreType.DMA((count * width // block,)),
         ],
         compiler_params=pltpu.CompilerParams(vmem_limit_bytes=16 << 20),
-        cost_estimate=pl.CostEstimate(flops=0, bytes_accessed=4 * n * rows * width, transcendentals=0),
+        cost_estimate=pl.CostEstimate(
+            flops=0, bytes_accessed=4 * count * rows * width, transcendentals=0
+        ),
         name="pack",
     )(*lists, block_slot, pool_latent, rope_turned)
-    return out[:n], out[n]
 
 
 def half_of(ref, which):
@@ -448,7 +453,11 @@
         new_latent, q_nope, q_rope, rope_turned, pool_latent, pool_turned
     )
     other = swap(other)
-    sent, where = pack(n, lists, slots, pool_latent, pool_turned)
+    early = n // 2
+    sent = {early: pack(n, [early], [lists[early]], slots, pool_latent, pool_turned)[0]}
+    kinds = [k for k in range(n) if k != early]
+    *rest, where = pack(n, kinds, [lists[k] for k in kinds], slots, pool_latent, pool_turned)
+    sent.update(zip(kinds, rest))
     local = swap(sent[0])
     length = prefix_len - lax.broadcasted_iota(jnp.int32, (8, LANES), 1)
     mine = []

time: 47.9 us -> 46.2 us (0.965)
  waiting for transfers between devices: 12.4 us -> 9.35 us
  starting transfers between devices: 10.8 us -> 11.5 us
  Pallas kernels: 23.8 us -> 24.4 us
    ppermute x6, waiting for transfers between devices: 10.5 us -> 7.8 us  [shards(): cross = lambda a, k: lax.ppermute(a, 'req', [(i, i ^ k) for i in range(n)])]
    pallas_call x1 -> x2, Pallas kernels: 2.4 us -> 3.03 us  [pack(): pl.pallas_call(body, out_shape=[jax.ShapeDtypeStruct((rows, width), jnp.b...]
    ppermute x6, starting transfers between devices: 1.16 us -> 1.7 us  [shards(): swap = lambda a: lax.ppermute(a, 'sub', [(0, 1), (1, 0)])]
  transfers between devices with their start and end apart: 12 -> 12, of which waited for: 5 -> 5; matrix products, arithmetic and copies ran while one was open for 0% -> 0% of each run, Pallas kernels for 24% -> 26%
where the time goes in v9:
time: 46.2 us; the launch traced here: 46 us
  Pallas kernels  24.4 us (53%)
  starting transfers between devices  11.5 us (25%)
  waiting for transfers between devices  9.35 us (20%)
  between operations  0.76 us (2%)
    pallas_call x2, Pallas kernels, attend(): pl.pallas_call(functools.partial(attend_kernel, steps, fresh), in_specs=s...  16.4 us
    ppermute x6, starting transfers between devices, shards(): cross = lambda a, k: lax.ppermute(a, 'req', [(i, i ^ k) for i in range(n)])  9.83 us
    ppermute x6, waiting for transfers between devices, shards(): cross = lambda a, k: lax.ppermute(a, 'req', [(i, i ^ k) for i in range(n)])  7.8 us
    pallas_call x2, Pallas kernels, gather_call(): pl.pallas_call(kernel, out_shape=[jax.ShapeDtypeStruct(shape, jnp.bfloat1...  4.17 us
    pallas_call x2, Pallas kernels, pack(): pl.pallas_call(body, out_shape=[jax.ShapeDtypeStruct((rows, width), jnp.b...  3.03 us
    ppermute x6, starting transfers between devices, shards(): swap = lambda a: lax.ppermute(a, 'sub', [(0, 1), (1, 0)])  1.7 us
    ppermute x6, waiting for transfers between devices, shards(): swap = lambda a: lax.ppermute(a, 'sub', [(0, 1), (1, 0)])  1.55 us
  transfers between devices with their start and end apart: 12, of which 5 were waited for; matrix products, arithmetic and copies ran while one was open for 0% of the time, Pallas kernels for 26%

profile of v9, /device:TPU:0, one launch (start us, length us, event | category | flops | bytes accessed | tf_op | source)
XLA Modules:
  0.0 46.0 jit_solution(16658187236543389895)
XLA Ops:
  0.0 1.6 %shard_map.109 = (bf16[128,3712]{1,0:T(8,128)(2,1)S(1)}, bf16[16,128,256]{2,1,0:T(8,128)(2,1)S(1)}, bf16[16,64,128]{2,1,0:T(8,128)(2,1)S(1)}) custom-call(bf16[128,512]{1,0:T(8,128)(2,1)} %refs_2_.5, bf16[128,4096]{1,0:T(8,128)(2,1)} %refs_0_.3, bf16[128,2048]{1,0:T(8,128)(2,1)} %refs_1_.2, bf16[64,128]{1,0:T(8,128)(2,1)} %bitcast.5, ...), custom_call_target="tpu_custom_call" | custom-call | bytes 4521984 | tf_op jit(solution)/shard_map/pallas_call | solution.py:148
  1.7 0.6 %collective-permute-start.2 = (bf16[128,3712]{1,0:T(8,128)(2,1)S(1)}, bf16[128,3712]{1,0:T(8,128)(2,1)S(1)}, u32[]{:S(2)}, u32[]{:S(2)}) collective-permute-start(bf16[128,3712]{1,0:T(8,128)(2,1)S(1)} %get-tuple-element.23), channel_id=1, source_target_pairs={{0,1},{1,0},{2,3},{3,2},{4,5},{5,4},{6,7},{7,6},{8,9},{9,8},{10,11... | collective-permute-start | bytes 2850824 | tf_op jit(solution)/shard_map/ppermute | solution.py:439
  2.2 4.7 %collective-permute-start.1 = (s32[1,6]{1,0:T(1,128)S(1)}, s32[1,6]{1,0:T(1,128)S(1)}, u32[]{:S(2)}, u32[]{:S(2)}) collective-permute-start(s32[1,6]{1,0:T(1,128)S(1)} %copy-done), channel_id=1, source_target_pairs={{0,12},{4,8},{8,4},{12,0},{1,13},{5,9},{9,5},{13,1},{2,14},{6,10},... | collective-permute-start | bytes 80 | tf_op jit(solution)/shard_map/ppermute | solution.py:440
  6.9 0.6 %collective-permute-start.4 = (s32[1,6]{1,0:T(1,128)S(1)}, s32[1,6]{1,0:T(1,128)S(1)}, u32[]{:S(2)}, u32[]{:S(2)}) collective-permute-start(s32[1,6]{1,0:T(1,128)S(1)} %copy-done), channel_id=1, source_target_pairs={{0,8},{4,12},{8,0},{12,4},{1,9},{5,13},{9,1},{13,5},{2,10},{6,14},... | collective-permute-start | bytes 80 | tf_op jit(solution)/shard_map/ppermute | solution.py:440
  7.5 0.9 %collective-permute-done.1.refs_2_ = s32[1,6]{1,0:T(1,128)S(1)} collective-permute-done((s32[1,6]{1,0:T(1,128)S(1)}, s32[1,6]{1,0:T(1,128)S(1)}, u32[]{:S(2)}, u32[]{:S(2)}) %collective-permute-start.1) | collective-permute-done | bytes 56 | tf_op jit(solution)/shard_map/ppermute | solution.py:440
  8.4 2.0 %collective-permute-done.refs_1_ = s32[1,6]{1,0:T(1,128)S(1)} collective-permute-done((s32[1,6]{1,0:T(1,128)S(1)}, s32[1,6]{1,0:T(1,128)S(1)}, u32[]{:S(2)}, u32[]{:S(2)}) %collective-permute-start) | collective-permute-done | bytes 56 | tf_op jit(solution)/shard_map/ppermute | solution.py:440
  10.5 2.1 %pack.2 = (bf16[288,256]{1,0:T(8,128)(2,1)S(1)}, bf16[288,256]{1,0:T(8,128)(2,1)S(1)}, bf16[288,256]{1,0:T(8,128)(2,1)S(1)}, s32[8]{0:T(128)S(1)}) custom-call(s32[1,6]{1,0:T(1,128)} %refs_0_.2, s32[1,6]{1,0:T(1,128)S(1)} %collective-permute-done.refs_1_, s32[1,6]{1,0:T(1,128)S(1)} %collective-permute-done.1.refs_2_, s32[64]{0:T(128)} %refs_1_.3, ...), custom_call_target="tpu_custom_call" | custom-call | bytes 884736 | tf_op jit(solution)/shard_map/pack/pallas_call | solution.py:87
  12.6 1.9 %collective-permute-start.3 = (bf16[288,256]{1,0:T(8,128)(2,1)S(1)}, bf16[288,256]{1,0:T(8,128)(2,1)S(1)}, u32[]{:S(2)}, u32[]{:S(2)}) collective-permute-start(bf16[288,256]{1,0:T(8,128)(2,1)S(1)} %get-tuple-element.28), channel_id=1, source_target_pairs={{0,12},{4,8},{8,4},{12,0},{1,13},{5,9},{9,5},{13,1},{2,14},{6,10},... | collective-permute-start | bytes 442376 | tf_op jit(solution)/shard_map/ppermute | solution.py:440
  14.4 0.9 %pack.3 = bf16[288,256]{1,0:T(8,128)(2,1)S(1)} custom-call(s32[1,6]{1,0:T(1,128)S(1)} %collective-permute-done.4.refs_0_, s32[64]{0:T(128)} %refs_1_.3, bf16[16,128,256]{2,1,0:T(8,128)(2,1)S(1)} %get-tuple-element.20.refs_4_.refs_2_, bf16[16,64,128]{2,1,0:T(8,128)(2,1)S(1)} %get-tuple-element.21.refs_5_.refs_3_), custom_call_target="tpu_custom_call" | custom-call | bytes 294912 | tf_op jit(solution)/shard_map/pack/pallas_call | solution.py:87
  15.4 2.6 %collective-permute-start.5 = (bf16[288,256]{1,0:T(8,128)(2,1)S(1)}, bf16[288,256]{1,0:T(8,128)(2,1)S(1)}, u32[]{:S(2)}, u32[]{:S(2)}) collective-permute-start(bf16[288,256]{1,0:T(8,128)(2,1)S(1)} %pack.3), channel_id=1, source_target_pairs={{0,8},{4,12},{8,0},{12,4},{1,9},{5,13},{9,1},{13,5},{2,10},{6,14},... | collective-permute-start | bytes 442376 | tf_op jit(solution)/shard_map/ppermute | solution.py:440
  18.0 0.0 collective-permute-start.10
  18.7 2.5 %shard_map.110 = (bf16[128,2048]{1,0:T(8,128)(2,1)S(1)}, bf16[128,1024]{1,0:T(8,128)(2,1)S(1)}, bf16[512,2048]{1,0:T(8,128)(2,1)S(1)}, bf16[512,2048]{1,0:T(8,128)(2,1)S(1)}) custom-call(bf16[128,4096]{1,0:T(8,128)(2,1)} %refs_0_.3, bf16[128,2048]{1,0:T(8,128)(2,1)} %refs_1_.2, bf16[512,4096]{1,0:T(8,128)(2,1)} %refs_2_.3, bf16[512,4096]{1,0:T(8,128)(2,1)} %refs_3_.3), custom_call_target="tpu_custom_call" | custom-call | bytes 9961472 | tf_op jit(solution)/shard_map/pallas_call | solution.py:148
  21.2 0.6 %collective-permute-start.7 = (bf16[288,256]{1,0:T(8,128)(2,1)S(1)}, bf16[288,256]{1,0:T(8,128)(2,1)S(1)}, u32[]{:S(2)}, u32[]{:S(2)}) collective-permute-start(bf16[288,256]{1,0:T(8,128)(2,1)S(1)} %collective-permute-done.3.refs_9_), channel_id=1, source_target_pairs={{0,1},{1,0},{2,3},{3,2},{4,5},{5,4},{6,7},{7,6},{8,9},{9,8},{10,11... | collective-permute-start | bytes 442376 | tf_op jit(solution)/shard_map/ppermute | solution.py:439
  21.8 2.5 %collective-permute-done.6.refs_11_ = bf16[288,256]{1,0:T(8,128)(2,1)S(1)} collective-permute-done((bf16[288,256]{1,0:T(8,128)(2,1)S(1)}, bf16[288,256]{1,0:T(8,128)(2,1)S(1)}, u32[]{:S(2)}, u32[]{:S(2)}) %collective-permute-start.6) | collective-permute-done | bytes 147488 | tf_op jit(solution)/shard_map/ppermute | solution.py:440
  24.3 2.3 %collective-permute-done.5.refs_10_ = bf16[288,256]{1,0:T(8,128)(2,1)S(1)} collective-permute-done((bf16[288,256]{1,0:T(8,128)(2,1)S(1)}, bf16[288,256]{1,0:T(8,128)(2,1)S(1)}, u32[]{:S(2)}, u32[]{:S(2)}) %collective-permute-start.5) | collective-permute-done | bytes 147488 | tf_op jit(solution)/shard_map/ppermute | solution.py:440
  26.7 0.0 collective-permute-start.8
  26.7 0.0 collective-permute-done.10.refs_10_
  26.7 0.0 collective-permute-done.2.refs_4_
  26.7 6.6 %attend_new.1 = (f32[2048,256]{1,0:T(8,128)S(1)}, f32[128,256]{1,0:T(8,128)S(1)}) custom-call(s32[8]{0:T(128)S(1)} %get-tuple-element.22.refs_0_, s32[8,128]{1,0:T(8,128)S(1)} %iota.7.refs_1_, bf16[128,512]{1,0:T(8,128)(2,1)} %refs_2_.5, bf16[64,128]{1,0:T(8,128)(2,1)} %bitcast.6, bf16[128,3712]{1,0:T(8,128)(2,1)S(1)} %collective-permute-done.2.refs_4_, ...), custom_call_target="tpu_custom_call" | custom-call | flops 4294967296 | bytes 8388608 | tf_op jit(solution)/shard_map/attend_new/pallas_call | solution.py:386
  33.3 0.0 collective-permute-done.9.refs_14_
  33.4 9.8 %attend_prefix.1 = (bf16[128,4096]{1,0:T(8,128)(2,1)}, bf16[128,2048]{1,0:T(8,128)(2,1)S(1)}) custom-call(s32[8]{0:T(128)S(1)} %get-tuple-element.22.refs_0_, s32[8,128]{1,0:T(8,128)S(1)} %iota.7.refs_1_, bf16[128,512]{1,0:T(8,128)(2,1)} %refs_2_.5, bf16[64,128]{1,0:T(8,128)(2,1)} %bitcast.7, bf16[128,3712]{1,0:T(8,128)(2,1)S(1)} %collective-permute-done.2.refs_4_, ...), custom_call_target="tpu_custom_call" | custom-call | flops 6442450944 | bytes 8388608 | tf_op jit(solution)/shard_map/attend_prefix/pallas_call | solution.py:386
  43.1 0.6 %collective-permute-start.11 = (bf16[128,2048]{1,0:T(8,128)(2,1)S(1)}, bf16[128,2048]{1,0:T(8,128)(2,1)S(1)}, u32[]{:S(2)}, u32[]{:S(2)}) collective-permute-start(bf16[128,2048]{1,0:T(8,128)(2,1)S(1)} %get-tuple-element.34), channel_id=1, source_target_pairs={{0,1},{1,0},{2,3},{3,2},{4,5},{5,4},{6,7},{7,6},{8,9},{9,8},{10,11... | collective-permute-start | bytes 1572872 | tf_op jit(solution)/shard_map/ppermute | solution.py:439
  43.7 1.5 %collective-permute-done.11.back_ref = bf16[128,2048]{1,0:T(8,128)(2,1)S(1)} collective-permute-done((bf16[128,2048]{1,0:T(8,128)(2,1)S(1)}, bf16[128,2048]{1,0:T(8,128)(2,1)S(1)}, u32[]{:S(2)}, u32[]{:S(2)}) %collective-permute-start.11) | collective-permute-done | bytes 524320 | tf_op jit(solution)/shard_map/ppermute | solution.py:439
  45.2 0.8 %join.1 = bf16[128,4096]{1,0:T(8,128)(2,1)} custom-call(bf16[128,4096]{1,0:T(8,128)(2,1)} %get-tuple-element.33.kept_ref, bf16[128,2048]{1,0:T(8,128)(2,1)S(1)} %collective-permute-done.11.back_ref), custom_call_target="tpu_custom_call", output_to_operand_aliasing={{}: (0, {})} | custom-call | tf_op jit(solution)/shard_map/join/pallas_call | solution.py:413
  (11 shorter events, 0.0 us)
Async XLA Ops:
  0.0 2.2 %copy-start = (s32[1,6]{1,0:T(1,128)S(1)}, s32[1,6]{1,0:T(1,128)}, u32[]{:S(2)}) copy-start(s32[1,6]{1,0:T(1,128)} %refs_0_.2) | copy-start | bytes 76
  1.7 25.0 %collective-permute-start.2 = (bf16[128,3712]{1,0:T(8,128)(2,1)S(1)}, bf16[128,3712]{1,0:T(8,128)(2,1)S(1)}, u32[]{:S(2)}, u32[]{:S(2)}) collective-permute-start(bf16[128,3712]{1,0:T(8,128)(2,1)S(1)} %get-tuple-element.23), channel_id=1, source_target_pairs={{0,1},{1,0},{2,3},{3,2},{4,5},{5,4},{6,7},{7,6},{8,9},{9,8},{10,11... | collective-permute-start | bytes 2850824 | tf_op jit(solution)/shard_map/ppermute | solution.py:439
  2.2 6.2 %collective-permute-start.1 = (s32[1,6]{1,0:T(1,128)S(1)}, s32[1,6]{1,0:T(1,128)S(1)}, u32[]{:S(2)}, u32[]{:S(2)}) collective-permute-start(s32[1,6]{1,0:T(1,128)S(1)} %copy-done), channel_id=1, source_target_pairs={{0,12},{4,8},{8,4},{12,0},{1,13},{5,9},{9,5},{13,1},{2,14},{6,10},... | collective-permute-start | bytes 80 | tf_op jit(solution)/shard_map/ppermute | solution.py:440
  6.9 3.6 %collective-permute-start = (s32[1,6]{1,0:T(1,128)S(1)}, s32[1,6]{1,0:T(1,128)S(1)}, u32[]{:S(2)}, u32[]{:S(2)}) collective-permute-start(s32[1,6]{1,0:T(1,128)S(1)} %copy-done), channel_id=1, source_target_pairs={{0,4},{4,0},{8,12},{12,8},{1,5},{5,1},{9,13},{13,9},{2,6},{6,2},{1... | collective-permute-start | bytes 80 | tf_op jit(solution)/shard_map/ppermute | solution.py:440
  6.9 7.5 %collective-permute-start.4 = (s32[1,6]{1,0:T(1,128)S(1)}, s32[1,6]{1,0:T(1,128)S(1)}, u32[]{:S(2)}, u32[]{:S(2)}) collective-permute-start(s32[1,6]{1,0:T(1,128)S(1)} %copy-done), channel_id=1, source_target_pairs={{0,8},{4,12},{8,0},{12,4},{1,9},{5,13},{9,1},{13,5},{2,10},{6,14},... | collective-permute-start | bytes 80 | tf_op jit(solution)/shard_map/ppermute | solution.py:440
  12.6 8.7 %collective-permute-start.3 = (bf16[288,256]{1,0:T(8,128)(2,1)S(1)}, bf16[288,256]{1,0:T(8,128)(2,1)S(1)}, u32[]{:S(2)}, u32[]{:S(2)}) collective-permute-start(bf16[288,256]{1,0:T(8,128)(2,1)S(1)} %get-tuple-element.28), channel_id=1, source_target_pairs={{0,12},{4,8},{8,4},{12,0},{1,13},{5,9},{9,5},{13,1},{2,14},{6,10},... | collective-permute-start | bytes 442376 | tf_op jit(solution)/shard_map/ppermute | solution.py:440
  14.4 9.9 %collective-permute-start.6 = (bf16[288,256]{1,0:T(8,128)(2,1)S(1)}, bf16[288,256]{1,0:T(8,128)(2,1)S(1)}, u32[]{:S(2)}, u32[]{:S(2)}) collective-permute-start(bf16[288,256]{1,0:T(8,128)(2,1)S(1)} %get-tuple-element.29), channel_id=1, source_target_pairs={{0,4},{4,0},{8,12},{12,8},{1,5},{5,1},{9,13},{13,9},{2,6},{6,2},{1... | collective-permute-start | bytes 442376 | tf_op jit(solution)/shard_map/ppermute | solution.py:440
  15.4 11.3 %collective-permute-start.5 = (bf16[288,256]{1,0:T(8,128)(2,1)S(1)}, bf16[288,256]{1,0:T(8,128)(2,1)S(1)}, u32[]{:S(2)}, u32[]{:S(2)}) collective-permute-start(bf16[288,256]{1,0:T(8,128)(2,1)S(1)} %pack.3), channel_id=1, source_target_pairs={{0,8},{4,12},{8,0},{12,4},{1,9},{5,13},{9,1},{13,5},{2,10},{6,14},... | collective-permute-start | bytes 442376 | tf_op jit(solution)/shard_map/ppermute | solution.py:440
  18.0 8.7 %collective-permute-start.10 = (bf16[288,256]{1,0:T(8,128)(2,1)S(1)}, bf16[288,256]{1,0:T(8,128)(2,1)S(1)}, u32[]{:S(2)}, u32[]{:S(2)}) collective-permute-start(bf16[288,256]{1,0:T(8,128)(2,1)S(1)} %get-tuple-element.30.refs_9_), channel_id=1, source_target_pairs={{0,1},{1,0},{2,3},{3,2},{4,5},{5,4},{6,7},{7,6},{8,9},{9,8},{10,11... | collective-permute-start | bytes 442376 | tf_op jit(solution)/shard_map/ppermute | solution.py:439
  21.2 12.1 %collective-permute-start.7 = (bf16[288,256]{1,0:T(8,128)(2,1)S(1)}, bf16[288,256]{1,0:T(8,128)(2,1)S(1)}, u32[]{:S(2)}, u32[]{:S(2)}) collective-permute-start(bf16[288,256]{1,0:T(8,128)(2,1)S(1)} %collective-permute-done.3.refs_9_), channel_id=1, source_target_pairs={{0,1},{1,0},{2,3},{3,2},{4,5},{5,4},{6,7},{7,6},{8,9},{9,8},{10,11... | collective-permute-start | bytes 442376 | tf_op jit(solution)/shard_map/ppermute | solution.py:439
  24.3 9.0 %collective-permute-start.9 = (bf16[288,256]{1,0:T(8,128)(2,1)S(1)}, bf16[288,256]{1,0:T(8,128)(2,1)S(1)}, u32[]{:S(2)}, u32[]{:S(2)}) collective-permute-start(bf16[288,256]{1,0:T(8,128)(2,1)S(1)} %collective-permute-done.6.refs_11_), channel_id=1, source_target_pairs={{0,1},{1,0},{2,3},{3,2},{4,5},{5,4},{6,7},{7,6},{8,9},{9,8},{10,11... | collective-permute-start | bytes 442376 | tf_op jit(solution)/shard_map/ppermute | solution.py:439
  26.7 6.7 %collective-permute-start.8 = (bf16[288,256]{1,0:T(8,128)(2,1)S(1)}, bf16[288,256]{1,0:T(8,128)(2,1)S(1)}, u32[]{:S(2)}, u32[]{:S(2)}) collective-permute-start(bf16[288,256]{1,0:T(8,128)(2,1)S(1)} %collective-permute-done.5.refs_10_), channel_id=1, source_target_pairs={{0,1},{1,0},{2,3},{3,2},{4,5},{5,4},{6,7},{7,6},{8,9},{9,8},{10,11... | collective-permute-start | bytes 442376 | tf_op jit(solution)/shard_map/ppermute | solution.py:439
  43.1 2.1 %collective-permute-start.11 = (bf16[128,2048]{1,0:T(8,128)(2,1)S(1)}, bf16[128,2048]{1,0:T(8,128)(2,1)S(1)}, u32[]{:S(2)}, u32[]{:S(2)}) collective-permute-start(bf16[128,2048]{1,0:T(8,128)(2,1)S(1)} %get-tuple-element.34), channel_id=1, source_target_pairs={{0,1},{1,0},{2,3},{3,2},{4,5},{5,4},{6,7},{7,6},{8,9},{9,8},{10,11... | collective-permute-start | bytes 1572872 | tf_op jit(solution)/shard_map/ppermute | solution.py:439

commit v10 on v9

--- a/solution.py
+++ b/solution.py
@@ -137,13 +137,6 @@
     )
 
 
-def load_kernel(*refs):
-    sub = lax.axis_index("sub")
-    *refs, sem = refs
-    count = len(refs) // 2
-    move([(half_of(a, sub), b) for a, b in zip(refs[:count], refs[count:])], sem)
-
-
 def gather_call(kernel, args, shapes):
     return pl.pallas_call(
         kernel,
@@ -166,10 +159,6 @@
     return gather_call(prepare_kernel, args, shapes)
 
 
-def load(*args):
-    return gather_call(load_kernel, args, [(a.shape[0], a.shape[1] // 2) for a in args])
-
-
 RATE = math.log2(math.e) / math.sqrt(NOPE + ROPE)
 
 
@@ -180,7 +169,9 @@
     theirs = refs[count : 2 * count]
     refs = refs[2 * count :]
     if fresh:
-        acc_ref, stat_ref, lat, kc, vt, score, weight, peak, norms, bias = refs
+        wide = (qn_ref, qr_ref, wk_ref, wv_ref)
+        (acc_ref, stat_ref, qn_ref, qr_ref, wk_ref, wv_ref,
+         lat, kc, vt, score, weight, peak, norms, bias, sem) = refs
     else:
         (acc_ref, stat_ref, out_ref, send_ref, lat, kc, vt, score, weight, peak, norms, result,
          sem) = refs
@@ -197,6 +188,23 @@
     tail_at = rope_at + qr_ref.shape[1]
     head = lambda j: slice(j * LANES, (j + 1) * LANES)
     at = lambda start, size: pl.ds(pl.multiple_of(start, size), size)
+
+    def fetch(pair):
+        copies = []
+        for i, (ref, out) in enumerate(zip(wide, (qn_ref, qr_ref, wk_ref, wv_ref))):
+            span = out.shape[1]
+            size = span * 2 * NOPE // half
+            copies.append(pltpu.make_async_copy(
+                ref.at[:, at(sub * span + pair * size, size)],
+                out.at[:, at(pair * size, size)],
+                sem.at[i, pair],
+            ))
+        return copies
+
+    def arrive(pair):
+        if fresh:
+            for copy in fetch(pair):
+                copy.wait()
 
     def build():
         def put_tails(base, rope, mask):
@@ -306,6 +314,7 @@
         form_weights(pair, slot, 0)
         form_weights(pair, slot, 1)
         if more:
+            arrive(pair + 1)
             form_keys(pair + 1)
             form_values(pair + 1, 1 - slot)
         for j in range(2):
@@ -324,7 +333,12 @@
             sem.at[t],
         )
 
+    if fresh:
+        for pair in range(2 * halves):
+            for copy in fetch(pair):
+                copy.start()
     build()
+    arrive(0)
     form_keys(0)
     form_values(0, 0)
     for j in range(2):
@@ -350,11 +364,13 @@
 def attend(steps, where, length, mine, theirs, new_latent, rope_turned, other, qn, qr, wk, wv, state):
     fresh = state is None
     block, latent = new_latent.shape
-    heads = wk.shape[1] // NOPE
+    heads = wk.shape[1] // NOPE // (2 if fresh else 1)
     keys = (len(steps) + (1 if fresh else 0)) * CAP * block
     vmem = pl.BlockSpec(memory_space=pltpu.VMEM)
     args = [where, length, new_latent, rope_turned, other, qn, qr, wk, wv, *mine, *theirs]
-    specs = [pl.BlockSpec(memory_space=pltpu.SMEM)] + [vmem] * (len(args) - 1)
+    place = pl.BlockSpec(memory_space=pl.ANY) if fresh else vmem
+    specs = [pl.BlockSpec(memory_space=pltpu.SMEM)] + [vmem] * 4 + [place] * 4
+    specs += [vmem] * (2 * len(steps))
     scratch = [
         pltpu.VMEM((keys, latent), jnp.bfloat16),
         pltpu.VMEM((2, keys, NOPE + LANES), jnp.bfloat16),
@@ -365,12 +381,18 @@
         pltpu.VMEM((2, 2, 8, 2 * block), jnp.float32),
     ]
     if fresh:
-        out_specs = [vmem, vmem]
+        out_specs = [vmem] * 6
         out_shape = [
             jax.ShapeDtypeStruct((heads * VDIM, 2 * block), jnp.float32),
             jax.ShapeDtypeStruct((heads * 8, 2 * block), jnp.float32),
+        ] + [
+            jax.ShapeDtypeStruct((a.shape[0], a.shape[1] // 2), jnp.bfloat16)
+            for a in (qn, qr, wk, wv)
         ]
-        scratch.append(pltpu.VMEM((2 * block, 2 * block), jnp.float32))
+        scratch += [
+            pltpu.VMEM((2 * block, 2 * block), jnp.float32),
+            pltpu.SemaphoreType.DMA((4, heads // 2)),
+        ]
     else:
         specs += [vmem, vmem]
         args += state
@@ -466,10 +488,12 @@
     theirs = []
     for k, a in zip(far, mine):
         theirs.append(swap(a))
-    loaded = load(q_nope, q_rope, w_uk, w_uv)
-    common = (new_latent, rope_turned, other, *loaded)
-    state = attend([0], where, length, [sent[0]], [local], *common, None)
-    kept, gone = attend(far, where, length, mine, theirs, *common, state)
+    common = (new_latent, rope_turned, other)
+    wide = (q_nope, q_rope, w_uk, w_uv)
+    *state, qn, qr, wk, wv = attend([0], where, length, [sent[0]], [local], *common, *wide, None)
+    kept, gone = attend(
+        far, where, length, mine, theirs, *common, qn, qr, wk, wv, state
+    )
     back = swap(gone)
     return join(kept, back)
 

time: 46.2 us -> 49.3 us (1.067)
  waiting for transfers between devices: 9.35 us -> 12.5 us
  Pallas kernels: 24.4 us -> 24.9 us
  starting transfers between devices: 11.5 us -> 11 us
    ppermute x6, waiting for transfers between devices: 7.8 us -> 10.9 us  [shards(): cross = lambda a, k: lax.ppermute(a, 'req', [(i, i ^ k) for i in range(n)])]
    pallas_call x2, Pallas kernels: 16.4 us -> 19.4 us  [attend(): pl.pallas_call(functools.partial(attend_kernel, steps, fresh), in_specs=s...]
    pallas_call x2 -> x1, Pallas kernels: 4.17 us -> 1.65 us  [gather_call(): pl.pallas_call(kernel, out_shape=[jax.ShapeDtypeStruct(shape, jnp.bfloat1...]
    ppermute x6, starting transfers between devices: 1.7 us -> 1.13 us  [shards(): swap = lambda a: lax.ppermute(a, 'sub', [(0, 1), (1, 0)])]
  transfers between devices with their start and end apart: 12 -> 12, of which waited for: 5 -> 6; matrix products, arithmetic and copies ran while one was open for 0% -> 0% of each run, Pallas kernels for 26% -> 26%
where the time goes in v10:
time: 49.3 us; the launch traced here: 49.1 us
  Pallas kernels  24.9 us (51%)
  waiting for transfers between devices  12.5 us (25%)
  starting transfers between devices  11 us (22%)
  between operations  0.75 us (2%)
    pallas_call x2, Pallas kernels, attend(): pl.pallas_call(functools.partial(attend_kernel, steps, fresh), in_specs=s...  19.4 us
    ppermute x6, waiting for transfers between devices, shards(): cross = lambda a, k: lax.ppermute(a, 'req', [(i, i ^ k) for i in range(n)])  10.9 us
    ppermute x6, starting transfers between devices, shards(): cross = lambda a, k: lax.ppermute(a, 'req', [(i, i ^ k) for i in range(n)])  9.83 us
    pallas_call x2, Pallas kernels, pack(): pl.pallas_call(body, out_shape=[jax.ShapeDtypeStruct((rows, width), jnp.b...  3.03 us
    pallas_call x1, Pallas kernels, gather_call(): pl.pallas_call(kernel, out_shape=[jax.ShapeDtypeStruct(shape, jnp.bfloat1...  1.65 us
    ppermute x6, waiting for transfers between devices, shards(): swap = lambda a: lax.ppermute(a, 'sub', [(0, 1), (1, 0)])  1.55 us
    ppermute x6, starting transfers between devices, shards(): swap = lambda a: lax.ppermute(a, 'sub', [(0, 1), (1, 0)])  1.13 us
  transfers between devices with their start and end apart: 12, of which 6 were waited for; matrix products, arithmetic and copies ran while one was open for 0% of the time, Pallas kernels for 26%

profile of v10, /device:TPU:0, one launch (start us, length us, event | category | flops | bytes accessed | tf_op | source)
XLA Modules:
  0.0 49.1 jit_solution(15396370141722333969)
XLA Ops:
  0.0 1.6 %shard_map.109 = (bf16[128,3712]{1,0:T(8,128)(2,1)S(1)}, bf16[16,128,256]{2,1,0:T(8,128)(2,1)S(1)}, bf16[16,64,128]{2,1,0:T(8,128)(2,1)S(1)}) custom-call(bf16[128,512]{1,0:T(8,128)(2,1)} %refs_2_.3, bf16[128,4096]{1,0:T(8,128)(2,1)} %refs_5_.1, bf16[128,2048]{1,0:T(8,128)(2,1)} %refs_6_.1, bf16[64,128]{1,0:T(8,128)(2,1)} %bitcast.5, ...), custom_call_target="tpu_custom_call" | custom-call | bytes 4521984 | tf_op jit(solution)/shard_map/pallas_call | solution.py:141
  1.7 0.6 %collective-permute-start.2 = (bf16[128,3712]{1,0:T(8,128)(2,1)S(1)}, bf16[128,3712]{1,0:T(8,128)(2,1)S(1)}, u32[]{:S(2)}, u32[]{:S(2)}) collective-permute-start(bf16[128,3712]{1,0:T(8,128)(2,1)S(1)} %get-tuple-element.23), channel_id=1, source_target_pairs={{0,1},{1,0},{2,3},{3,2},{4,5},{5,4},{6,7},{7,6},{8,9},{9,8},{10,11... | collective-permute-start | bytes 2850824 | tf_op jit(solution)/shard_map/ppermute | solution.py:461
  2.2 4.7 %collective-permute-start.1 = (s32[1,6]{1,0:T(1,128)S(1)}, s32[1,6]{1,0:T(1,128)S(1)}, u32[]{:S(2)}, u32[]{:S(2)}) collective-permute-start(s32[1,6]{1,0:T(1,128)S(1)} %copy-done), channel_id=1, source_target_pairs={{0,12},{4,8},{8,4},{12,0},{1,13},{5,9},{9,5},{13,1},{2,14},{6,10},... | collective-permute-start | bytes 80 | tf_op jit(solution)/shard_map/ppermute | solution.py:462
  6.9 0.6 %collective-permute-start.5 = (s32[1,6]{1,0:T(1,128)S(1)}, s32[1,6]{1,0:T(1,128)S(1)}, u32[]{:S(2)}, u32[]{:S(2)}) collective-permute-start(s32[1,6]{1,0:T(1,128)S(1)} %copy-done), channel_id=1, source_target_pairs={{0,8},{4,12},{8,0},{12,4},{1,9},{5,13},{9,1},{13,5},{2,10},{6,14},... | collective-permute-start | bytes 80 | tf_op jit(solution)/shard_map/ppermute | solution.py:462
  7.5 0.9 %collective-permute-done.1.refs_2_ = s32[1,6]{1,0:T(1,128)S(1)} collective-permute-done((s32[1,6]{1,0:T(1,128)S(1)}, s32[1,6]{1,0:T(1,128)S(1)}, u32[]{:S(2)}, u32[]{:S(2)}) %collective-permute-start.1) | collective-permute-done | bytes 56 | tf_op jit(solution)/shard_map/ppermute | solution.py:462
  8.4 2.0 %collective-permute-done.refs_1_ = s32[1,6]{1,0:T(1,128)S(1)} collective-permute-done((s32[1,6]{1,0:T(1,128)S(1)}, s32[1,6]{1,0:T(1,128)S(1)}, u32[]{:S(2)}, u32[]{:S(2)}) %collective-permute-start) | collective-permute-done | bytes 56 | tf_op jit(solution)/shard_map/ppermute | solution.py:462
  10.5 2.1 %pack.2 = (bf16[288,256]{1,0:T(8,128)(2,1)S(1)}, bf16[288,256]{1,0:T(8,128)(2,1)S(1)}, bf16[288,256]{1,0:T(8,128)(2,1)S(1)}, s32[8]{0:T(128)S(1)}) custom-call(s32[1,6]{1,0:T(1,128)} %refs_0_.1, s32[1,6]{1,0:T(1,128)S(1)} %collective-permute-done.refs_1_, s32[1,6]{1,0:T(1,128)S(1)} %collective-permute-done.1.refs_2_, s32[64]{0:T(128)} %refs_1_.1, ...), custom_call_target="tpu_custom_call" | custom-call | bytes 884736 | tf_op jit(solution)/shard_map/pack/pallas_call | solution.py:87
  12.6 1.9 %collective-permute-start.4 = (bf16[288,256]{1,0:T(8,128)(2,1)S(1)}, bf16[288,256]{1,0:T(8,128)(2,1)S(1)}, u32[]{:S(2)}, u32[]{:S(2)}) collective-permute-start(bf16[288,256]{1,0:T(8,128)(2,1)S(1)} %get-tuple-element.29), channel_id=1, source_target_pairs={{0,12},{4,8},{8,4},{12,0},{1,13},{5,9},{9,5},{13,1},{2,14},{6,10},... | collective-permute-start | bytes 442376 | tf_op jit(solution)/shard_map/ppermute | solution.py:462
  14.4 0.9 %pack.3 = bf16[288,256]{1,0:T(8,128)(2,1)S(1)} custom-call(s32[1,6]{1,0:T(1,128)S(1)} %collective-permute-done.5.refs_0_, s32[64]{0:T(128)} %refs_1_.1, bf16[16,128,256]{2,1,0:T(8,128)(2,1)S(1)} %get-tuple-element.20.refs_4_.refs_2_, bf16[16,64,128]{2,1,0:T(8,128)(2,1)S(1)} %get-tuple-element.21.refs_5_.refs_3_), custom_call_target="tpu_custom_call" | custom-call | bytes 294912 | tf_op jit(solution)/shard_map/pack/pallas_call | solution.py:87
  15.4 2.6 %collective-permute-start.6 = (bf16[288,256]{1,0:T(8,128)(2,1)S(1)}, bf16[288,256]{1,0:T(8,128)(2,1)S(1)}, u32[]{:S(2)}, u32[]{:S(2)}) collective-permute-start(bf16[288,256]{1,0:T(8,128)(2,1)S(1)} %pack.3), channel_id=1, source_target_pairs={{0,8},{4,12},{8,0},{12,4},{1,9},{5,13},{9,1},{13,5},{2,10},{6,14},... | collective-permute-start | bytes 442376 | tf_op jit(solution)/shard_map/ppermute | solution.py:462
  18.0 0.0 collective-permute-start.3
  18.7 2.4 %collective-permute-done.4.refs_9_ = bf16[288,256]{1,0:T(8,128)(2,1)S(1)} collective-permute-done((bf16[288,256]{1,0:T(8,128)(2,1)S(1)}, bf16[288,256]{1,0:T(8,128)(2,1)S(1)}, u32[]{:S(2)}, u32[]{:S(2)}) %collective-permute-start.4) | collective-permute-done | bytes 147488 | tf_op jit(solution)/shard_map/ppermute | solution.py:462
  21.1 3.2 %collective-permute-done.7.refs_11_ = bf16[288,256]{1,0:T(8,128)(2,1)S(1)} collective-permute-done((bf16[288,256]{1,0:T(8,128)(2,1)S(1)}, bf16[288,256]{1,0:T(8,128)(2,1)S(1)}, u32[]{:S(2)}, u32[]{:S(2)}) %collective-permute-start.7) | collective-permute-done | bytes 147488 | tf_op jit(solution)/shard_map/ppermute | solution.py:462
  24.3 2.3 %collective-permute-done.6.refs_10_ = bf16[288,256]{1,0:T(8,128)(2,1)S(1)} collective-permute-done((bf16[288,256]{1,0:T(8,128)(2,1)S(1)}, bf16[288,256]{1,0:T(8,128)(2,1)S(1)}, u32[]{:S(2)}, u32[]{:S(2)}) %collective-permute-start.6) | collective-permute-done | bytes 147488 | tf_op jit(solution)/shard_map/ppermute | solution.py:462
  26.7 0.0 collective-permute-start.9
  26.7 0.0 collective-permute-done.3.refs_10_
  26.7 0.0 collective-permute-done.2.refs_4_
  26.7 9.7 %attend_new.1 = (f32[2048,256]{1,0:T(8,128)S(1)}, f32[128,256]{1,0:T(8,128)S(1)}, bf16[128,2048]{1,0:T(8,128)(2,1)S(1)}, bf16[128,1024]{1,0:T(8,128)(2,1)S(1)}, ...) custom-call(s32[8]{0:T(128)S(1)} %get-tuple-element.22.refs_0_, s32[8,128]{1,0:T(8,128)S(1)} %iota.7.refs_1_, ...), custom_call_target="tpu_custom_call" | custom-call | flops 4294967296 | bytes 8388608 | tf_op jit(solution)/shard_map/attend_new/pallas_call | solution.py:408
  36.4 0.0 collective-permute-done.10.refs_14_
  36.4 0.0 collective-permute-done.9.refs_13_
  36.4 9.7 %attend_prefix.1 = (bf16[128,4096]{1,0:T(8,128)(2,1)}, bf16[128,2048]{1,0:T(8,128)(2,1)S(1)}) custom-call(s32[8]{0:T(128)S(1)} %get-tuple-element.22.refs_0_, s32[8,128]{1,0:T(8,128)S(1)} %iota.7.refs_1_, bf16[128,512]{1,0:T(8,128)(2,1)} %refs_2_.3, bf16[64,128]{1,0:T(8,128)(2,1)} %bitcast.7, bf16[128,3712]{1,0:T(8,128)(2,1)S(1)} %collective-permute-done.2.refs_4_, ...), custom_call_target="tpu_custom_call" | custom-call | flops 6442450944 | bytes 8388608 | tf_op jit(solution)/shard_map/attend_prefix/pallas_call | solution.py:408
  46.2 0.6 %collective-permute-start.11 = (bf16[128,2048]{1,0:T(8,128)(2,1)S(1)}, bf16[128,2048]{1,0:T(8,128)(2,1)S(1)}, u32[]{:S(2)}, u32[]{:S(2)}) collective-permute-start(bf16[128,2048]{1,0:T(8,128)(2,1)S(1)} %get-tuple-element.34), channel_id=1, source_target_pairs={{0,1},{1,0},{2,3},{3,2},{4,5},{5,4},{6,7},{7,6},{8,9},{9,8},{10,11... | collective-permute-start | bytes 1572872 | tf_op jit(solution)/shard_map/ppermute | solution.py:461
  46.7 1.5 %collective-permute-done.11.back_ref = bf16[128,2048]{1,0:T(8,128)(2,1)S(1)} collective-permute-done((bf16[128,2048]{1,0:T(8,128)(2,1)S(1)}, bf16[128,2048]{1,0:T(8,128)(2,1)S(1)}, u32[]{:S(2)}, u32[]{:S(2)}) %collective-permute-start.11) | collective-permute-done | bytes 524320 | tf_op jit(solution)/shard_map/ppermute | solution.py:461
  48.3 0.8 %join.1 = bf16[128,4096]{1,0:T(8,128)(2,1)} custom-call(bf16[128,4096]{1,0:T(8,128)(2,1)} %get-tuple-element.33.kept_ref, bf16[128,2048]{1,0:T(8,128)(2,1)S(1)} %collective-permute-done.11.back_ref), custom_call_target="tpu_custom_call", output_to_operand_aliasing={{}: (0, {})} | custom-call | tf_op jit(solution)/shard_map/join/pallas_call | solution.py:435
  (10 shorter events, 0.0 us)
Async XLA Ops:
  0.0 2.2 %copy-start = (s32[1,6]{1,0:T(1,128)S(1)}, s32[1,6]{1,0:T(1,128)}, u32[]{:S(2)}) copy-start(s32[1,6]{1,0:T(1,128)} %refs_0_.1) | copy-start | bytes 76
  1.7 25.0 %collective-permute-start.2 = (bf16[128,3712]{1,0:T(8,128)(2,1)S(1)}, bf16[128,3712]{1,0:T(8,128)(2,1)S(1)}, u32[]{:S(2)}, u32[]{:S(2)}) collective-permute-start(bf16[128,3712]{1,0:T(8,128)(2,1)S(1)} %get-tuple-element.23), channel_id=1, source_target_pairs={{0,1},{1,0},{2,3},{3,2},{4,5},{5,4},{6,7},{7,6},{8,9},{9,8},{10,11... | collective-permute-start | bytes 2850824 | tf_op jit(solution)/shard_map/ppermute | solution.py:461
  2.2 6.2 %collective-permute-start.1 = (s32[1,6]{1,0:T(1,128)S(1)}, s32[1,6]{1,0:T(1,128)S(1)}, u32[]{:S(2)}, u32[]{:S(2)}) collective-permute-start(s32[1,6]{1,0:T(1,128)S(1)} %copy-done), channel_id=1, source_target_pairs={{0,12},{4,8},{8,4},{12,0},{1,13},{5,9},{9,5},{13,1},{2,14},{6,10},... | collective-permute-start | bytes 80 | tf_op jit(solution)/shard_map/ppermute | solution.py:462
  6.9 3.6 %collective-permute-start = (s32[1,6]{1,0:T(1,128)S(1)}, s32[1,6]{1,0:T(1,128)S(1)}, u32[]{:S(2)}, u32[]{:S(2)}) collective-permute-start(s32[1,6]{1,0:T(1,128)S(1)} %copy-done), channel_id=1, source_target_pairs={{0,4},{4,0},{8,12},{12,8},{1,5},{5,1},{9,13},{13,9},{2,6},{6,2},{1... | collective-permute-start | bytes 80 | tf_op jit(solution)/shard_map/ppermute | solution.py:462
  6.9 7.5 %collective-permute-start.5 = (s32[1,6]{1,0:T(1,128)S(1)}, s32[1,6]{1,0:T(1,128)S(1)}, u32[]{:S(2)}, u32[]{:S(2)}) collective-permute-start(s32[1,6]{1,0:T(1,128)S(1)} %copy-done), channel_id=1, source_target_pairs={{0,8},{4,12},{8,0},{12,4},{1,9},{5,13},{9,1},{13,5},{2,10},{6,14},... | collective-permute-start | bytes 80 | tf_op jit(solution)/shard_map/ppermute | solution.py:462
  12.6 8.6 %collective-permute-start.4 = (bf16[288,256]{1,0:T(8,128)(2,1)S(1)}, bf16[288,256]{1,0:T(8,128)(2,1)S(1)}, u32[]{:S(2)}, u32[]{:S(2)}) collective-permute-start(bf16[288,256]{1,0:T(8,128)(2,1)S(1)} %get-tuple-element.29), channel_id=1, source_target_pairs={{0,12},{4,8},{8,4},{12,0},{1,13},{5,9},{9,5},{13,1},{2,14},{6,10},... | collective-permute-start | bytes 442376 | tf_op jit(solution)/shard_map/ppermute | solution.py:462
  14.4 9.9 %collective-permute-start.7 = (bf16[288,256]{1,0:T(8,128)(2,1)S(1)}, bf16[288,256]{1,0:T(8,128)(2,1)S(1)}, u32[]{:S(2)}, u32[]{:S(2)}) collective-permute-start(bf16[288,256]{1,0:T(8,128)(2,1)S(1)} %get-tuple-element.30), channel_id=1, source_target_pairs={{0,4},{4,0},{8,12},{12,8},{1,5},{5,1},{9,13},{13,9},{2,6},{6,2},{1... | collective-permute-start | bytes 442376 | tf_op jit(solution)/shard_map/ppermute | solution.py:462
  15.4 11.3 %collective-permute-start.6 = (bf16[288,256]{1,0:T(8,128)(2,1)S(1)}, bf16[288,256]{1,0:T(8,128)(2,1)S(1)}, u32[]{:S(2)}, u32[]{:S(2)}) collective-permute-start(bf16[288,256]{1,0:T(8,128)(2,1)S(1)} %pack.3), channel_id=1, source_target_pairs={{0,8},{4,12},{8,0},{12,4},{1,9},{5,13},{9,1},{13,5},{2,10},{6,14},... | collective-permute-start | bytes 442376 | tf_op jit(solution)/shard_map/ppermute | solution.py:462
  18.0 8.7 %collective-permute-start.3 = (bf16[288,256]{1,0:T(8,128)(2,1)S(1)}, bf16[288,256]{1,0:T(8,128)(2,1)S(1)}, u32[]{:S(2)}, u32[]{:S(2)}) collective-permute-start(bf16[288,256]{1,0:T(8,128)(2,1)S(1)} %get-tuple-element.24.refs_9_), channel_id=1, source_target_pairs={{0,1},{1,0},{2,3},{3,2},{4,5},{5,4},{6,7},{7,6},{8,9},{9,8},{10,11... | collective-permute-start | bytes 442376 | tf_op jit(solution)/shard_map/ppermute | solution.py:461
  21.1 15.3 %collective-permute-start.8 = (bf16[288,256]{1,0:T(8,128)(2,1)S(1)}, bf16[288,256]{1,0:T(8,128)(2,1)S(1)}, u32[]{:S(2)}, u32[]{:S(2)}) collective-permute-start(bf16[288,256]{1,0:T(8,128)(2,1)S(1)} %collective-permute-done.4.refs_9_), channel_id=1, source_target_pairs={{0,1},{1,0},{2,3},{3,2},{4,5},{5,4},{6,7},{7,6},{8,9},{9,8},{10,11... | collective-permute-start | bytes 442376 | tf_op jit(solution)/shard_map/ppermute | solution.py:461
  24.3 12.1 %collective-permute-start.10 = (bf16[288,256]{1,0:T(8,128)(2,1)S(1)}, bf16[288,256]{1,0:T(8,128)(2,1)S(1)}, u32[]{:S(2)}, u32[]{:S(2)}) collective-permute-start(bf16[288,256]{1,0:T(8,128)(2,1)S(1)} %collective-permute-done.7.refs_11_), channel_id=1, source_target_pairs={{0,1},{1,0},{2,3},{3,2},{4,5},{5,4},{6,7},{7,6},{8,9},{9,8},{10,11... | collective-permute-start | bytes 442376 | tf_op jit(solution)/shard_map/ppermute | solution.py:461
  26.7 9.7 %collective-permute-start.9 = (bf16[288,256]{1,0:T(8,128)(2,1)S(1)}, bf16[288,256]{1,0:T(8,128)(2,1)S(1)}, u32[]{:S(2)}, u32[]{:S(2)}) collective-permute-start(bf16[288,256]{1,0:T(8,128)(2,1)S(1)} %collective-permute-done.6.refs_10_), channel_id=1, source_target_pairs={{0,1},{1,0},{2,3},{3,2},{4,5},{5,4},{6,7},{7,6},{8,9},{9,8},{10,11... | collective-permute-start | bytes 442376 | tf_op jit(solution)/shard_map/ppermute | solution.py:461
  46.2 2.1 %collective-permute-start.11 = (bf16[128,2048]{1,0:T(8,128)(2,1)S(1)}, bf16[128,2048]{1,0:T(8,128)(2,1)S(1)}, u32[]{:S(2)}, u32[]{:S(2)}) collective-permute-start(bf16[128,2048]{1,0:T(8,128)(2,1)S(1)} %get-tuple-element.34), channel_id=1, source_target_pairs={{0,1},{1,0},{2,3},{3,2},{4,5},{5,4},{6,7},{7,6},{8,9},{9,8},{10,11... | collective-permute-start | bytes 1572872 | tf_op jit(solution)/shard_map/ppermute | solution.py:461

commit v11 on v10

--- a/solution.py
+++ b/solution.py
@@ -200,6 +200,11 @@
                 sem.at[i, pair],
             ))
         return copies
+
+    def send_for(pair):
+        if fresh:
+            for copy in fetch(pair):
+                copy.start()
 
     def arrive(pair):
         if fresh:
@@ -310,7 +315,9 @@
             result[:, columns] = o[:block]
             send_ref[:, columns] = o[block:]
 
-    def both(pair, slot, more=True):
+    def both(pair, slot, more=True, ahead=True):
+        if ahead:
+            send_for(pair + 2)
         form_weights(pair, slot, 0)
         form_weights(pair, slot, 1)
         if more:
@@ -333,10 +340,8 @@
             sem.at[t],
         )
 
-    if fresh:
-        for pair in range(2 * halves):
-            for copy in fetch(pair):
-                copy.start()
+    send_for(0)
+    send_for(1)
     build()
     arrive(0)
     form_keys(0)
@@ -353,8 +358,8 @@
 
     if halves > 1:
         lax.fori_loop(0, halves - 1, body, 0)
-    both(2 * halves - 2, 0)
-    both(2 * halves - 1, 1, False)
+    both(2 * halves - 2, 0, ahead=False)
+    both(2 * halves - 1, 1, more=False, ahead=False)
     if not fresh:
         deliver(halves - 1).start()
         for t in range(halves):

time: 49.3 us -> 49.5 us (level)
  no operation moved by 1% of the time
where the time goes in v11:
time: 49.5 us; the launch traced here: 49.2 us
  Pallas kernels  25 us (51%)
  waiting for transfers between devices  12.5 us (25%)
  starting transfers between devices  11 us (22%)
  between operations  0.75 us (2%)
    pallas_call x2, Pallas kernels, attend(): pl.pallas_call(functools.partial(attend_kernel, steps, fresh), in_specs=s...  19.5 us
    ppermute x6, waiting for transfers between devices, shards(): cross = lambda a, k: lax.ppermute(a, 'req', [(i, i ^ k) for i in range(n)])  10.9 us
    ppermute x6, starting transfers between devices, shards(): cross = lambda a, k: lax.ppermute(a, 'req', [(i, i ^ k) for i in range(n)])  9.83 us
    pallas_call x2, Pallas kernels, pack(): pl.pallas_call(body, out_shape=[jax.ShapeDtypeStruct((rows, width), jnp.b...  3.03 us
    pallas_call x1, Pallas kernels, gather_call(): pl.pallas_call(kernel, out_shape=[jax.ShapeDtypeStruct(shape, jnp.bfloat1...  1.65 us
    ppermute x6, waiting for transfers between devices, shards(): swap = lambda a: lax.ppermute(a, 'sub', [(0, 1), (1, 0)])  1.55 us
    ppermute x6, starting transfers between devices, shards(): swap = lambda a: lax.ppermute(a, 'sub', [(0, 1), (1, 0)])  1.13 us
  transfers between devices with their start and end apart: 12, of which 6 were waited for; matrix products, arithmetic and copies ran while one was open for 0% of the time, Pallas kernels for 26%

profile of v11, /device:TPU:0, one launch (start us, length us, event | category | flops | bytes accessed | tf_op | source)
XLA Modules:
  0.0 49.2 jit_solution(11843096440115141268)
XLA Ops:
  0.0 1.6 %shard_map.109 = (bf16[128,3712]{1,0:T(8,128)(2,1)S(1)}, bf16[16,128,256]{2,1,0:T(8,128)(2,1)S(1)}, bf16[16,64,128]{2,1,0:T(8,128)(2,1)S(1)}) custom-call(bf16[128,512]{1,0:T(8,128)(2,1)} %refs_2_.3, bf16[128,4096]{1,0:T(8,128)(2,1)} %refs_5_.1, bf16[128,2048]{1,0:T(8,128)(2,1)} %refs_6_.1, bf16[64,128]{1,0:T(8,128)(2,1)} %bitcast.5, ...), custom_call_target="tpu_custom_call" | custom-call | bytes 4521984 | tf_op jit(solution)/shard_map/pallas_call | solution.py:141
  1.7 0.6 %collective-permute-start.2 = (bf16[128,3712]{1,0:T(8,128)(2,1)S(1)}, bf16[128,3712]{1,0:T(8,128)(2,1)S(1)}, u32[]{:S(2)}, u32[]{:S(2)}) collective-permute-start(bf16[128,3712]{1,0:T(8,128)(2,1)S(1)} %get-tuple-element.23), channel_id=1, source_target_pairs={{0,1},{1,0},{2,3},{3,2},{4,5},{5,4},{6,7},{7,6},{8,9},{9,8},{10,11... | collective-permute-start | bytes 2850824 | tf_op jit(solution)/shard_map/ppermute | solution.py:466
  2.2 4.7 %collective-permute-start.1 = (s32[1,6]{1,0:T(1,128)S(1)}, s32[1,6]{1,0:T(1,128)S(1)}, u32[]{:S(2)}, u32[]{:S(2)}) collective-permute-start(s32[1,6]{1,0:T(1,128)S(1)} %copy-done), channel_id=1, source_target_pairs={{0,12},{4,8},{8,4},{12,0},{1,13},{5,9},{9,5},{13,1},{2,14},{6,10},... | collective-permute-start | bytes 80 | tf_op jit(solution)/shard_map/ppermute | solution.py:467
  6.9 0.6 %collective-permute-start.5 = (s32[1,6]{1,0:T(1,128)S(1)}, s32[1,6]{1,0:T(1,128)S(1)}, u32[]{:S(2)}, u32[]{:S(2)}) collective-permute-start(s32[1,6]{1,0:T(1,128)S(1)} %copy-done), channel_id=1, source_target_pairs={{0,8},{4,12},{8,0},{12,4},{1,9},{5,13},{9,1},{13,5},{2,10},{6,14},... | collective-permute-start | bytes 80 | tf_op jit(solution)/shard_map/ppermute | solution.py:467
  7.5 0.9 %collective-permute-done.1.refs_2_ = s32[1,6]{1,0:T(1,128)S(1)} collective-permute-done((s32[1,6]{1,0:T(1,128)S(1)}, s32[1,6]{1,0:T(1,128)S(1)}, u32[]{:S(2)}, u32[]{:S(2)}) %collective-permute-start.1) | collective-permute-done | bytes 56 | tf_op jit(solution)/shard_map/ppermute | solution.py:467
  8.4 2.0 %collective-permute-done.refs_1_ = s32[1,6]{1,0:T(1,128)S(1)} collective-permute-done((s32[1,6]{1,0:T(1,128)S(1)}, s32[1,6]{1,0:T(1,128)S(1)}, u32[]{:S(2)}, u32[]{:S(2)}) %collective-permute-start) | collective-permute-done | bytes 56 | tf_op jit(solution)/shard_map/ppermute | solution.py:467
  10.5 2.1 %pack.2 = (bf16[288,256]{1,0:T(8,128)(2,1)S(1)}, bf16[288,256]{1,0:T(8,128)(2,1)S(1)}, bf16[288,256]{1,0:T(8,128)(2,1)S(1)}, s32[8]{0:T(128)S(1)}) custom-call(s32[1,6]{1,0:T(1,128)} %refs_0_.1, s32[1,6]{1,0:T(1,128)S(1)} %collective-permute-done.refs_1_, s32[1,6]{1,0:T(1,128)S(1)} %collective-permute-done.1.refs_2_, s32[64]{0:T(128)} %refs_1_.1, ...), custom_call_target="tpu_custom_call" | custom-call | bytes 884736 | tf_op jit(solution)/shard_map/pack/pallas_call | solution.py:87
  12.6 1.9 %collective-permute-start.4 = (bf16[288,256]{1,0:T(8,128)(2,1)S(1)}, bf16[288,256]{1,0:T(8,128)(2,1)S(1)}, u32[]{:S(2)}, u32[]{:S(2)}) collective-permute-start(bf16[288,256]{1,0:T(8,128)(2,1)S(1)} %get-tuple-element.29), channel_id=1, source_target_pairs={{0,12},{4,8},{8,4},{12,0},{1,13},{5,9},{9,5},{13,1},{2,14},{6,10},... | collective-permute-start | bytes 442376 | tf_op jit(solution)/shard_map/ppermute | solution.py:467
  14.4 0.9 %pack.3 = bf16[288,256]{1,0:T(8,128)(2,1)S(1)} custom-call(s32[1,6]{1,0:T(1,128)S(1)} %collective-permute-done.5.refs_0_, s32[64]{0:T(128)} %refs_1_.1, bf16[16,128,256]{2,1,0:T(8,128)(2,1)S(1)} %get-tuple-element.20.refs_4_.refs_2_, bf16[16,64,128]{2,1,0:T(8,128)(2,1)S(1)} %get-tuple-element.21.refs_5_.refs_3_), custom_call_target="tpu_custom_call" | custom-call | bytes 294912 | tf_op jit(solution)/shard_map/pack/pallas_call | solution.py:87
  15.4 2.6 %collective-permute-start.6 = (bf16[288,256]{1,0:T(8,128)(2,1)S(1)}, bf16[288,256]{1,0:T(8,128)(2,1)S(1)}, u32[]{:S(2)}, u32[]{:S(2)}) collective-permute-start(bf16[288,256]{1,0:T(8,128)(2,1)S(1)} %pack.3), channel_id=1, source_target_pairs={{0,8},{4,12},{8,0},{12,4},{1,9},{5,13},{9,1},{13,5},{2,10},{6,14},... | collective-permute-start | bytes 442376 | tf_op jit(solution)/shard_map/ppermute | solution.py:467
  18.0 0.0 collective-permute-start.3
  18.7 2.4 %collective-permute-done.4.refs_9_ = bf16[288,256]{1,0:T(8,128)(2,1)S(1)} collective-permute-done((bf16[288,256]{1,0:T(8,128)(2,1)S(1)}, bf16[288,256]{1,0:T(8,128)(2,1)S(1)}, u32[]{:S(2)}, u32[]{:S(2)}) %collective-permute-start.4) | collective-permute-done | bytes 147488 | tf_op jit(solution)/shard_map/ppermute | solution.py:467
  21.1 3.2 %collective-permute-done.7.refs_11_ = bf16[288,256]{1,0:T(8,128)(2,1)S(1)} collective-permute-done((bf16[288,256]{1,0:T(8,128)(2,1)S(1)}, bf16[288,256]{1,0:T(8,128)(2,1)S(1)}, u32[]{:S(2)}, u32[]{:S(2)}) %collective-permute-start.7) | collective-permute-done | bytes 147488 | tf_op jit(solution)/shard_map/ppermute | solution.py:467
  24.3 2.3 %collective-permute-done.6.refs_10_ = bf16[288,256]{1,0:T(8,128)(2,1)S(1)} collective-permute-done((bf16[288,256]{1,0:T(8,128)(2,1)S(1)}, bf16[288,256]{1,0:T(8,128)(2,1)S(1)}, u32[]{:S(2)}, u32[]{:S(2)}) %collective-permute-start.6) | collective-permute-done | bytes 147488 | tf_op jit(solution)/shard_map/ppermute | solution.py:467
  26.7 0.0 collective-permute-start.9
  26.7 0.0 collective-permute-done.3.refs_10_
  26.7 0.0 collective-permute-done.2.refs_4_
  26.7 9.8 %attend_new.1 = (f32[2048,256]{1,0:T(8,128)S(1)}, f32[128,256]{1,0:T(8,128)S(1)}, bf16[128,2048]{1,0:T(8,128)(2,1)S(1)}, bf16[128,1024]{1,0:T(8,128)(2,1)S(1)}, ...) custom-call(s32[8]{0:T(128)S(1)} %get-tuple-element.22.refs_0_, s32[8,128]{1,0:T(8,128)S(1)} %iota.7.refs_1_, ...), custom_call_target="tpu_custom_call" | custom-call | flops 4294967296 | bytes 8388608 | tf_op jit(solution)/shard_map/attend_new/pallas_call | solution.py:413
  36.5 0.0 collective-permute-done.10.refs_14_
  36.5 0.0 collective-permute-done.9.refs_13_
  36.5 9.7 %attend_prefix.1 = (bf16[128,4096]{1,0:T(8,128)(2,1)}, bf16[128,2048]{1,0:T(8,128)(2,1)S(1)}) custom-call(s32[8]{0:T(128)S(1)} %get-tuple-element.22.refs_0_, s32[8,128]{1,0:T(8,128)S(1)} %iota.7.refs_1_, bf16[128,512]{1,0:T(8,128)(2,1)} %refs_2_.3, bf16[64,128]{1,0:T(8,128)(2,1)} %bitcast.7, bf16[128,3712]{1,0:T(8,128)(2,1)S(1)} %collective-permute-done.2.refs_4_, ...), custom_call_target="tpu_custom_call" | custom-call | flops 6442450944 | bytes 8388608 | tf_op jit(solution)/shard_map/attend_prefix/pallas_call | solution.py:413
  46.3 0.6 %collective-permute-start.11 = (bf16[128,2048]{1,0:T(8,128)(2,1)S(1)}, bf16[128,2048]{1,0:T(8,128)(2,1)S(1)}, u32[]{:S(2)}, u32[]{:S(2)}) collective-permute-start(bf16[128,2048]{1,0:T(8,128)(2,1)S(1)} %get-tuple-element.34), channel_id=1, source_target_pairs={{0,1},{1,0},{2,3},{3,2},{4,5},{5,4},{6,7},{7,6},{8,9},{9,8},{10,11... | collective-permute-start | bytes 1572872 | tf_op jit(solution)/shard_map/ppermute | solution.py:466
  46.8 1.5 %collective-permute-done.11.back_ref = bf16[128,2048]{1,0:T(8,128)(2,1)S(1)} collective-permute-done((bf16[128,2048]{1,0:T(8,128)(2,1)S(1)}, bf16[128,2048]{1,0:T(8,128)(2,1)S(1)}, u32[]{:S(2)}, u32[]{:S(2)}) %collective-permute-start.11) | collective-permute-done | bytes 524320 | tf_op jit(solution)/shard_map/ppermute | solution.py:466
  48.4 0.8 %join.1 = bf16[128,4096]{1,0:T(8,128)(2,1)} custom-call(bf16[128,4096]{1,0:T(8,128)(2,1)} %get-tuple-element.33.kept_ref, bf16[128,2048]{1,0:T(8,128)(2,1)S(1)} %collective-permute-done.11.back_ref), custom_call_target="tpu_custom_call", output_to_operand_aliasing={{}: (0, {})} | custom-call | tf_op jit(solution)/shard_map/join/pallas_call | solution.py:440
  (10 shorter events, 0.0 us)
Async XLA Ops:
  0.0 2.2 %copy-start = (s32[1,6]{1,0:T(1,128)S(1)}, s32[1,6]{1,0:T(1,128)}, u32[]{:S(2)}) copy-start(s32[1,6]{1,0:T(1,128)} %refs_0_.1) | copy-start | bytes 76
  1.7 25.0 %collective-permute-start.2 = (bf16[128,3712]{1,0:T(8,128)(2,1)S(1)}, bf16[128,3712]{1,0:T(8,128)(2,1)S(1)}, u32[]{:S(2)}, u32[]{:S(2)}) collective-permute-start(bf16[128,3712]{1,0:T(8,128)(2,1)S(1)} %get-tuple-element.23), channel_id=1, source_target_pairs={{0,1},{1,0},{2,3},{3,2},{4,5},{5,4},{6,7},{7,6},{8,9},{9,8},{10,11... | collective-permute-start | bytes 2850824 | tf_op jit(solution)/shard_map/ppermute | solution.py:466
  2.2 6.2 %collective-permute-start.1 = (s32[1,6]{1,0:T(1,128)S(1)}, s32[1,6]{1,0:T(1,128)S(1)}, u32[]{:S(2)}, u32[]{:S(2)}) collective-permute-start(s32[1,6]{1,0:T(1,128)S(1)} %copy-done), channel_id=1, source_target_pairs={{0,12},{4,8},{8,4},{12,0},{1,13},{5,9},{9,5},{13,1},{2,14},{6,10},... | collective-permute-start | bytes 80 | tf_op jit(solution)/shard_map/ppermute | solution.py:467
  6.9 3.6 %collective-permute-start = (s32[1,6]{1,0:T(1,128)S(1)}, s32[1,6]{1,0:T(1,128)S(1)}, u32[]{:S(2)}, u32[]{:S(2)}) collective-permute-start(s32[1,6]{1,0:T(1,128)S(1)} %copy-done), channel_id=1, source_target_pairs={{0,4},{4,0},{8,12},{12,8},{1,5},{5,1},{9,13},{13,9},{2,6},{6,2},{1... | collective-permute-start | bytes 80 | tf_op jit(solution)/shard_map/ppermute | solution.py:467
  6.9 7.5 %collective-permute-start.5 = (s32[1,6]{1,0:T(1,128)S(1)}, s32[1,6]{1,0:T(1,128)S(1)}, u32[]{:S(2)}, u32[]{:S(2)}) collective-permute-start(s32[1,6]{1,0:T(1,128)S(1)} %copy-done), channel_id=1, source_target_pairs={{0,8},{4,12},{8,0},{12,4},{1,9},{5,13},{9,1},{13,5},{2,10},{6,14},... | collective-permute-start | bytes 80 | tf_op jit(solution)/shard_map/ppermute | solution.py:467
  12.6 8.6 %collective-permute-start.4 = (bf16[288,256]{1,0:T(8,128)(2,1)S(1)}, bf16[288,256]{1,0:T(8,128)(2,1)S(1)}, u32[]{:S(2)}, u32[]{:S(2)}) collective-permute-start(bf16[288,256]{1,0:T(8,128)(2,1)S(1)} %get-tuple-element.29), channel_id=1, source_target_pairs={{0,12},{4,8},{8,4},{12,0},{1,13},{5,9},{9,5},{13,1},{2,14},{6,10},... | collective-permute-start | bytes 442376 | tf_op jit(solution)/shard_map/ppermute | solution.py:467
  14.4 9.9 %collective-permute-start.7 = (bf16[288,256]{1,0:T(8,128)(2,1)S(1)}, bf16[288,256]{1,0:T(8,128)(2,1)S(1)}, u32[]{:S(2)}, u32[]{:S(2)}) collective-permute-start(bf16[288,256]{1,0:T(8,128)(2,1)S(1)} %get-tuple-element.30), channel_id=1, source_target_pairs={{0,4},{4,0},{8,12},{12,8},{1,5},{5,1},{9,13},{13,9},{2,6},{6,2},{1... | collective-permute-start | bytes 442376 | tf_op jit(solution)/shard_map/ppermute | solution.py:467
  15.4 11.3 %collective-permute-start.6 = (bf16[288,256]{1,0:T(8,128)(2,1)S(1)}, bf16[288,256]{1,0:T(8,128)(2,1)S(1)}, u32[]{:S(2)}, u32[]{:S(2)}) collective-permute-start(bf16[288,256]{1,0:T(8,128)(2,1)S(1)} %pack.3), channel_id=1, source_target_pairs={{0,8},{4,12},{8,0},{12,4},{1,9},{5,13},{9,1},{13,5},{2,10},{6,14},... | collective-permute-start | bytes 442376 | tf_op jit(solution)/shard_map/ppermute | solution.py:467
  18.0 8.7 %collective-permute-start.3 = (bf16[288,256]{1,0:T(8,128)(2,1)S(1)}, bf16[288,256]{1,0:T(8,128)(2,1)S(1)}, u32[]{:S(2)}, u32[]{:S(2)}) collective-permute-start(bf16[288,256]{1,0:T(8,128)(2,1)S(1)} %get-tuple-element.24.refs_9_), channel_id=1, source_target_pairs={{0,1},{1,0},{2,3},{3,2},{4,5},{5,4},{6,7},{7,6},{8,9},{9,8},{10,11... | collective-permute-start | bytes 442376 | tf_op jit(solution)/shard_map/ppermute | solution.py:466
  21.1 15.4 %collective-permute-start.8 = (bf16[288,256]{1,0:T(8,128)(2,1)S(1)}, bf16[288,256]{1,0:T(8,128)(2,1)S(1)}, u32[]{:S(2)}, u32[]{:S(2)}) collective-permute-start(bf16[288,256]{1,0:T(8,128)(2,1)S(1)} %collective-permute-done.4.refs_9_), channel_id=1, source_target_pairs={{0,1},{1,0},{2,3},{3,2},{4,5},{5,4},{6,7},{7,6},{8,9},{9,8},{10,11... | collective-permute-start | bytes 442376 | tf_op jit(solution)/shard_map/ppermute | solution.py:466
  24.3 12.2 %collective-permute-start.10 = (bf16[288,256]{1,0:T(8,128)(2,1)S(1)}, bf16[288,256]{1,0:T(8,128)(2,1)S(1)}, u32[]{:S(2)}, u32[]{:S(2)}) collective-permute-start(bf16[288,256]{1,0:T(8,128)(2,1)S(1)} %collective-permute-done.7.refs_11_), channel_id=1, source_target_pairs={{0,1},{1,0},{2,3},{3,2},{4,5},{5,4},{6,7},{7,6},{8,9},{9,8},{10,11... | collective-permute-start | bytes 442376 | tf_op jit(solution)/shard_map/ppermute | solution.py:466
  26.7 9.8 %collective-permute-start.9 = (bf16[288,256]{1,0:T(8,128)(2,1)S(1)}, bf16[288,256]{1,0:T(8,128)(2,1)S(1)}, u32[]{:S(2)}, u32[]{:S(2)}) collective-permute-start(bf16[288,256]{1,0:T(8,128)(2,1)S(1)} %collective-permute-done.6.refs_10_), channel_id=1, source_target_pairs={{0,1},{1,0},{2,3},{3,2},{4,5},{5,4},{6,7},{7,6},{8,9},{9,8},{10,11... | collective-permute-start | bytes 442376 | tf_op jit(solution)/shard_map/ppermute | solution.py:466
  46.3 2.1 %collective-permute-start.11 = (bf16[128,2048]{1,0:T(8,128)(2,1)S(1)}, bf16[128,2048]{1,0:T(8,128)(2,1)S(1)}, u32[]{:S(2)}, u32[]{:S(2)}) collective-permute-start(bf16[128,2048]{1,0:T(8,128)(2,1)S(1)} %get-tuple-element.34), channel_id=1, source_target_pairs={{0,1},{1,0},{2,3},{3,2},{4,5},{5,4},{6,7},{7,6},{8,9},{9,8},{10,11... | collective-permute-start | bytes 1572872 | tf_op jit(solution)/shard_map/ppermute | solution.py:466
